TPU v7x, 128 devices: a whole 4x4x4 slice. The times are simulated.
128 devices in a mesh: gx: 16 (over z, y), gy: 8 (over x, core).
Axes of the slice: x: 4, y: 4, z: 4, core: 2. Of those that a mesh axis runs over, the one named last changes fastest.
Arguments:
- rate_x: float32 [40, 128, 1024], P(None, 'gx', 'gy'), may hold values from 0.0025 to 0.25
- rate_y: float32 [40, 128, 1024], P(None, 'gx', 'gy'), may hold values from 0.00015625 to 0.015625
- land_mask: int32 [128, 1024], P('gx', 'gy'), may hold values 0 or 1
- obs_cell: int32 [128, 128, 32], P(('gx', 'gy')), may hold values from 0 to 81919
- obs_count: int32 [128, 128], P(('gx', 'gy')), may hold values from 0 to 32, as said below
- innovation: float32 [128, 128, 32], P(('gx', 'gy')), may hold values from -12 to 12
- obs_weight: float32 [128, 16, 256, 256], P(('gx', 'gy')), may hold values from -9 to 9, as said below
Outputs:
- solution: float32 [2, 40, 128, 1024], P(None, None, 'gx', 'gy')
- residual: float32 [2, 40, 128, 1024], P(None, None, 'gx', 'gy')
Inputs may be any that keep to these rules, and one draw needn't show every extreme that they name: obs_count[s, d] slots of pair (s, d) hold observations, slots 0 to obs_count[s, d] - 1; in every draw some owner d has obs_count[s, d] = 32 for every source s. Each block obs_weight[s, n] is symmetric positive definite.
All inputs are finite; a program needn't handle non-finite values. No bound on the sum of `land_mask` on one device may be relied on, other than what follows from the above.
Results may differ from a plain program's by a relative error of at most 0.0003.
Values sent between devices are 32-bit elements; how exact they have to be, the bound alone decides.
No kernel may reach another device: no remote copies, remote signals or barrier semaphores. Data moves between devices by JAX's collectives and lax.ppermute only.
A program may use at most 128 MiB of HBM per device.

v0:
```python
import jax
import jax.numpy as jnp
from jax import lax
from jax.sharding import PartitionSpec as P

TR = 2
ITERS = 2


def entering_2(part, axis, combine, identity, reverse):
    count = lax.axis_size(axis)
    place = lax.axis_index(axis)
    ahead = count - 1 - place if reverse else place
    gathered = jax.tree.map(lambda a: lax.all_gather(a, axis), part)
    state = jax.tree.map(lambda a, e: jnp.zeros_like(a) + jnp.asarray(e, a.dtype), part, identity)

    def one(lap, state):
        source = count - 1 - lap if reverse else lap
        return combine(
            state, jax.tree.map(lambda a: lax.dynamic_index_in_dim(a, source, 0, False), gathered)
        )

    return lax.fori_loop(0, ahead, one, state)


def from_root(value, axis, source):
    kept = jnp.where(lax.axis_index(axis) == source, value, 0).astype(value.dtype)
    return lax.psum(kept, axis)


def compose_maps(earlier, following):
    return (earlier[0] * following[0], following[0] * earlier[1] + following[1])


def shift_along(values, distance, line_axis, reverse, filler):
    length = values.shape[line_axis]
    edge_shape = list(values.shape)
    edge_shape[line_axis] = distance
    edge = jnp.full(tuple(edge_shape), filler, values.dtype)
    if reverse:
        return jnp.concatenate(
            [lax.slice_in_dim(values, distance, length, axis=line_axis), edge], axis=line_axis
        )
    return jnp.concatenate(
        [edge, lax.slice_in_dim(values, 0, length - distance, axis=line_axis)], axis=line_axis
    )


def factor_levels(retention, line_axis, reverse):
    length = retention.shape[line_axis]
    stored = []
    factor = retention
    distance = 1
    while distance < length:
        stored.append(factor)
        factor = factor * shift_along(factor, distance, line_axis, reverse, 1.0)
        distance = distance * 2
    return (stored, factor)


def scan_offsets(stored, forcing, line_axis, reverse):
    distance = 1
    for level_factor in stored:
        forcing = forcing + level_factor * shift_along(forcing, distance, line_axis, reverse, 0.0)
        distance = distance * 2
    return forcing


def local_maps(direction_plan, forcing, line_axis, reverse):
    stored, overall = direction_plan
    return (overall, scan_offsets(stored, forcing, line_axis, reverse))


def make_plan(decay_rate, line_axis):
    retention = jnp.exp(-decay_rate)[None]
    one_minus = -jnp.expm1(-decay_rate)
    scaling = jnp.sqrt(one_minus * (1.0 + jnp.exp(-decay_rate)))
    weight = jnp.sqrt(jnp.sqrt(one_minus))
    return (
        retention,
        scaling,
        weight,
        factor_levels(retention, line_axis, False),
        factor_levels(retention, line_axis, True),
    )


def carry_x(totals, reverse):
    identity_map = (jnp.ones_like(totals[0]), jnp.zeros_like(totals[1]))
    before = entering_2(totals, "gx", compose_maps, identity_map, reverse)
    through = compose_maps(before, totals)
    root_index = 0 if reverse else lax.axis_size("gx") - 1
    stacked = from_root(jnp.stack(through), "gx", root_index)
    closure = (stacked[0], stacked[1])
    start_state = closure[1] / (1.0 - closure[0])
    return before[1] + before[0] * start_state


def carry_y(totals, reverse):
    identity_map = (jnp.ones_like(totals[0]), jnp.zeros_like(totals[1]))
    before = entering_2(totals, "gy", compose_maps, identity_map, reverse)
    return before[1]


def shifted_next(back_factor, back_offset, line_axis):
    line_length = back_factor.shape[line_axis]
    next_factor = jnp.concatenate(
        [
            lax.slice_in_dim(back_factor, 1, line_length, axis=line_axis),
            jnp.ones_like(lax.slice_in_dim(back_factor, 0, 1, axis=line_axis)),
        ],
        axis=line_axis,
    )
    next_offset = jnp.concatenate(
        [
            lax.slice_in_dim(back_offset, 1, line_length, axis=line_axis),
            jnp.zeros_like(lax.slice_in_dim(back_offset, 0, 1, axis=line_axis)),
        ],
        axis=line_axis,
    )
    return (next_factor, next_offset)


def line_operator(state_field, line_plan, line_axis, carry_fn):
    retention, scaling, weight, forward_plan, backward_plan = line_plan
    line_length = state_field.shape[line_axis]
    factor, offset = local_maps(forward_plan, scaling * weight * state_field, line_axis, False)
    last_offset = lax.index_in_dim(offset, line_length - 1, line_axis, keepdims=False)
    totals = (
        jnp.broadcast_to(
            lax.index_in_dim(factor, line_length - 1, line_axis, keepdims=False), last_offset.shape
        ),
        last_offset,
    )
    entering = jnp.expand_dims(carry_fn(totals, False), line_axis)
    forward = offset + factor * entering
    back_factor, back_offset = local_maps(backward_plan, retention * forward, line_axis, True)
    first_offset = lax.index_in_dim(back_offset, 0, line_axis, keepdims=False)
    totals = (
        jnp.broadcast_to(
            lax.index_in_dim(back_factor, 0, line_axis, keepdims=False), first_offset.shape
        ),
        first_offset,
    )
    entering = jnp.expand_dims(carry_fn(totals, True), line_axis)
    next_factor, next_offset = shifted_next(back_factor, back_offset, line_axis)
    return weight * scaling * (forward + next_offset + next_factor * entering)


def global_dot(first_field, second_field):
    return lax.psum(jnp.sum(first_field * second_field), ("gx", "gy"))


def on_device(rate_x, rate_y, land_mask, obs_cell, obs_count, innovation, obs_weight):
    ocean = land_mask.astype(jnp.float32)
    field_shape = (TR,) + rate_x.shape
    plan_along_x = make_plan(rate_x, 2)
    plan_along_y = make_plan(rate_y, 3)

    def along_x(state_field):
        return line_operator(state_field, plan_along_x, 2, carry_x)

    def along_y(state_field):
        return line_operator(state_field, plan_along_y, 3, carry_y)

    def gather_back(vector):
        return ocean * along_x(along_y(ocean * vector))

    cell_index = obs_cell[0]
    occupied = (
        lax.broadcasted_iota(jnp.int32, cell_index.shape, 1) < obs_count[0][:, None]
    ).astype(jnp.float32)
    blocks = obs_weight[0]

    def weigh_obs(values):
        packed = (occupied * values).reshape(blocks.shape[0], blocks.shape[1])
        mixed = jnp.einsum("nij,nj->ni", blocks, packed, precision=lax.Precision.HIGHEST)
        return occupied * mixed.reshape(occupied.shape)

    def deposit(values):
        arrived = lax.all_to_all(values, ("gx", "gy"), split_axis=0, concat_axis=0, tiled=True)
        flat_cells = (
            jnp.zeros((TR * rate_x.size,), jnp.float32)
            .at[cell_index.reshape(-1)]
            .add(arrived.reshape(-1))
        )
        return flat_cells.reshape(field_shape)

    right_side = gather_back(deposit(weigh_obs(innovation[0])))
    solution = jnp.zeros_like(right_side)
    residual = right_side
    direction = right_side
    norm_now = global_dot(residual, residual)
    for iteration in range(ITERS):
        picked = jnp.take(
            (ocean * along_y(along_x(ocean * direction))).reshape(-1),
            cell_index.reshape(-1),
            axis=0,
        ).reshape(cell_index.shape)
        hessian_dir = direction + gather_back(
            deposit(
                weigh_obs(
                    lax.all_to_all(picked, ("gx", "gy"), split_axis=0, concat_axis=0, tiled=True)
                )
            )
        )
        step_length = norm_now / global_dot(direction, hessian_dir)
        solution = solution + step_length * direction
        residual = residual - step_length * hessian_dir
        norm_next = global_dot(residual, residual)
        direction = residual + norm_next / norm_now * direction
        norm_now = norm_next
    return (solution, residual)


def solution(mesh):
    placed = (
        P(None, "gx", "gy"),
        P(None, "gx", "gy"),
        P("gx", "gy"),
        P(("gx", "gy"), None, None),
        P(("gx", "gy"), None),
        P(("gx", "gy"), None, None),
        P(("gx", "gy"), None, None, None),
    )
    return jax.shard_map(
        on_device,
        mesh=mesh,
        in_specs=placed,
        out_specs=(P(None, None, "gx", "gy"), P(None, None, "gx", "gy")),
        check_vma=False,
    )
```

profile of v0, /device:TPU:0, one launch (start us, length us, event | category | flops | bytes accessed | tf_op | source)
XLA Modules:
  0.0 1965.4 jit_solution(16719417107121420118)
XLA Ops:
  10.3 5.7 fusion.4
  16.7 11.2 all-to-all-start
  33.3 26.2 %all-gather.4 = f32[16,40,1,128]{3,1,2,0:T(8,128)} all-gather(f32[1,40,1,128]{3,1,2,0:T(8,128)S(1)} %bitcast.601), channel_id=10, replica_groups=mesh['gx'=16,'gy'=8] {'gx'}, dimensions={0}, use_global_device_ids=true | all-gather | bytes 348160 | tf_op jit(solution)/shard_map/all_gather | solution.py:14
  67.7 13.2 all-gather
  80.9 12.9 all-gather.2
  96.7 22.9 %scatter_custom_fusion = f32[81920]{0:T(1024)} fusion(s32[4096]{0:T(1024)} %bitcast.639, f32[4096]{0:T(1024)S(1)} %reshape.333, f32[]{:T(128)} %constant.419.clone.1), kind=kCustom, calls=%fused_computation.284 | custom fusion | flops 4096 | bytes 328192 | tf_op jit(solution)/shard_map/scatter-add | solution.py:185
  126.2 12.8 all-gather.1
  142.8 18.7 all-gather.3
  161.4 2.7 copy.466
  166.6 25.3 %all-gather.5 = f32[32,40,1,128]{3,1,2,0:T(8,128)} all-gather(f32[2,40,1,128]{3,1,2,0:T(8,128)S(1)} %bitcast.618), channel_id=11, replica_groups=mesh['gx'=16,'gy'=8] {'gx'}, dimensions={0}, use_global_device_ids=true | all-gather | bytes 696320 | tf_op jit(solution)/shard_map/all_gather | solution.py:14
  196.4 36.1 %all-gather.6 = f32[16,40,1,128]{3,1,2,0:T(8,128)} all-gather(f32[1,40,1,128]{3,1,2,0:T(8,128)S(1)} %bitcast.607), channel_id=12, replica_groups=mesh['gx'=16,'gy'=8] {'gx'}, dimensions={0}, use_global_device_ids=true | all-gather | bytes 348160 | tf_op jit(solution)/shard_map/all_gather | solution.py:14
  232.5 53.4 %all-reduce.144.cloned.1.call-done = f32[2,2,40,128]{3,2,1,0:T(8,128)} async-done(((f32[2,2,40,128]{3,2,1,0:T(8,128)}), f32[2,2,40,128]{3,2,1,0:T(8,128)}) %all-reduce.144.cloned.1.call-update) | async-done | bytes 81936 | tf_op jit(solution)/shard_map/psum | solution.py:28
  288.3 25.7 %all-gather.7 = f32[32,40,1,128]{3,1,2,0:T(8,128)} all-gather(f32[2,40,1,128]{3,1,2,0:T(8,128)S(1)} %slice_bitcast_fusion.6), channel_id=13, replica_groups=mesh['gx'=16,'gy'=8] {'gx'}, dimensions={0}, use_global_device_ids=true | all-gather | bytes 696320 | tf_op jit(solution)/shard_map/all_gather | solution.py:14
  315.0 12.7 while.263
  332.0 75.4 %all-reduce.146.cloned.1.call-done = f32[2,2,40,128]{3,2,1,0:T(8,128)} async-done(((f32[2,2,40,128]{3,2,1,0:T(8,128)}), f32[2,2,40,128]{3,2,1,0:T(8,128)}) %all-reduce.146.cloned.1.call-update) | async-done | bytes 81936 | tf_op jit(solution)/shard_map/psum | solution.py:28
  410.5 25.9 %all-gather.8 = f32[32,40,1,128]{3,1,2,0:T(8,128)} all-gather(f32[2,40,1,128]{3,1,2,0:T(8,128)S(1)} %slice_bitcast_fusion.5), channel_id=14, replica_groups=mesh['gx'=16,'gy'=8] {'gx'}, dimensions={0}, use_global_device_ids=true | all-gather | bytes 696320 | tf_op jit(solution)/shard_map/all_gather | solution.py:14
  438.7 91.5 %all-reduce.148.cloned.1.call-done = f32[2,2,40,128]{3,2,1,0:T(8,128)} async-done(((f32[2,2,40,128]{3,2,1,0:T(8,128)}), f32[2,2,40,128]{3,2,1,0:T(8,128)}) %all-reduce.148.cloned.1.call-update) | async-done | bytes 81936 | tf_op jit(solution)/shard_map/psum | solution.py:28
  532.8 25.7 %all-gather.9 = f32[32,40,1,128]{3,1,2,0:T(8,128)} all-gather(f32[2,40,1,128]{3,1,2,0:T(8,128)S(1)} %slice_bitcast_fusion.4), channel_id=15, replica_groups=mesh['gx'=16,'gy'=8] {'gx'}, dimensions={0}, use_global_device_ids=true | all-gather | bytes 696320 | tf_op jit(solution)/shard_map/all_gather | solution.py:14
  558.5 13.2 while.265
  576.9 74.5 %all-reduce.150.cloned.1.call-done = f32[2,2,40,128]{3,2,1,0:T(8,128)} async-done(((f32[2,2,40,128]{3,2,1,0:T(8,128)}), f32[2,2,40,128]{3,2,1,0:T(8,128)}) %all-reduce.150.cloned.1.call-update) | async-done | bytes 81936 | tf_op jit(solution)/shard_map/psum | solution.py:28
  655.7 18.8 all-gather.10
  679.9 21.5 %all-gather.11 = f32[16,40,8,1]{3,1,0,2:T(8,128)} all-gather(f32[2,40,8,1]{3,1,0,2:T(8,128)S(1)} %bitcast.557), channel_id=17, replica_groups=mesh['gx'=16,'gy'=8] {'gy'}, dimensions={0}, use_global_device_ids=true | all-gather | bytes 23040 | tf_op jit(solution)/shard_map/all_gather | solution.py:14
  704.0 4.9 while.267
  710.3 23.2 %gather_fusion = f32[4096]{0:T(1024)S(1)} fusion(f32[81920]{0:T(1024)S(1)} %bitcast.513, s32[4096]{0:T(1024)} %fusion.89), kind=kCustom, calls=%fused_computation.clone | custom fusion | bytes 49152 | tf_op jit(solution)/shard_map/jit(_take)/gather | solution.py:195
  733.6 14.6 all_to_all.42
  749.1 5.7 fusion.2
  756.3 5.6 all-to-all-start.2
  762.0 9.2 all-to-all-done.2
  772.9 22.9 %scatter_custom_fusion.1 = f32[81920]{0:T(1024)} fusion(s32[4096]{0:T(1024)} %bitcast.640, f32[4096]{0:T(1024)S(1)} %reshape.341, f32[]{:T(128)} %constant.419.clone.1), kind=kCustom, calls=%fused_computation.282 | custom fusion | flops 4096 | bytes 328192 | tf_op jit(solution)/shard_map/scatter-add | solution.py:185
  801.0 17.6 all-gather.12
  823.9 21.7 %all-gather.13 = f32[16,40,8,1]{3,1,0,2:T(8,128)} all-gather(f32[2,40,8,1]{3,1,0,2:T(8,128)S(1)} %bitcast.558), channel_id=19, replica_groups=mesh['gx'=16,'gy'=8] {'gy'}, dimensions={0}, use_global_device_ids=true | all-gather | bytes 23040 | tf_op jit(solution)/shard_map/all_gather | solution.py:14
  845.7 2.7 copy.510
  848.4 4.9 while.269
  855.7 24.1 %all-gather.14 = f32[32,40,1,128]{3,1,2,0:T(8,128)} all-gather(f32[2,40,1,128]{3,1,2,0:T(8,128)S(1)} %slice_bitcast_fusion.3), channel_id=20, replica_groups=mesh['gx'=16,'gy'=8] {'gx'}, dimensions={0}, use_global_device_ids=true | all-gather | bytes 696320 | tf_op jit(solution)/shard_map/all_gather | solution.py:14
  880.6 90.7 %all-reduce.152.cloned.1.call-done = f32[2,2,40,128]{3,2,1,0:T(8,128)} async-done(((f32[2,2,40,128]{3,2,1,0:T(8,128)}), f32[2,2,40,128]{3,2,1,0:T(8,128)}) %all-reduce.152.cloned.1.call-update) | async-done | bytes 81936 | tf_op jit(solution)/shard_map/psum | solution.py:28
  973.3 25.7 %all-gather.15 = f32[32,40,1,128]{3,1,2,0:T(8,128)} all-gather(f32[2,40,1,128]{3,1,2,0:T(8,128)S(1)} %slice_bitcast_fusion.2), channel_id=21, replica_groups=mesh['gx'=16,'gy'=8] {'gx'}, dimensions={0}, use_global_device_ids=true | all-gather | bytes 696320 | tf_op jit(solution)/shard_map/all_gather | solution.py:14
  999.1 12.8 while.271
  1015.1 76.5 %all-reduce.154.cloned.1.call-done = f32[2,2,40,128]{3,2,1,0:T(8,128)} async-done(((f32[2,2,40,128]{3,2,1,0:T(8,128)}), f32[2,2,40,128]{3,2,1,0:T(8,128)}) %all-reduce.154.cloned.1.call-update) | async-done | bytes 81936 | tf_op jit(solution)/shard_map/psum | solution.py:28
  1094.3 64.7 %all-reduce.132 = (f32[]{:T(128)}, f32[]{:T(128)}) all-reduce(f32[]{:T(128)} %get-tuple-element.1522, f32[]{:T(128)} %get-tuple-element.1520), channel_id=1, replica_groups=mesh['gx'=16,'gy'=8] {'gx','gy'}, use_global_device_ids=true, to_apply=%region_12.13 | all-reduce | flops 2 | bytes 16 | tf_op jit(solution)/shard_map/psum | solution.py:151
  1161.1 62.0 %psum.106 = f32[]{:T(128)} all-reduce(f32[]{:T(128)} %multiply_reduce_fusion.1), channel_id=1, replica_groups=mesh['gx'=16,'gy'=8] {'gx','gy'}, use_global_device_ids=true, to_apply=%region_37.39 | all-reduce | flops 1 | bytes 8 | tf_op jit(solution)/shard_map/psum | solution.py:151
  1227.7 25.6 %all-gather.16 = f32[32,40,1,128]{3,1,2,0:T(8,128)} all-gather(f32[2,40,1,128]{3,1,2,0:T(8,128)S(1)} %slice_bitcast_fusion.1), channel_id=22, replica_groups=mesh['gx'=16,'gy'=8] {'gx'}, dimensions={0}, use_global_device_ids=true | all-gather | bytes 696320 | tf_op jit(solution)/shard_map/all_gather | solution.py:14
  1254.1 91.4 %all-reduce.156.cloned.1.call-done = f32[2,2,40,128]{3,2,1,0:T(8,128)} async-done(((f32[2,2,40,128]{3,2,1,0:T(8,128)}), f32[2,2,40,128]{3,2,1,0:T(8,128)}) %all-reduce.156.cloned.1.call-update) | async-done | bytes 81936 | tf_op jit(solution)/shard_map/psum | solution.py:28
  1348.8 25.7 %all-gather.17 = f32[32,40,1,128]{3,1,2,0:T(8,128)} all-gather(f32[2,40,1,128]{3,1,2,0:T(8,128)S(1)} %slice_bitcast_fusion), channel_id=23, replica_groups=mesh['gx'=16,'gy'=8] {'gx'}, dimensions={0}, use_global_device_ids=true | all-gather | bytes 696320 | tf_op jit(solution)/shard_map/all_gather | solution.py:14
  1374.6 13.0 while.273
  1390.8 76.5 %all-reduce.158.cloned.1.call-done = f32[2,2,40,128]{3,2,1,0:T(8,128)} async-done(((f32[2,2,40,128]{3,2,1,0:T(8,128)}), f32[2,2,40,128]{3,2,1,0:T(8,128)}) %all-reduce.158.cloned.1.call-update) | async-done | bytes 81936 | tf_op jit(solution)/shard_map/psum | solution.py:28
  1475.8 13.1 all-gather.18
  1490.9 22.7 %all-gather.19 = f32[16,40,8,1]{3,1,0,2:T(8,128)} all-gather(f32[2,40,8,1]{3,1,0,2:T(8,128)S(1)} %bitcast.559), channel_id=25, replica_groups=mesh['gx'=16,'gy'=8] {'gy'}, dimensions={0}, use_global_device_ids=true | all-gather | bytes 23040 | tf_op jit(solution)/shard_map/all_gather | solution.py:14
  1516.3 4.9 while.275
  1522.7 23.2 %gather_fusion.1 = f32[4096]{0:T(1024)S(1)} fusion(f32[81920]{0:T(1024)S(1)} %bitcast.512, s32[4096]{0:T(1024)} %fusion.89), kind=kCustom, calls=%fused_computation.1.clone | custom fusion | bytes 49152 | tf_op jit(solution)/shard_map/jit(_take)/gather | solution.py:195
  1546.0 14.6 all_to_all.43
  1561.5 5.7 fusion
  1568.6 5.7 all-to-all-start.4
  1574.6 9.0 all-to-all-done.4
  1585.3 22.7 %scatter_custom_fusion.2 = f32[81920]{0:T(1024)} fusion(s32[4096]{0:T(1024)} %bitcast.641, f32[4096]{0:T(1024)S(1)} %reshape.349, f32[]{:T(128)} %constant.419.clone.1), kind=kCustom, calls=%fused_computation.280 | custom fusion | flops 4096 | bytes 328192 | tf_op jit(solution)/shard_map/scatter-add | solution.py:185
  1613.7 12.8 all-gather.20
  1629.5 21.4 %all-gather.21 = f32[16,40,8,1]{3,1,0,2:T(8,128)} all-gather(f32[2,40,8,1]{3,1,0,2:T(8,128)S(1)} %bitcast.555), channel_id=27, replica_groups=mesh['gx'=16,'gy'=8] {'gy'}, dimensions={0}, use_global_device_ids=true | all-gather | bytes 23040 | tf_op jit(solution)/shard_map/all_gather | solution.py:14
  1650.9 2.7 copy.571
  1653.6 5.0 while.277
  1659.8 22.1 %all-gather.22 = f32[32,40,1,128]{3,1,2,0:T(8,128)S(1)} all-gather(f32[2,40,1,128]{3,1,2,0:T(8,128)S(1)} %bitcast.616), channel_id=28, replica_groups=mesh['gx'=16,'gy'=8] {'gx'}, dimensions={0}, use_global_device_ids=true | all-gather | bytes 696320 | tf_op jit(solution)/shard_map/all_gather | solution.py:14
  1682.6 90.4 %all-reduce.160.cloned.1.call-done = f32[2,2,40,128]{3,2,1,0:T(8,128)} async-done(((f32[2,2,40,128]{3,2,1,0:T(8,128)}), f32[2,2,40,128]{3,2,1,0:T(8,128)}) %all-reduce.160.cloned.1.call-update) | async-done | bytes 81936 | tf_op jit(solution)/shard_map/psum | solution.py:28
  1774.6 23.5 %all-gather.23 = f32[32,40,1,128]{3,1,2,0:T(8,128)S(1)} all-gather(f32[2,40,1,128]{3,1,2,0:T(8,128)S(1)} %bitcast.614), channel_id=29, replica_groups=mesh['gx'=16,'gy'=8] {'gx'}, dimensions={0}, use_global_device_ids=true | all-gather | bytes 696320 | tf_op jit(solution)/shard_map/all_gather | solution.py:14
  1798.1 12.5 while.279
  1811.4 78.2 %all-reduce.162.cloned.1.call-done = f32[2,2,40,128]{3,2,1,0:T(8,128)} async-done(((f32[2,2,40,128]{3,2,1,0:T(8,128)}), f32[2,2,40,128]{3,2,1,0:T(8,128)}) %all-reduce.162.cloned.1.call-update) | async-done | bytes 81936 | tf_op jit(solution)/shard_map/psum | solution.py:28
  1891.1 64.7 %psum.111 = f32[]{:T(128)} all-reduce(f32[]{:T(128)} %multiply_reduce_fusion), channel_id=1, replica_groups=mesh['gx'=16,'gy'=8] {'gx','gy'}, use_global_device_ids=true, to_apply=%region_60.62 | all-reduce | flops 1 | bytes 8 | tf_op jit(solution)/shard_map/psum | solution.py:151
  (755 shorter events, 222.0 us)
Async XLA Ops:
  7.2 8.9 copy-start.68
  7.2 20.8 %copy-start.62 = (f32[40,8,128]{2,1,0:T(8,128)S(1)}, f32[40,8,128]{2,1,0:T(8,128)}, u32[]{:S(2)}) copy-start(f32[40,8,128]{2,1,0:T(8,128)} %param.50) | copy-start | bytes 491524
  15.9 13.3 copy-start.67
  16.7 77.1 %all-to-all-start = ((f32[128,1,32]{2,1,0:T(1,128)}), f32[128,1,32]{2,1,0:T(1,128)S(1)}, u32[]{:S(2)}, u32[]{:S(2)}) async-start(f32[128,1,32]{2,1,0:T(1,128)} %bitcast.45), calls=%async_computation | async-start | bytes 131072 | tf_op jit(solution)/shard_map/all_to_all | solution.py:181
  27.9 258.0 %all-reduce.144.cloned.1.call-start = ((), (), s32[]{:S(2)}) async-start(), calls=%async_computation.5 | async-start | bytes 163840 | tf_op jit(solution)/shard_map/psum | solution.py:28
  30.3 31.0 %copy-start.69 = (s32[8,128]{1,0:T(8,128)S(1)}, s32[8,128]{1,0:T(8,128)}, u32[]{:S(2)}) copy-start(s32[8,128]{1,0:T(8,128)} %param.51) | copy-start | bytes 12292
  32.5 28.9 %copy-start.43 = (f32[1,40,8,128]{3,2,1,0:T(8,128)}, f32[1,40,8,128]{3,2,1,0:T(8,128)S(1)}, u32[]{:S(2)}) copy-start(f32[1,40,8,128]{3,2,1,0:T(8,128)S(1)} %get-tuple-element.1550) | copy-start | bytes 491524
  32.5 32.5 %copy-start.41 = (f32[1,40,8,128]{3,2,1,0:T(8,128)}, f32[1,40,8,128]{3,2,1,0:T(8,128)S(1)}, u32[]{:S(2)}) copy-start(f32[1,40,8,128]{3,2,1,0:T(8,128)S(1)} %get-tuple-element.1551) | copy-start | bytes 491524
  33.2 28.2 %copy-start.45 = (f32[1,40,8,128]{3,2,1,0:T(8,128)}, f32[1,40,8,128]{3,2,1,0:T(8,128)S(1)}, u32[]{:S(2)}) copy-start(f32[1,40,8,128]{3,2,1,0:T(8,128)S(1)} %get-tuple-element.1585) | copy-start | bytes 491524
  33.3 28.5 %copy-start.58 = (f32[1,40,8,128]{3,2,1,0:T(8,128)}, f32[1,40,8,128]{3,2,1,0:T(8,128)S(1)}, u32[]{:S(2)}) copy-start(f32[1,40,8,128]{3,2,1,0:T(8,128)S(1)} %pad_multiply_fusion.31) | copy-start | bytes 491524
  61.4 60.6 %copy-start.21 = (f32[40,8,128]{2,0,1:T(8,128)}, f32[40,8,128]{2,0,1:T(8,128)S(1)}, u32[]{:S(2)}) copy-start(f32[40,8,128]{2,0,1:T(8,128)S(1)} %copy.433) | copy-start | bytes 491524
  61.5 60.9 %copy-start.17 = (f32[40,8,128]{2,0,1:T(8,128)}, f32[40,8,128]{2,0,1:T(8,128)S(1)}, u32[]{:S(2)}) copy-start(f32[40,8,128]{2,0,1:T(8,128)S(1)} %copy.436) | copy-start | bytes 491524
  61.5 61.2 %copy-start.12 = (f32[40,8,128]{2,0,1:T(8,128)}, f32[40,8,128]{2,0,1:T(8,128)S(1)}, u32[]{:S(2)}) copy-start(f32[40,8,128]{2,0,1:T(8,128)S(1)} %copy.439) | copy-start | bytes 491524
  61.6 61.5 %copy-start.7 = (f32[40,8,128]{2,0,1:T(8,128)}, f32[40,8,128]{2,0,1:T(8,128)S(1)}, u32[]{:S(2)}) copy-start(f32[40,8,128]{2,0,1:T(8,128)S(1)} %copy.442) | copy-start | bytes 491524
  61.6 61.9 %copy-start.2 = (f32[40,8,128]{2,0,1:T(8,128)}, f32[40,8,128]{2,0,1:T(8,128)S(1)}, u32[]{:S(2)}) copy-start(f32[40,8,128]{2,0,1:T(8,128)S(1)} %copy.445) | copy-start | bytes 491524
  61.7 739.0 %copy-start = (f32[40,8,128]{2,0,1:T(8,128)}, f32[40,8,128]{2,0,1:T(8,128)S(1)}, u32[]{:S(2)}) copy-start(f32[40,8,128]{2,0,1:T(8,128)S(1)} %copy.448) | copy-start | bytes 491524
  65.0 345.3 %copy-start.26 = (f32[40,8,128]{2,0,1:T(8,128)}, f32[40,8,128]{2,0,1:T(8,128)S(1)}, u32[]{:S(2)}) copy-start(f32[40,8,128]{2,0,1:T(8,128)S(1)} %copy.474) | copy-start | bytes 491524
  66.0 344.4 %copy-start.23 = (f32[40,8,128]{2,0,1:T(8,128)}, f32[40,8,128]{2,0,1:T(8,128)S(1)}, u32[]{:S(2)}) copy-start(f32[40,8,128]{2,0,1:T(8,128)S(1)} %copy.477) | copy-start | bytes 491524
  124.2 14.8 copy-start.40
  165.8 26.1 %copy-start.51 = (f32[16,40,1,128]{3,1,2,0:T(8,128)S(1)}, f32[16,40,1,128]{3,1,2,0:T(8,128)}, u32[]{:S(2)}) copy-start(f32[16,40,1,128]{3,1,2,0:T(8,128)} %all-gather.4) | copy-start | bytes 983044
  166.1 27.5 %copy-start.44 = (f32[1,40,8,128]{3,2,1,0:T(8,128)S(1)}, f32[1,40,8,128]{3,2,1,0:T(8,128)}, u32[]{:S(2)}) copy-start(f32[1,40,8,128]{3,2,1,0:T(8,128)} %get-tuple-element.1584) | copy-start | bytes 491524
  166.2 29.1 %copy-start.59 = (f32[1,40,8,128]{3,2,1,0:T(8,128)S(1)}, f32[1,40,8,128]{3,2,1,0:T(8,128)}, u32[]{:S(2)}) copy-start(f32[1,40,8,128]{3,2,1,0:T(8,128)} %copy-done.58) | copy-start | bytes 491524
  166.2 29.1 %copy-start.42 = (f32[1,40,8,128]{3,2,1,0:T(8,128)S(1)}, f32[1,40,8,128]{3,2,1,0:T(8,128)}, u32[]{:S(2)}) copy-start(f32[1,40,8,128]{3,2,1,0:T(8,128)} %copy-done.41) | copy-start | bytes 491524
  166.6 25.4 %copy-start.46 = (f32[2,40,8,128]{3,2,1,0:T(8,128)}, f32[2,40,8,128]{3,2,1,0:T(8,128)S(1)}, u32[]{:S(2)}) copy-start(f32[2,40,8,128]{3,2,1,0:T(8,128)S(1)} %copy_add_fusion.23) | copy-start | bytes 983044
  193.6 213.9 %all-reduce.146.cloned.1.call-start = ((), (), s32[]{:S(2)}) async-start(), calls=%async_computation.6 | async-start | bytes 163840 | tf_op jit(solution)/shard_map/psum | solution.py:28
  194.6 133.2 %copy-start.55 = (f32[1,40,1,128]{3,2,1,0:T(1,128)}, f32[1,40,1,128]{3,2,1,0:T(1,128)S(1)}, u32[]{:S(2)}) copy-start(f32[1,40,1,128]{3,2,1,0:T(1,128)S(1)} %slice.784) | copy-start | bytes 61444
  195.4 118.6 %copy-start.33 = (f32[40,8,128]{2,0,1:T(8,128)}, f32[40,8,128]{2,0,1:T(8,128)S(1)}, u32[]{:S(2)}) copy-start(f32[40,8,128]{2,0,1:T(8,128)S(1)} %copy.486) | copy-start | bytes 491524
  196.4 118.5 %copy-start.28 = (f32[40,8,128]{2,0,1:T(8,128)}, f32[40,8,128]{2,0,1:T(8,128)S(1)}, u32[]{:S(2)}) copy-start(f32[40,8,128]{2,0,1:T(8,128)S(1)} %copy.487) | copy-start | bytes 491524
  285.9 28.1 %copy-start.52 = (f32[16,40,1,128]{3,1,2,0:T(8,128)S(1)}, f32[16,40,1,128]{3,1,2,0:T(8,128)}, u32[]{:S(2)}) copy-start(f32[16,40,1,128]{3,1,2,0:T(8,128)} %all-gather.6) | copy-start | bytes 983044
  287.9 27.1 %copy-start.37 = (f32[2,40,8,128]{3,2,1,0:T(8,128)}, f32[2,40,8,128]{3,2,1,0:T(8,128)S(1)}, u32[]{:S(2)}) copy-start(f32[2,40,8,128]{3,2,1,0:T(8,128)S(1)} %copy_add_fusion.22) | copy-start | bytes 983044
  288.3 26.7 %copy-start.47 = (f32[2,40,8,128]{3,1,0,2:T(8,128)}, f32[2,40,8,128]{3,1,0,2:T(8,128)S(1)}, u32[]{:S(2)}) copy-start(f32[2,40,8,128]{3,1,0,2:T(8,128)S(1)} %multiply_add_fusion.71) | copy-start | bytes 983044
  329.2 201.0 %all-reduce.148.cloned.1.call-start = ((), (), s32[]{:S(2)}) async-start(), calls=%async_computation.7 | async-start | bytes 163840 | tf_op jit(solution)/shard_map/psum | solution.py:28
  410.5 122.2 %copy-start.29 = (f32[40,8,128]{2,0,1:T(8,128)S(1)}, f32[40,8,128]{2,0,1:T(8,128)}, u32[]{:S(2)}) copy-start(f32[40,8,128]{2,0,1:T(8,128)} %copy-done.28) | copy-start | bytes 491524
  437.1 214.3 %all-reduce.150.cloned.1.call-start = ((), (), s32[]{:S(2)}) async-start(), calls=%async_computation.8 | async-start | bytes 163840 | tf_op jit(solution)/shard_map/psum | solution.py:28
  532.7 25.8 %copy-start.48 = (f32[2,40,8,128]{3,1,0,2:T(8,128)}, f32[2,40,8,128]{3,1,0,2:T(8,128)S(1)}, u32[]{:S(2)}) copy-start(f32[2,40,8,128]{3,1,0,2:T(8,128)S(1)} %multiply_add_fusion.64) | copy-start | bytes 983044
  651.4 3.8 copy-start.3
  710.3 23.2 %copy-start.66 = (s32[4096]{0:T(1024)S(1)}, s32[4096]{0:T(1024)}, u32[]{:S(2)}) copy-start(s32[4096]{0:T(1024)} %reshape_squeeze.10) | copy-start | bytes 49156
  754.8 45.6 %copy-start.9 = (f32[40,8,128]{2,0,1:T(8,128)S(1)}, f32[40,8,128]{2,0,1:T(8,128)}, u32[]{:S(2)}) copy-start(f32[40,8,128]{2,0,1:T(8,128)} %copy-done.7) | copy-start | bytes 491524
  754.8 45.7 %copy-start.4 = (f32[40,8,128]{2,0,1:T(8,128)S(1)}, f32[40,8,128]{2,0,1:T(8,128)}, u32[]{:S(2)}) copy-start(f32[40,8,128]{2,0,1:T(8,128)} %copy-done.2) | copy-start | bytes 491524
  756.3 14.9 all-to-all-start.2
  761.9 209.3 %all-reduce.152.cloned.1.call-start = ((), (), s32[]{:S(2)}) async-start(), calls=%async_computation.9 | async-start | bytes 163840 | tf_op jit(solution)/shard_map/psum | solution.py:28
  795.8 4.4 copy-start.14
  845.7 10.0 copy-start.24
  855.7 117.6 %copy-start.30 = (f32[40,8,128]{2,0,1:T(8,128)S(1)}, f32[40,8,128]{2,0,1:T(8,128)}, u32[]{:S(2)}) copy-start(f32[40,8,128]{2,0,1:T(8,128)} %copy-done.28) | copy-start | bytes 491524
  880.5 131.4 %copy-start.56 = (f32[1,40,1,128]{3,2,1,0:T(1,128)S(1)}, f32[1,40,1,128]{3,2,1,0:T(1,128)}, u32[]{:S(2)}) copy-start(f32[1,40,1,128]{3,2,1,0:T(1,128)} %copy-done.55) | copy-start | bytes 61444
  880.5 211.1 %all-reduce.154.cloned.1.call-start = ((), (), s32[]{:S(2)}) async-start(), calls=%async_computation.10 | async-start | bytes 163840 | tf_op jit(solution)/shard_map/psum | solution.py:28
  973.3 25.8 %copy-start.49 = (f32[2,40,8,128]{3,1,0,2:T(8,128)}, f32[2,40,8,128]{3,1,0,2:T(8,128)S(1)}, u32[]{:S(2)}) copy-start(f32[2,40,8,128]{3,1,0,2:T(8,128)S(1)} %multiply_add_fusion.27) | copy-start | bytes 983044
  1013.4 332.1 %all-reduce.156.cloned.1.call-start = ((), (), s32[]{:S(2)}) async-start(), calls=%async_computation.11 | async-start | bytes 163840 | tf_op jit(solution)/shard_map/psum | solution.py:28
  1094.3 128.7 %copy-start.35 = (f32[2,40,8,128]{3,1,0,2:T(8,128)}, f32[2,40,8,128]{3,1,0,2:T(8,128)S(1)}, u32[]{:S(2)}) copy-start(f32[2,40,8,128]{3,1,0,2:T(8,128)S(1)} %get-tuple-element.1521) | copy-start | bytes 983044
  1226.7 121.2 %copy-start.31 = (f32[40,8,128]{2,0,1:T(8,128)S(1)}, f32[40,8,128]{2,0,1:T(8,128)}, u32[]{:S(2)}) copy-start(f32[40,8,128]{2,0,1:T(8,128)} %copy-done.28) | copy-start | bytes 491524
  1254.0 213.3 %all-reduce.158.cloned.1.call-start = ((), (), s32[]{:S(2)}) async-start(), calls=%async_computation.12 | async-start | bytes 163840 | tf_op jit(solution)/shard_map/psum | solution.py:28
  1348.0 26.6 %copy-start.50 = (f32[2,40,8,128]{3,1,0,2:T(8,128)}, f32[2,40,8,128]{3,1,0,2:T(8,128)S(1)}, u32[]{:S(2)}) copy-start(f32[2,40,8,128]{3,1,0,2:T(8,128)S(1)} %multiply_add_fusion.18) | copy-start | bytes 983044
  1389.0 83.0 %copy-start.19 = (f32[40,8,128]{2,0,1:T(8,128)S(1)}, f32[40,8,128]{2,0,1:T(8,128)}, u32[]{:S(2)}) copy-start(f32[40,8,128]{2,0,1:T(8,128)} %copy-done.17) | copy-start | bytes 491524
  1561.5 49.1 %copy-start.22 = (f32[40,8,128]{2,0,1:T(8,128)S(1)}, f32[40,8,128]{2,0,1:T(8,128)}, u32[]{:S(2)}) copy-start(f32[40,8,128]{2,0,1:T(8,128)} %copy-done.21) | copy-start | bytes 491524
  1567.2 43.7 %copy-start.20 = (f32[40,8,128]{2,0,1:T(8,128)S(1)}, f32[40,8,128]{2,0,1:T(8,128)}, u32[]{:S(2)}) copy-start(f32[40,8,128]{2,0,1:T(8,128)} %copy-done.17) | copy-start | bytes 491524
  1568.6 15.0 all-to-all-start.4
  1574.3 198.7 %all-reduce.160.cloned.1.call-start = ((), (), s32[]{:S(2)}) async-start(), calls=%async_computation.13 | async-start | bytes 163840 | tf_op jit(solution)/shard_map/psum | solution.py:28
  1650.9 8.4 copy-start.27
  1653.6 5.9 copy-start.25
  1659.6 114.7 %copy-start.34 = (f32[40,8,128]{2,0,1:T(8,128)S(1)}, f32[40,8,128]{2,0,1:T(8,128)}, u32[]{:S(2)}) copy-start(f32[40,8,128]{2,0,1:T(8,128)} %copy-done.33) | copy-start | bytes 491524
  1681.8 92.5 %copy-start.32 = (f32[40,8,128]{2,0,1:T(8,128)S(1)}, f32[40,8,128]{2,0,1:T(8,128)}, u32[]{:S(2)}) copy-start(f32[40,8,128]{2,0,1:T(8,128)} %copy-done.28) | copy-start | bytes 491524
  1682.6 207.1 %all-reduce.162.cloned.1.call-start = ((), (), s32[]{:S(2)}) async-start(), calls=%async_computation.14 | async-start | bytes 163840 | tf_op jit(solution)/shard_map/psum | solution.py:28
  1774.0 36.7 %copy-start.57 = (f32[1,40,1,128]{3,2,1,0:T(1,128)S(1)}, f32[1,40,1,128]{3,2,1,0:T(1,128)}, u32[]{:S(2)}) copy-start(f32[1,40,1,128]{3,2,1,0:T(1,128)} %copy-done.55) | copy-start | bytes 61444
  1774.2 182.9 %copy-start.36 = (f32[2,40,8,128]{3,1,0,2:T(8,128)S(1)}, f32[2,40,8,128]{3,1,0,2:T(8,128)}, u32[]{:S(2)}) copy-start(f32[2,40,8,128]{3,1,0,2:T(8,128)} %copy-done.35) | copy-start | bytes 983044
  (19 other events, 34.3 us)
Sparse Core Ops, SparseCore 0:
  193.7 92.1 all-reduce.143
  329.3 78.0 all-reduce.145
  437.2 92.9 all-reduce.147
  573.3 78.0 all-reduce.149
  880.7 90.5 all-reduce.151
  1013.5 78.1 all-reduce.153
  1254.1 91.2 all-reduce.155
  1389.2 78.0 all-reduce.157
  1682.7 90.2 all-reduce.159
  1811.5 78.0 all-reduce.161
where the time goes:
time: 1980 us; the launch traced here: 1970 us
  waiting for transfers between devices  817 us (41%)
  blocking collectives  739 us (37%)
  other arithmetic  234 us (12%)
  local copies, waits for them, and re-layouts  109 us (6%)
  starting transfers between devices  23.2 us (1%)
  between operations  22.2 us (1%)
    psum x10, waiting for transfers between devices, from_root(): return lax.psum(kept, axis)  799 us
    all_gather x24, blocking collectives, entering_2(): gathered = jax.tree.map(lambda a: lax.all_gather(a, axis), part)  519 us
    psum x3, blocking collectives, global_dot(): return lax.psum(jnp.sum(first_field * second_field), ('gx', 'gy'))  191 us
    add x110, other arithmetic, compose_maps(): return (earlier[0] * following[0], following[0] * earlier[1] + following[1])  81.4 us
    scatter-add x3, other arithmetic, deposit(): flat_cells = jnp.zeros((TR * rate_x.size,), jnp.float32).at[cell_index.re...  68.6 us
    gather x2, local copies, waits for them, and re-layouts, on_device(): jnp.take((ocean * along_y(along_x(ocean * direction))).reshape(-1), cell_...  46.3 us
  transfers between devices with their start and end apart: 13, of which 12 were waited for; matrix products, arithmetic and copies ran while one was open for 1% of the time, Pallas kernels for 0%

commit v1 on v0

v1 whole, which is shorter than its diff:
```python
import jax
import jax.numpy as jnp
from jax import lax
from jax.sharding import PartitionSpec as P

TR = 2
ITERS = 2


def shift_along(values, distance, line_axis, reverse, filler):
    length = values.shape[line_axis]
    edge_shape = list(values.shape)
    edge_shape[line_axis] = distance
    edge = jnp.full(tuple(edge_shape), filler, values.dtype)
    if reverse:
        return jnp.concatenate(
            [lax.slice_in_dim(values, distance, length, axis=line_axis), edge], axis=line_axis
        )
    return jnp.concatenate(
        [edge, lax.slice_in_dim(values, 0, length - distance, axis=line_axis)], axis=line_axis
    )


def factor_levels(retention, line_axis, reverse):
    length = retention.shape[line_axis]
    stored = []
    factor = retention
    distance = 1
    while distance < length:
        stored.append(factor)
        factor = factor * shift_along(factor, distance, line_axis, reverse, 1.0)
        distance = distance * 2
    return (stored, factor)


def scan_offsets(stored, forcing, line_axis, reverse):
    distance = 1
    for level_factor in stored:
        forcing = forcing + level_factor * shift_along(forcing, distance, line_axis, reverse, 0.0)
        distance = distance * 2
    return forcing


def make_plan(decay_rate, line_axis, axis_name, periodic):
    retention = jnp.exp(-decay_rate)[None]
    one_minus = -jnp.expm1(-decay_rate)
    scaling = jnp.sqrt(one_minus * (1.0 + jnp.exp(-decay_rate)))
    weight = jnp.sqrt(jnp.sqrt(one_minus))
    length = retention.shape[line_axis]
    forward_stored, prefix = factor_levels(retention, line_axis, False)
    backward_stored, suffix = factor_levels(retention, line_axis, True)
    back_of_prefix = scan_offsets(backward_stored, retention * prefix, line_axis, True)
    totals = jnp.stack(
        [
            lax.index_in_dim(prefix, length - 1, line_axis, keepdims=False),
            lax.index_in_dim(suffix, 0, line_axis, keepdims=False),
            lax.index_in_dim(back_of_prefix, 0, line_axis, keepdims=False),
        ]
    )
    return dict(
        retention=retention,
        gain=scaling * weight,
        gain_out=weight * scaling,
        forward_stored=forward_stored,
        backward_stored=backward_stored,
        prefix=prefix,
        suffix=suffix,
        back_of_prefix=back_of_prefix,
        rate_totals=lax.all_gather(totals, axis_name),
        axis_name=axis_name,
        periodic=periodic,
        line_axis=line_axis,
    )


def carries(got, rate_totals, periodic, axis_name):
    count = got.shape[0]
    offsets = [got[k, 0] for k in range(count)]
    back_parts = [got[k, 1] for k in range(count)]
    factors = [rate_totals[k, 0] for k in range(count)]
    back_factors = [rate_totals[k, 1] for k in range(count)]
    back_gains = [rate_totals[k, 2] for k in range(count)]
    if periodic:
        total = offsets[0]
        product = factors[0]
        for k in range(1, count):
            total = factors[k] * total + offsets[k]
            product = product * factors[k]
        first = total / (1.0 - product)
    else:
        first = jnp.zeros_like(offsets[0])
    entering = [first]
    for k in range(count - 1):
        entering.append(offsets[k] + factors[k] * entering[k])
    back_totals = [back_parts[k] + entering[k] * back_gains[k] for k in range(count)]
    if periodic:
        total = back_totals[count - 1]
        product = back_factors[count - 1]
        for k in range(count - 2, -1, -1):
            total = back_totals[k] + back_factors[k] * total
            product = product * back_factors[k]
        last = total / (1.0 - product)
    else:
        last = jnp.zeros_like(offsets[0])
    leaving = [None] * count
    leaving[count - 1] = last
    for k in range(count - 2, -1, -1):
        leaving[k] = back_totals[k + 1] + back_factors[k + 1] * leaving[k + 1]
    place = lax.axis_index(axis_name)
    mine_in = lax.dynamic_index_in_dim(jnp.stack(entering), place, 0, False)
    mine_out = lax.dynamic_index_in_dim(jnp.stack(leaving), place, 0, False)
    return mine_in, mine_out


def line_operator(state_field, plan):
    line_axis = plan["line_axis"]
    length = state_field.shape[line_axis]
    offset = scan_offsets(plan["forward_stored"], plan["gain"] * state_field, line_axis, False)
    back_offset = scan_offsets(
        plan["backward_stored"], plan["retention"] * offset, line_axis, True
    )
    mine = jnp.stack(
        [
            lax.index_in_dim(offset, length - 1, line_axis, keepdims=False),
            lax.index_in_dim(back_offset, 0, line_axis, keepdims=False),
        ]
    )
    got = lax.all_gather(mine, plan["axis_name"])
    entering, leaving = carries(got, plan["rate_totals"], plan["periodic"], plan["axis_name"])
    entering = jnp.expand_dims(entering, line_axis)
    leaving = jnp.expand_dims(leaving, line_axis)
    forward = offset + plan["prefix"] * entering
    back_offset = back_offset + entering * plan["back_of_prefix"]
    next_factor = shift_along(plan["suffix"], 1, line_axis, True, 1.0)
    next_offset = shift_along(back_offset, 1, line_axis, True, 0.0)
    return plan["gain_out"] * (forward + next_offset + next_factor * leaving)


def global_dot(first_field, second_field):
    return lax.psum(jnp.sum(first_field * second_field), ("gx", "gy"))


def on_device(rate_x, rate_y, land_mask, obs_cell, obs_count, innovation, obs_weight):
    ocean = land_mask.astype(jnp.float32)
    field_shape = (TR,) + rate_x.shape
    plan_along_x = make_plan(rate_x, 2, "gx", True)
    plan_along_y = make_plan(rate_y, 3, "gy", False)

    def along_x(state_field):
        return line_operator(state_field, plan_along_x)

    def along_y(state_field):
        return line_operator(state_field, plan_along_y)

    def gather_back(vector):
        return ocean * along_x(along_y(ocean * vector))

    cell_index = obs_cell[0]
    occupied = (
        lax.broadcasted_iota(jnp.int32, cell_index.shape, 1) < obs_count[0][:, None]
    ).astype(jnp.float32)
    blocks = obs_weight[0]

    def weigh_obs(values):
        packed = (occupied * values).reshape(blocks.shape[0], blocks.shape[1])
        mixed = jnp.einsum("nij,nj->ni", blocks, packed, precision=lax.Precision.HIGHEST)
        return occupied * mixed.reshape(occupied.shape)

    def deposit(values):
        arrived = lax.all_to_all(values, ("gx", "gy"), split_axis=0, concat_axis=0, tiled=True)
        flat_cells = (
            jnp.zeros((TR * rate_x.size,), jnp.float32)
            .at[cell_index.reshape(-1)]
            .add(arrived.reshape(-1))
        )
        return flat_cells.reshape(field_shape)

    right_side = gather_back(deposit(weigh_obs(innovation[0])))
    solution = jnp.zeros_like(right_side)
    residual = right_side
    direction = right_side
    norm_now = global_dot(residual, residual)
    for iteration in range(ITERS):
        picked = jnp.take(
            (ocean * along_y(along_x(ocean * direction))).reshape(-1),
            cell_index.reshape(-1),
            axis=0,
        ).reshape(cell_index.shape)
        hessian_dir = direction + gather_back(
            deposit(
                weigh_obs(
                    lax.all_to_all(picked, ("gx", "gy"), split_axis=0, concat_axis=0, tiled=True)
                )
            )
        )
        step_length = norm_now / global_dot(direction, hessian_dir)
        solution = solution + step_length * direction
        residual = residual - step_length * hessian_dir
        norm_next = global_dot(residual, residual)
        direction = residual + norm_next / norm_now * direction
        norm_now = norm_next
    return (solution, residual)


def solution(mesh):
    placed = (
        P(None, "gx", "gy"),
        P(None, "gx", "gy"),
        P("gx", "gy"),
        P(("gx", "gy"), None, None),
        P(("gx", "gy"), None),
        P(("gx", "gy"), None, None),
        P(("gx", "gy"), None, None, None),
    )
    return jax.shard_map(
        on_device,
        mesh=mesh,
        in_specs=placed,
        out_specs=(P(None, None, "gx", "gy"), P(None, None, "gx", "gy")),
        check_vma=False,
    )
```

time: 1980 us -> 890 us (0.45)
  waiting for transfers between devices: 817 us -> 187 us
  blocking collectives: 739 us -> 328 us
  other arithmetic: 234 us -> 146 us
  local copies, waits for them, and re-layouts: 109 us -> 155 us
    psum x10 -> x0, waiting for transfers between devices: 799 us -> none  [from_root(): return lax.psum(kept, axis)]
    all_gather x24 -> x7, blocking collectives: 519 us -> 104 us  [the longest x5 64.7 us: line_operator(): got = lax.all_gather(mine, plan['axis_name'])]
    all_gather x0 -> x5, waiting for transfers between devices: none -> 169 us  [line_operator(): got = lax.all_gather(mine, plan['axis_name'])]
    add x127 -> x10, other arithmetic: 96.1 us -> 3.39 us  [line_operator(): back_offset = back_offset + entering * plan['back_of_prefix']]
    unnamed x179 -> x616, local copies, waits for them, and re-layouts: 10.2 us -> 46.4 us
    unnamed x1 -> x56, other arithmetic: 1.32 us -> 21.2 us
  transfers between devices with their start and end apart: 13 -> 8, of which waited for: 12 -> 7; matrix products, arithmetic and copies ran while one was open for 1% -> 3% of each run, Pallas kernels for 0% -> 0%
where the time goes in v1:
time: 890 us; the launch traced here: 879 us
  blocking collectives  328 us (37%)
  waiting for transfers between devices  187 us (21%)
  local copies, waits for them, and re-layouts  155 us (17%)
  other arithmetic  146 us (16%)
  between operations  24.5 us (3%)
  starting transfers between devices  21.5 us (2%)
  matrix products  17 us (2%)
    psum x3, blocking collectives, global_dot(): return lax.psum(jnp.sum(first_field * second_field), ('gx', 'gy'))  191 us
    all_gather x5, waiting for transfers between devices, line_operator(): got = lax.all_gather(mine, plan['axis_name'])  169 us
    scatter-add x3, other arithmetic, deposit(): flat_cells = jnp.zeros((TR * rate_x.size,), jnp.float32).at[cell_index.re...  67.8 us
    all_gather x5, blocking collectives, line_operator(): got = lax.all_gather(mine, plan['axis_name'])  64.7 us
    gather x2, local copies, waits for them, and re-layouts, on_device(): jnp.take((ocean * along_y(along_x(ocean * direction))).reshape(-1), cell_...  63.8 us
    unnamed x616, local copies, waits for them, and re-layouts  46.4 us
    all_gather x2, blocking collectives, make_plan(): lax.all_gather(totals, axis_name)  39 us
    all_to_all x2, blocking collectives, on_device(): lax.all_to_all(picked, ('gx', 'gy'), split_axis=0, concat_axis=0, tiled=T...  33.3 us
  transfers between devices with their start and end apart: 8, of which 7 were waited for; matrix products, arithmetic and copies ran while one was open for 3% of the time, Pallas kernels for 0%

profile of v1, /device:TPU:0, one launch (start us, length us, event | category | flops | bytes accessed | tf_op | source)
XLA Modules:
  0.0 878.7 jit_solution(8408309512666178443)
XLA Ops:
  7.7 1.3 reduce.18
  10.9 5.7 fusion.4
  17.4 11.7 %all-to-all-start = ((f32[128,1,32]{2,1,0:T(1,128)}), f32[128,1,32]{2,1,0:T(1,128)}, u32[]{:S(2)}, u32[]{:S(2)}) async-start(f32[128,1,32]{2,1,0:T(1,128)} %bitcast.5), calls=%async_computation | async-start | bytes 131072 | tf_op jit(solution)/shard_map/all_to_all | solution.py:170
  33.2 12.7 %all-gather.1 = f32[24,1,40,8]{2,3,1,0:T(8,128)S(1)} all-gather(f32[3,1,40,8]{2,3,1,0:T(8,128)S(1)} %pad_maximum_fusion.11), channel_id=3, replica_groups=mesh['gx'=16,'gy'=8] {'gy'}, dimensions={0}, use_global_device_ids=true | all-gather | bytes 34560 | tf_op jit(solution)/shard_map/all_gather | solution.py:69
  50.6 1.6 pad_bitcast_fusion.1
  55.5 1.1 copy.1574
  56.6 1.0 slice.2210
  58.3 0.9 copy.1595
  61.3 1.7 reduce.19
  63.1 22.9 %scatter_custom_fusion = f32[81920]{0:T(1024)} fusion(s32[4096]{0:T(1024)} %bitcast.2403, f32[4096]{0:T(1024)S(1)} %reshape.27287, f32[]{:T(128)} %constant.105.clone.1), kind=kCustom, calls=%fused_computation.490 | custom fusion | flops 4096 | bytes 328192 | tf_op jit(solution)/shard_map/scatter-add | solution.py:174
  86.1 1.1 multiply_multiply_fusion.6
  94.1 1.1 copy.1559
  95.3 1.2 copy.1551
  96.4 12.9 %all-gather = f32[16,2,40,8]{2,3,1,0:T(8,128)S(1)} all-gather(f32[2,2,40,8]{2,3,1,0:T(8,128)S(1)} %pad_maximum_fusion.6), channel_id=2, replica_groups=mesh['gx'=16,'gy'=8] {'gy'}, dimensions={0}, use_global_device_ids=true | all-gather | bytes 46080 | tf_op jit(solution)/shard_map/all_gather | solution.py:128
  115.4 1.0 slice.2248
  116.5 1.0 slice.2286
  118.2 0.9 pad_bitcast_fusion
  119.2 26.2 %all-gather.2 = f32[48,1,40,128]{3,2,1,0:T(8,128)S(1)} all-gather(f32[3,1,40,128]{3,2,1,0:T(8,128)S(1)} %pad_maximum_fusion.5), channel_id=4, replica_groups=mesh['gx'=16,'gy'=8] {'gx'}, dimensions={0}, use_global_device_ids=true | all-gather | bytes 1044480 | tf_op jit(solution)/shard_map/all_gather | solution.py:69
  148.9 10.0 %all-gather.18.cloned.1.call-done = f32[32,2,40,128]{3,2,1,0:T(8,128)} async-done(((f32[2,2,40,128]{3,2,1,0:T(8,128)}), f32[32,2,40,128]{3,2,1,0:T(8,128)}) %all-gather.18.cloned.1.call-update) | async-done | bytes 1310736 | tf_op jit(solution)/shard_map/all_gather | solution.py:128
  158.9 1.8 constant_dynamic-update-slice_fusion.47
  166.9 0.9 reshape_squeeze.10
  169.1 39.9 %all-gather.20.cloned.1.call-done = f32[32,2,40,128]{3,2,1,0:T(8,128)} async-done(((f32[2,2,40,128]{3,2,1,0:T(8,128)}), f32[32,2,40,128]{3,2,1,0:T(8,128)}) %all-gather.20.cloned.1.call-update) | async-done | bytes 1310736 | tf_op jit(solution)/shard_map/all_gather | solution.py:128
  209.0 1.9 constant_dynamic-update-slice_fusion.79
  218.2 1.7 copy.1652
  219.9 1.7 copy.1651
  222.4 13.0 %all-gather.5 = f32[16,2,40,8]{2,3,1,0:T(8,128)S(1)} all-gather(f32[2,2,40,8]{2,3,1,0:T(8,128)S(1)} %pad_maximum_fusion.7), channel_id=7, replica_groups=mesh['gx'=16,'gy'=8] {'gy'}, dimensions={0}, use_global_device_ids=true | all-gather | bytes 46080 | tf_op jit(solution)/shard_map/all_gather | solution.py:128
  239.8 1.3 constant_dynamic-update-slice_fusion.89
  241.8 1.2 slice_add_fusion.6
  243.4 40.7 %gather_fusion = f32[4096]{0:T(1024)} fusion(f32[81920]{0:T(1024)S(1)} %bitcast.2258, s32[4096]{0:T(1024)} %fusion.140), kind=kCustom, calls=%fused_computation.clone | custom fusion | bytes 49152 | tf_op jit(solution)/shard_map/jit(_take)/gather | solution.py:184
  284.1 1.3 broadcast_select_fusion.1
  285.5 16.4 %all_to_all.42 = f32[128,1,32]{2,1,0:T(1,128)S(1)} all-to-all(f32[128,1,32]{2,1,0:T(1,128)S(1)} %bitcast.2380), channel_id=1, replica_groups=mesh['gx'=16,'gy'=8] {'gx','gy'}, dimensions={0} | all-to-all | bytes 32768 | tf_op jit(solution)/shard_map/all_to_all | solution.py:192
  303.6 5.7 fusion.2
  310.1 4.8 all-to-all-start.2
  315.5 8.6 all-to-all-done.2
  325.1 22.7 %scatter_custom_fusion.1 = f32[81920]{0:T(1024)} fusion(s32[4096]{0:T(1024)} %bitcast.2404, f32[4096]{0:T(1024)S(1)} %reshape.27295, f32[]{:T(128)} %constant.105.clone.1), kind=kCustom, calls=%fused_computation.488 | custom fusion | flops 4096 | bytes 328192 | tf_op jit(solution)/shard_map/scatter-add | solution.py:174
  347.8 1.0 fusion.24
  348.9 1.2 multiply_add_fusion.41
  355.3 1.7 copy.1662
  357.0 1.7 copy.1661
  359.5 12.7 %all-gather.6 = f32[16,2,40,8]{2,3,1,0:T(8,128)S(1)} all-gather(f32[2,2,40,8]{2,3,1,0:T(8,128)S(1)} %pad_maximum_fusion.8), channel_id=8, replica_groups=mesh['gx'=16,'gy'=8] {'gy'}, dimensions={0}, use_global_device_ids=true | all-gather | bytes 46080 | tf_op jit(solution)/shard_map/all_gather | solution.py:128
  376.7 1.3 constant_dynamic-update-slice_fusion.105
  378.7 1.2 slice_add_fusion.5
  384.2 39.6 %all-gather.22.cloned.1.call-done = f32[32,2,40,128]{3,2,1,0:T(8,128)} async-done(((f32[2,2,40,128]{3,2,1,0:T(8,128)}), f32[32,2,40,128]{3,2,1,0:T(8,128)}) %all-gather.22.cloned.1.call-update) | async-done | bytes 1310736 | tf_op jit(solution)/shard_map/all_gather | solution.py:128
  423.9 1.9 constant_dynamic-update-slice_fusion.143
  428.0 1.5 multiply_reduce_fusion.2
  429.5 64.6 %all-reduce.142 = (f32[]{:T(128)}, f32[]{:T(128)}) all-reduce(f32[]{:T(128)} %get-tuple-element.6, f32[]{:T(128)} %get-tuple-element.5), channel_id=1, replica_groups=mesh['gx'=16,'gy'=8] {'gx','gy'}, use_global_device_ids=true, to_apply=%region_2.3 | all-reduce | flops 2 | bytes 16 | tf_op jit(solution)/shard_map/psum | solution.py:140
  495.5 1.7 multiply_reduce_fusion.1
  497.1 62.2 %psum.30 = f32[]{:T(128)} all-reduce(f32[]{:T(128)} %multiply_reduce_fusion.1), channel_id=1, replica_groups=mesh['gx'=16,'gy'=8] {'gx','gy'}, use_global_device_ids=true, to_apply=%region_7.9 | all-reduce | flops 1 | bytes 8 | tf_op jit(solution)/shard_map/psum | solution.py:140
  560.6 1.8 multiply_multiply_fusion.2
  566.4 40.1 %all-gather.24.cloned.1.call-done = f32[32,2,40,128]{3,2,1,0:T(8,128)} async-done(((f32[2,2,40,128]{3,2,1,0:T(8,128)}), f32[32,2,40,128]{3,2,1,0:T(8,128)}) %all-gather.24.cloned.1.call-update) | async-done | bytes 1310736 | tf_op jit(solution)/shard_map/all_gather | solution.py:128
  606.6 1.9 constant_dynamic-update-slice_fusion.175
  619.5 1.7 copy.1695
  621.9 13.0 %all-gather.9 = f32[16,2,40,8]{2,3,1,0:T(8,128)S(1)} all-gather(f32[2,2,40,8]{2,3,1,0:T(8,128)S(1)} %pad_maximum_fusion.9), channel_id=11, replica_groups=mesh['gx'=16,'gy'=8] {'gy'}, dimensions={0}, use_global_device_ids=true | all-gather | bytes 46080 | tf_op jit(solution)/shard_map/all_gather | solution.py:128
  639.3 1.3 constant_dynamic-update-slice_fusion.185
  642.3 23.2 %gather_fusion.1 = f32[4096]{0:T(1024)S(1)} fusion(f32[81920]{0:T(1024)S(1)} %bitcast.2257, s32[4096]{0:T(1024)} %fusion.140), kind=kCustom, calls=%fused_computation.1.clone | custom fusion | bytes 49152 | tf_op jit(solution)/shard_map/jit(_take)/gather | solution.py:184
  665.6 16.8 %all_to_all.43 = f32[128,1,32]{2,1,0:T(1,128)S(1)} all-to-all(f32[128,1,32]{2,1,0:T(1,128)S(1)} %bitcast.2381), channel_id=1, replica_groups=mesh['gx'=16,'gy'=8] {'gx','gy'}, dimensions={0} | all-to-all | bytes 32768 | tf_op jit(solution)/shard_map/all_to_all | solution.py:192
  683.3 5.7 fusion
  689.8 4.8 all-to-all-start.4
  695.3 8.7 all-to-all-done.4
  704.9 22.1 %scatter_custom_fusion.2 = f32[81920]{0:T(1024)S(1)} fusion(s32[4096]{0:T(1024)} %bitcast.2405, f32[4096]{0:T(1024)S(1)} %reshape.27303, f32[]{:T(128)} %constant.105.clone.1), kind=kCustom, calls=%fused_computation.486 | custom fusion | flops 4096 | bytes 328192 | tf_op jit(solution)/shard_map/scatter-add | solution.py:174
  736.3 13.0 %all-gather.10 = f32[16,2,40,8]{2,3,1,0:T(8,128)S(1)} all-gather(f32[2,2,40,8]{2,3,1,0:T(8,128)S(1)} %pad_maximum_fusion.10), channel_id=12, replica_groups=mesh['gx'=16,'gy'=8] {'gy'}, dimensions={0}, use_global_device_ids=true | all-gather | bytes 46080 | tf_op jit(solution)/shard_map/all_gather | solution.py:128
  760.2 39.7 %all-gather.26.cloned.1.call-done = f32[32,2,40,128]{3,2,1,0:T(8,128)} async-done(((f32[2,2,40,128]{3,2,1,0:T(8,128)}), f32[32,2,40,128]{3,2,1,0:T(8,128)}) %all-gather.26.cloned.1.call-update) | async-done | bytes 1310736 | tf_op jit(solution)/shard_map/all_gather | solution.py:128
  800.2 1.8 constant_dynamic-update-slice_fusion.239
  804.8 64.6 %psum.31 = f32[]{:T(128)} all-reduce(f32[]{:T(128)} %get-tuple-element.9), channel_id=1, replica_groups=mesh['gx'=16,'gy'=8] {'gx','gy'}, use_global_device_ids=true, to_apply=%region_10.12 | all-reduce | flops 1 | bytes 8 | tf_op jit(solution)/shard_map/psum | solution.py:140
  (1080 shorter events, 121.6 us)
Async XLA Ops:
  17.4 43.4 %all-to-all-start = ((f32[128,1,32]{2,1,0:T(1,128)}), f32[128,1,32]{2,1,0:T(1,128)}, u32[]{:S(2)}, u32[]{:S(2)}) async-start(f32[128,1,32]{2,1,0:T(1,128)} %bitcast.5), calls=%async_computation | async-start | bytes 131072 | tf_op jit(solution)/shard_map/all_to_all | solution.py:170
  29.1 129.8 %all-gather.18.cloned.1.call-start = ((), (), s32[]{:S(2)}) async-start(), calls=%async_computation.5 | async-start | bytes 1392640 | tf_op jit(solution)/shard_map/all_gather | solution.py:128
  46.6 63.0 %copy-start.174 = (f32[40,8]{0,1:T(8,128)}, f32[40,8]{0,1:T(8,128)S(1)}, u32[]{:S(2)}) copy-start(f32[40,8]{0,1:T(8,128)S(1)} %get-tuple-element.334) | copy-start | bytes 3844
  46.6 63.0 %copy-start.176 = (f32[40,8]{0,1:T(8,128)}, f32[40,8]{0,1:T(8,128)S(1)}, u32[]{:S(2)}) copy-start(f32[40,8]{0,1:T(8,128)S(1)} %get-tuple-element.347) | copy-start | bytes 3844
  59.3 52.5 %copy-start.3 = (f32[40,8,128]{2,0,1:T(8,128)}, f32[40,8,128]{2,0,1:T(8,128)S(1)}, u32[]{:S(2)}) copy-start(f32[40,8,128]{2,0,1:T(8,128)S(1)} %copy.1595) | copy-start | bytes 491524
  114.5 94.4 %all-gather.20.cloned.1.call-start = ((), (), s32[]{:S(2)}) async-start(), calls=%async_computation.6 | async-start | bytes 1392640 | tf_op jit(solution)/shard_map/all_gather | solution.py:128
  115.4 97.1 %copy-start.43 = (f32[40,8,128]{2,0,1:T(8,128)}, f32[40,8,128]{2,0,1:T(8,128)S(1)}, u32[]{:S(2)}) copy-start(f32[40,8,128]{2,0,1:T(8,128)S(1)} %copy.1780) | copy-start | bytes 491524
  116.4 45.7 %copy-start.91 = (f32[40,8,128]{2,0,1:T(8,128)}, f32[40,8,128]{2,0,1:T(8,128)S(1)}, u32[]{:S(2)}) copy-start(f32[40,8,128]{2,0,1:T(8,128)S(1)} %copy.1774) | copy-start | bytes 491524
  119.1 47.0 %copy-start = (f32[40,8,128]{2,1,0:T(8,128)}, f32[40,8,128]{2,1,0:T(8,128)S(1)}, u32[]{:S(2)}) copy-start(f32[40,8,128]{2,1,0:T(8,128)S(1)} %pad_bitcast_fusion) | copy-start | bytes 491524
  167.9 41.1 %copy-start.195 = (s32[4096]{0:T(1024)}, s32[4096]{0:T(1024)S(1)}, u32[]{:S(2)}) copy-start(s32[4096]{0:T(1024)S(1)} %reshape_squeeze.10) | copy-start | bytes 49156
  310.1 14.1 %all-to-all-start.2 = ((f32[128,1,32]{2,1,0:T(1,128)}), f32[128,1,32]{2,1,0:T(1,128)S(1)}, u32[]{:S(2)}, u32[]{:S(2)}) async-start(f32[128,1,32]{2,1,0:T(1,128)} %bitcast.276), calls=%async_computation.2 | async-start | bytes 131072 | tf_op jit(solution)/shard_map/all_to_all | solution.py:170
  314.9 108.9 %all-gather.22.cloned.1.call-start = ((), (), s32[]{:S(2)}) async-start(), calls=%async_computation.7 | async-start | bytes 1392640 | tf_op jit(solution)/shard_map/all_gather | solution.py:128
  382.3 41.5 %copy-start.68 = (f32[40,128]{1,0:T(8,128)S(1)}, f32[40,128]{1,0:T(8,128)}, u32[]{:S(2)}) copy-start(f32[40,128]{1,0:T(8,128)} %copy-done.66) | copy-start | bytes 61444
  382.3 41.4 %copy-start.74 = (f32[40,128]{1,0:T(8,128)S(1)}, f32[40,128]{1,0:T(8,128)}, u32[]{:S(2)}) copy-start(f32[40,128]{1,0:T(8,128)} %copy-done.72) | copy-start | bytes 61444
  382.4 41.4 %copy-start.80 = (f32[40,128]{1,0:T(8,128)S(1)}, f32[40,128]{1,0:T(8,128)}, u32[]{:S(2)}) copy-start(f32[40,128]{1,0:T(8,128)} %copy-done.78) | copy-start | bytes 61444
  382.4 41.4 %copy-start.104 = (f32[40,128]{1,0:T(8,128)S(1)}, f32[40,128]{1,0:T(8,128)}, u32[]{:S(2)}) copy-start(f32[40,128]{1,0:T(8,128)} %copy-done.103) | copy-start | bytes 61444
  382.4 41.4 %copy-start.108 = (f32[40,128]{1,0:T(8,128)S(1)}, f32[40,128]{1,0:T(8,128)}, u32[]{:S(2)}) copy-start(f32[40,128]{1,0:T(8,128)} %copy-done.107) | copy-start | bytes 61444
  382.4 41.4 %copy-start.112 = (f32[40,128]{1,0:T(8,128)S(1)}, f32[40,128]{1,0:T(8,128)}, u32[]{:S(2)}) copy-start(f32[40,128]{1,0:T(8,128)} %copy-done.111) | copy-start | bytes 61444
  382.4 41.4 %copy-start.116 = (f32[40,128]{1,0:T(8,128)S(1)}, f32[40,128]{1,0:T(8,128)}, u32[]{:S(2)}) copy-start(f32[40,128]{1,0:T(8,128)} %copy-done.115) | copy-start | bytes 61444
  382.4 41.4 %copy-start.120 = (f32[40,128]{1,0:T(8,128)S(1)}, f32[40,128]{1,0:T(8,128)}, u32[]{:S(2)}) copy-start(f32[40,128]{1,0:T(8,128)} %copy-done.119) | copy-start | bytes 61444
  382.4 41.4 %copy-start.123 = (f32[40,128]{1,0:T(8,128)S(1)}, f32[40,128]{1,0:T(8,128)}, u32[]{:S(2)}) copy-start(f32[40,128]{1,0:T(8,128)} %get-tuple-element.296) | copy-start | bytes 61444
  382.4 41.4 %copy-start.126 = (f32[40,128]{1,0:T(8,128)S(1)}, f32[40,128]{1,0:T(8,128)}, u32[]{:S(2)}) copy-start(f32[40,128]{1,0:T(8,128)} %get-tuple-element.297) | copy-start | bytes 61444
  382.4 41.4 %copy-start.129 = (f32[40,128]{1,0:T(8,128)S(1)}, f32[40,128]{1,0:T(8,128)}, u32[]{:S(2)}) copy-start(f32[40,128]{1,0:T(8,128)} %get-tuple-element.298) | copy-start | bytes 61444
  382.4 41.4 %copy-start.132 = (f32[40,128]{1,0:T(8,128)S(1)}, f32[40,128]{1,0:T(8,128)}, u32[]{:S(2)}) copy-start(f32[40,128]{1,0:T(8,128)} %get-tuple-element.299) | copy-start | bytes 61444
  382.5 41.4 %copy-start.135 = (f32[40,128]{1,0:T(8,128)S(1)}, f32[40,128]{1,0:T(8,128)}, u32[]{:S(2)}) copy-start(f32[40,128]{1,0:T(8,128)} %get-tuple-element.300) | copy-start | bytes 61444
  382.5 41.4 %copy-start.138 = (f32[40,128]{1,0:T(8,128)S(1)}, f32[40,128]{1,0:T(8,128)}, u32[]{:S(2)}) copy-start(f32[40,128]{1,0:T(8,128)} %get-tuple-element.301) | copy-start | bytes 61444
  382.5 41.4 %copy-start.141 = (f32[40,128]{1,0:T(8,128)S(1)}, f32[40,128]{1,0:T(8,128)}, u32[]{:S(2)}) copy-start(f32[40,128]{1,0:T(8,128)} %get-tuple-element.302) | copy-start | bytes 61444
  382.5 41.4 %copy-start.144 = (f32[40,128]{1,0:T(8,128)S(1)}, f32[40,128]{1,0:T(8,128)}, u32[]{:S(2)}) copy-start(f32[40,128]{1,0:T(8,128)} %get-tuple-element.303) | copy-start | bytes 61444
  384.1 222.4 %all-gather.24.cloned.1.call-start = ((), (), s32[]{:S(2)}) async-start(), calls=%async_computation.8 | async-start | bytes 1392640 | tf_op jit(solution)/shard_map/all_gather | solution.py:128
  564.0 42.5 %copy-start.70 = (f32[40,128]{1,0:T(8,128)S(1)}, f32[40,128]{1,0:T(8,128)}, u32[]{:S(2)}) copy-start(f32[40,128]{1,0:T(8,128)} %copy-done.66) | copy-start | bytes 61444
  564.0 42.5 %copy-start.76 = (f32[40,128]{1,0:T(8,128)S(1)}, f32[40,128]{1,0:T(8,128)}, u32[]{:S(2)}) copy-start(f32[40,128]{1,0:T(8,128)} %copy-done.72) | copy-start | bytes 61444
  564.0 42.5 %copy-start.81 = (f32[40,128]{1,0:T(8,128)S(1)}, f32[40,128]{1,0:T(8,128)}, u32[]{:S(2)}) copy-start(f32[40,128]{1,0:T(8,128)} %copy-done.78) | copy-start | bytes 61444
  564.0 42.5 %copy-start.105 = (f32[40,128]{1,0:T(8,128)S(1)}, f32[40,128]{1,0:T(8,128)}, u32[]{:S(2)}) copy-start(f32[40,128]{1,0:T(8,128)} %copy-done.103) | copy-start | bytes 61444
  564.0 42.5 %copy-start.109 = (f32[40,128]{1,0:T(8,128)S(1)}, f32[40,128]{1,0:T(8,128)}, u32[]{:S(2)}) copy-start(f32[40,128]{1,0:T(8,128)} %copy-done.107) | copy-start | bytes 61444
  564.0 42.5 %copy-start.113 = (f32[40,128]{1,0:T(8,128)S(1)}, f32[40,128]{1,0:T(8,128)}, u32[]{:S(2)}) copy-start(f32[40,128]{1,0:T(8,128)} %copy-done.111) | copy-start | bytes 61444
  564.1 42.5 %copy-start.117 = (f32[40,128]{1,0:T(8,128)S(1)}, f32[40,128]{1,0:T(8,128)}, u32[]{:S(2)}) copy-start(f32[40,128]{1,0:T(8,128)} %copy-done.115) | copy-start | bytes 61444
  564.1 42.5 %copy-start.121 = (f32[40,128]{1,0:T(8,128)S(1)}, f32[40,128]{1,0:T(8,128)}, u32[]{:S(2)}) copy-start(f32[40,128]{1,0:T(8,128)} %copy-done.119) | copy-start | bytes 61444
  564.1 42.5 %copy-start.124 = (f32[40,128]{1,0:T(8,128)S(1)}, f32[40,128]{1,0:T(8,128)}, u32[]{:S(2)}) copy-start(f32[40,128]{1,0:T(8,128)} %get-tuple-element.296) | copy-start | bytes 61444
  564.1 42.5 %copy-start.127 = (f32[40,128]{1,0:T(8,128)S(1)}, f32[40,128]{1,0:T(8,128)}, u32[]{:S(2)}) copy-start(f32[40,128]{1,0:T(8,128)} %get-tuple-element.297) | copy-start | bytes 61444
  564.1 42.5 %copy-start.130 = (f32[40,128]{1,0:T(8,128)S(1)}, f32[40,128]{1,0:T(8,128)}, u32[]{:S(2)}) copy-start(f32[40,128]{1,0:T(8,128)} %get-tuple-element.298) | copy-start | bytes 61444
  564.1 42.5 %copy-start.133 = (f32[40,128]{1,0:T(8,128)S(1)}, f32[40,128]{1,0:T(8,128)}, u32[]{:S(2)}) copy-start(f32[40,128]{1,0:T(8,128)} %get-tuple-element.299) | copy-start | bytes 61444
  564.1 42.5 %copy-start.136 = (f32[40,128]{1,0:T(8,128)S(1)}, f32[40,128]{1,0:T(8,128)}, u32[]{:S(2)}) copy-start(f32[40,128]{1,0:T(8,128)} %get-tuple-element.300) | copy-start | bytes 61444
  564.1 42.5 %copy-start.139 = (f32[40,128]{1,0:T(8,128)S(1)}, f32[40,128]{1,0:T(8,128)}, u32[]{:S(2)}) copy-start(f32[40,128]{1,0:T(8,128)} %get-tuple-element.301) | copy-start | bytes 61444
  564.1 42.5 %copy-start.142 = (f32[40,128]{1,0:T(8,128)S(1)}, f32[40,128]{1,0:T(8,128)}, u32[]{:S(2)}) copy-start(f32[40,128]{1,0:T(8,128)} %get-tuple-element.302) | copy-start | bytes 61444
  564.1 42.5 %copy-start.145 = (f32[40,128]{1,0:T(8,128)S(1)}, f32[40,128]{1,0:T(8,128)}, u32[]{:S(2)}) copy-start(f32[40,128]{1,0:T(8,128)} %get-tuple-element.303) | copy-start | bytes 61444
  642.3 41.0 %copy-start.196 = (pred[16,256]{1,0:T(8,128)(4,1)S(1)}, pred[16,256]{1,0:T(8,128)(4,1)}, u32[]{:S(2)}) copy-start(pred[16,256]{1,0:T(8,128)(4,1)} %get-tuple-element.259) | copy-start | bytes 12292
  689.8 14.1 %all-to-all-start.4 = ((f32[128,1,32]{2,1,0:T(1,128)}), f32[128,1,32]{2,1,0:T(1,128)S(1)}, u32[]{:S(2)}, u32[]{:S(2)}) async-start(f32[128,1,32]{2,1,0:T(1,128)} %bitcast.394), calls=%async_computation.4 | async-start | bytes 131072 | tf_op jit(solution)/shard_map/all_to_all | solution.py:170
  694.6 105.2 %all-gather.26.cloned.1.call-start = ((), (), s32[]{:S(2)}) async-start(), calls=%async_computation.9 | async-start | bytes 1392640 | tf_op jit(solution)/shard_map/all_gather | solution.py:128
  758.9 40.9 %copy-start.110 = (f32[40,128]{1,0:T(8,128)S(1)}, f32[40,128]{1,0:T(8,128)}, u32[]{:S(2)}) copy-start(f32[40,128]{1,0:T(8,128)} %copy-done.107) | copy-start | bytes 61444
  759.0 40.9 %copy-start.114 = (f32[40,128]{1,0:T(8,128)S(1)}, f32[40,128]{1,0:T(8,128)}, u32[]{:S(2)}) copy-start(f32[40,128]{1,0:T(8,128)} %copy-done.111) | copy-start | bytes 61444
  759.0 40.9 %copy-start.118 = (f32[40,128]{1,0:T(8,128)S(1)}, f32[40,128]{1,0:T(8,128)}, u32[]{:S(2)}) copy-start(f32[40,128]{1,0:T(8,128)} %copy-done.115) | copy-start | bytes 61444
  759.0 40.9 %copy-start.122 = (f32[40,128]{1,0:T(8,128)S(1)}, f32[40,128]{1,0:T(8,128)}, u32[]{:S(2)}) copy-start(f32[40,128]{1,0:T(8,128)} %copy-done.119) | copy-start | bytes 61444
  759.0 40.9 %copy-start.125 = (f32[40,128]{1,0:T(8,128)S(1)}, f32[40,128]{1,0:T(8,128)}, u32[]{:S(2)}) copy-start(f32[40,128]{1,0:T(8,128)} %get-tuple-element.296) | copy-start | bytes 61444
  759.0 40.9 %copy-start.128 = (f32[40,128]{1,0:T(8,128)S(1)}, f32[40,128]{1,0:T(8,128)}, u32[]{:S(2)}) copy-start(f32[40,128]{1,0:T(8,128)} %get-tuple-element.297) | copy-start | bytes 61444
  759.0 40.9 %copy-start.131 = (f32[40,128]{1,0:T(8,128)S(1)}, f32[40,128]{1,0:T(8,128)}, u32[]{:S(2)}) copy-start(f32[40,128]{1,0:T(8,128)} %get-tuple-element.298) | copy-start | bytes 61444
  759.0 40.9 %copy-start.134 = (f32[40,128]{1,0:T(8,128)S(1)}, f32[40,128]{1,0:T(8,128)}, u32[]{:S(2)}) copy-start(f32[40,128]{1,0:T(8,128)} %get-tuple-element.299) | copy-start | bytes 61444
  759.0 40.9 %copy-start.137 = (f32[40,128]{1,0:T(8,128)S(1)}, f32[40,128]{1,0:T(8,128)}, u32[]{:S(2)}) copy-start(f32[40,128]{1,0:T(8,128)} %get-tuple-element.300) | copy-start | bytes 61444
  759.0 40.9 %copy-start.140 = (f32[40,128]{1,0:T(8,128)S(1)}, f32[40,128]{1,0:T(8,128)}, u32[]{:S(2)}) copy-start(f32[40,128]{1,0:T(8,128)} %get-tuple-element.301) | copy-start | bytes 61444
  759.0 40.9 %copy-start.143 = (f32[40,128]{1,0:T(8,128)S(1)}, f32[40,128]{1,0:T(8,128)}, u32[]{:S(2)}) copy-start(f32[40,128]{1,0:T(8,128)} %get-tuple-element.302) | copy-start | bytes 61444
  759.1 40.9 %copy-start.146 = (f32[40,128]{1,0:T(8,128)S(1)}, f32[40,128]{1,0:T(8,128)}, u32[]{:S(2)}) copy-start(f32[40,128]{1,0:T(8,128)} %get-tuple-element.303) | copy-start | bytes 61444
  759.1 40.9 %copy-start.147 = (f32[40,128]{1,0:T(8,128)S(1)}, f32[40,128]{1,0:T(8,128)}, u32[]{:S(2)}) copy-start(f32[40,128]{1,0:T(8,128)} %get-tuple-element.304) | copy-start | bytes 61444
  759.1 40.9 %copy-start.148 = (f32[40,128]{1,0:T(8,128)S(1)}, f32[40,128]{1,0:T(8,128)}, u32[]{:S(2)}) copy-start(f32[40,128]{1,0:T(8,128)} %get-tuple-element.305) | copy-start | bytes 61444
  759.1 40.9 %copy-start.149 = (f32[40,128]{1,0:T(8,128)S(1)}, f32[40,128]{1,0:T(8,128)}, u32[]{:S(2)}) copy-start(f32[40,128]{1,0:T(8,128)} %get-tuple-element.306) | copy-start | bytes 61444
  803.3 67.5 %copy-start.40 = (f32[2,40,8,128]{3,2,1,0:T(8,128)S(1)}, f32[2,40,8,128]{3,2,1,0:T(8,128)}, u32[]{:S(2)}) copy-start(f32[2,40,8,128]{3,2,1,0:T(8,128)} %get-tuple-element.101) | copy-start | bytes 983044
  (148 other events, 1843.0 us)
Sparse Core Ops, SparseCore 0:
  114.6 44.2 all-gather.17
  166.3 42.6 all-gather.19
  384.2 39.4 all-gather.21
  565.9 40.5 all-gather.23
  760.3 39.4 all-gather.25

commit v2 on v1

--- a/solution.py
+++ b/solution.py
@@ -136,8 +136,13 @@
     return plan["gain_out"] * (forward + next_offset + next_factor * leaving)
 
 
-def global_dot(first_field, second_field):
-    return lax.psum(jnp.sum(first_field * second_field), ("gx", "gy"))
+def exchange(values, partial):
+    rows = values.shape[0]
+    packed = jnp.concatenate(
+        [values, jnp.broadcast_to(partial.astype(values.dtype), (rows, 1))], axis=1
+    )
+    arrived = lax.all_to_all(packed, ("gx", "gy"), split_axis=0, concat_axis=0, tiled=True)
+    return arrived[:, :-1], jnp.sum(arrived[:, -1])
 
 
 def on_device(rate_x, rate_y, land_mask, obs_cell, obs_count, innovation, obs_weight):
@@ -152,6 +157,9 @@
     def along_y(state_field):
         return line_operator(state_field, plan_along_y)
 
+    def spread(vector):
+        return ocean * along_y(along_x(ocean * vector))
+
     def gather_back(vector):
         return ocean * along_x(along_y(ocean * vector))
 
@@ -166,8 +174,7 @@
         mixed = jnp.einsum("nij,nj->ni", blocks, packed, precision=lax.Precision.HIGHEST)
         return occupied * mixed.reshape(occupied.shape)
 
-    def deposit(values):
-        arrived = lax.all_to_all(values, ("gx", "gy"), split_axis=0, concat_axis=0, tiled=True)
+    def deposit_local(arrived):
         flat_cells = (
             jnp.zeros((TR * rate_x.size,), jnp.float32)
             .at[cell_index.reshape(-1)]
@@ -175,30 +182,37 @@
         )
         return flat_cells.reshape(field_shape)
 
-    right_side = gather_back(deposit(weigh_obs(innovation[0])))
+    def observe(vector):
+        return jnp.take(vector.reshape(-1), cell_index.reshape(-1), axis=0).reshape(
+            cell_index.shape
+        )
+
+    weighted = weigh_obs(innovation[0])
+    arrived = lax.all_to_all(weighted, ("gx", "gy"), split_axis=0, concat_axis=0, tiled=True)
+    right_side = gather_back(deposit_local(arrived))
     solution = jnp.zeros_like(right_side)
     residual = right_side
     direction = right_side
-    norm_now = global_dot(residual, residual)
+    norm_now = None
+    previous_seen = None
     for iteration in range(ITERS):
-        picked = jnp.take(
-            (ocean * along_y(along_x(ocean * direction))).reshape(-1),
-            cell_index.reshape(-1),
-            axis=0,
-        ).reshape(cell_index.shape)
-        hessian_dir = direction + gather_back(
-            deposit(
-                weigh_obs(
-                    lax.all_to_all(picked, ("gx", "gy"), split_axis=0, concat_axis=0, tiled=True)
-                )
-            )
-        )
-        step_length = norm_now / global_dot(direction, hessian_dir)
+        seen, norm_next = exchange(observe(spread(residual)), jnp.sum(residual * residual))
+        if iteration == 0:
+            direction = residual
+        else:
+            ratio = norm_next / norm_now
+            seen = seen + ratio * previous_seen
+            direction = residual + ratio * direction
+        norm_now = norm_next
+        mixed = weigh_obs(seen)
+        returned, curvature = exchange(
+            mixed, jnp.sum(direction * direction) + jnp.sum(seen * mixed)
+        )
+        hessian_dir = direction + gather_back(deposit_local(returned))
+        step_length = norm_now / curvature
         solution = solution + step_length * direction
         residual = residual - step_length * hessian_dir
-        norm_next = global_dot(residual, residual)
-        direction = residual + norm_next / norm_now * direction
-        norm_now = norm_next
+        previous_seen = seen
     return (solution, residual)
 
 

time: 890 us -> 706 us (0.79)
  blocking collectives: 328 us -> 136 us
    psum x3 -> x0, blocking collectives: 191 us -> none  [global_dot(): return lax.psum(jnp.sum(first_field * second_field), ('gx', 'gy'))]
    gather x2, local copies, waits for them, and re-layouts: 63.8 us -> 81.4 us  [observe(): jnp.take(vector.reshape(-1), cell_index.reshape(-1), axis=0)]
    unnamed x616 -> x564, local copies, waits for them, and re-layouts: 46.4 us -> 33.6 us
  transfers between devices with their start and end apart: 8 -> 8, of which waited for: 7 -> 7; matrix products, arithmetic and copies ran while one was open for 3% -> 4% of each run, Pallas kernels for 0% -> 0%
where the time goes in v2:
time: 706 us; the launch traced here: 696 us
  waiting for transfers between devices  183 us (26%)
  local copies, waits for them, and re-layouts  163 us (23%)
  other arithmetic  148 us (21%)
  blocking collectives  136 us (19%)
  between operations  26.1 us (4%)
  starting transfers between devices  22 us (3%)
  matrix products  17 us (2%)
    all_gather x5, waiting for transfers between devices, line_operator(): got = lax.all_gather(mine, plan['axis_name'])  165 us
    gather x2, local copies, waits for them, and re-layouts, observe(): jnp.take(vector.reshape(-1), cell_index.reshape(-1), axis=0)  81.4 us
    scatter-add x3, other arithmetic, deposit_local(): flat_cells = jnp.zeros((TR * rate_x.size,), jnp.float32).at[cell_index.re...  67 us
    all_gather x5, blocking collectives, line_operator(): got = lax.all_gather(mine, plan['axis_name'])  64.8 us
    all_gather x2, blocking collectives, make_plan(): lax.all_gather(totals, axis_name)  38.4 us
    unnamed x564, local copies, waits for them, and re-layouts  33.6 us
    all_to_all x2, blocking collectives, exchange(): lax.all_to_all(packed, ('gx', 'gy'), split_axis=0, concat_axis=0, tiled=T...  33.2 us
    unnamed x56, other arithmetic  19.2 us
  transfers between devices with their start and end apart: 8, of which 7 were waited for; matrix products, arithmetic and copies ran while one was open for 4% of the time, Pallas kernels for 0%

profile of v2, /device:TPU:0, one launch (start us, length us, event | category | flops | bytes accessed | tf_op | source)
XLA Modules:
  0.0 695.6 jit_solution(16636097269624037994)
XLA Ops:
  7.8 1.3 reduce.10
  10.3 5.7 fusion.4
  16.8 11.7 %all-to-all-start = ((f32[128,1,32]{2,1,0:T(1,128)}), f32[128,1,32]{2,1,0:T(1,128)}, u32[]{:S(2)}, u32[]{:S(2)}) async-start(f32[128,1,32]{2,1,0:T(1,128)} %bitcast.5), calls=%async_computation | async-start | bytes 131072 | tf_op jit(solution)/shard_map/all_to_all | solution.py:191
  32.6 12.7 %all-gather.1 = f32[24,1,40,8]{2,3,1,0:T(8,128)S(1)} all-gather(f32[3,1,40,8]{2,3,1,0:T(8,128)S(1)} %pad_maximum_fusion.11), channel_id=3, replica_groups=mesh['gx'=16,'gy'=8] {'gy'}, dimensions={0}, use_global_device_ids=true | all-gather | bytes 34560 | tf_op jit(solution)/shard_map/all_gather | solution.py:69
  52.9 1.8 slice.2242
  55.1 1.7 reduce.11
  56.9 22.7 %scatter_custom_fusion = f32[81920]{0:T(1024)} fusion(s32[4096]{0:T(1024)} %bitcast.2475, f32[4096]{0:T(1024)S(1)} %reshape.27207, f32[]{:T(128)} %constant.105.clone.1), kind=kCustom, calls=%fused_computation.441 | custom fusion | flops 4096 | bytes 328192 | tf_op jit(solution)/shard_map/scatter-add | solution.py:181
  79.6 1.0 multiply_multiply_fusion.10
  80.6 1.1 multiply_add_fusion.92
  85.4 1.1 copy.904
  86.6 1.1 multiply_add_fusion.84
  89.7 1.7 copy.905
  92.1 13.2 %all-gather = f32[16,2,40,8]{2,3,1,0:T(8,128)S(1)} all-gather(f32[2,2,40,8]{2,3,1,0:T(8,128)S(1)} %pad_maximum_fusion.6), channel_id=2, replica_groups=mesh['gx'=16,'gy'=8] {'gy'}, dimensions={0}, use_global_device_ids=true | all-gather | bytes 46080 | tf_op jit(solution)/shard_map/all_gather | solution.py:128
  110.6 1.3 slice_add_fusion.9
  111.8 1.3 multiply_multiply_fusion.9
  119.5 1.6 pad_bitcast_fusion
  121.1 25.7 %all-gather.2 = f32[48,1,40,128]{3,2,1,0:T(8,128)S(1)} all-gather(f32[3,1,40,128]{3,2,1,0:T(8,128)S(1)} %pad_maximum_fusion.5), channel_id=4, replica_groups=mesh['gx'=16,'gy'=8] {'gx'}, dimensions={0}, use_global_device_ids=true | all-gather | bytes 1044480 | tf_op jit(solution)/shard_map/all_gather | solution.py:69
  150.3 10.0 %all-gather.18.cloned.1.call-done = f32[32,2,40,128]{3,2,1,0:T(8,128)} async-done(((f32[2,2,40,128]{3,2,1,0:T(8,128)}), f32[32,2,40,128]{3,2,1,0:T(8,128)}) %all-gather.18.cloned.1.call-update) | async-done | bytes 1310736 | tf_op jit(solution)/shard_map/all_gather | solution.py:128
  160.3 1.8 constant_dynamic-update-slice_fusion.47
  170.1 40.6 %all-gather.20.cloned.1.call-done = f32[32,2,40,128]{3,2,1,0:T(8,128)} async-done(((f32[2,2,40,128]{3,2,1,0:T(8,128)}), f32[32,2,40,128]{3,2,1,0:T(8,128)}) %all-gather.20.cloned.1.call-update) | async-done | bytes 1310736 | tf_op jit(solution)/shard_map/all_gather | solution.py:128
  210.7 1.9 constant_dynamic-update-slice_fusion.79
  218.9 1.1 copy.959
  220.1 1.1 copy.958
  221.2 13.0 %all-gather.5 = f32[16,2,40,8]{2,3,1,0:T(8,128)S(1)} all-gather(f32[2,2,40,8]{2,3,1,0:T(8,128)S(1)} %pad_maximum_fusion.7), channel_id=7, replica_groups=mesh['gx'=16,'gy'=8] {'gy'}, dimensions={0}, use_global_device_ids=true | all-gather | bytes 46080 | tf_op jit(solution)/shard_map/all_gather | solution.py:128
  240.1 1.9 slice_add_fusion.6
  242.8 1.4 multiply_multiply_fusion.7
  244.2 40.7 %gather_fusion = f32[4096]{0:T(1024)} fusion(f32[81920]{0:T(1024)S(1)} %bitcast.2240, s32[4096]{0:T(1024)} %fusion.126), kind=kCustom, calls=%fused_computation.clone | custom fusion | bytes 49152 | tf_op jit(solution)/shard_map/jit(_take)/gather | solution.py:186
  284.9 1.3 broadcast_select_fusion.1
  287.0 16.7 %all_to_all.54 = f32[128,1,33]{2,1,0:T(1,128)S(1)} all-to-all(f32[128,1,33]{2,1,0:T(1,128)S(1)} %bitcast.2444), channel_id=1, replica_groups=mesh['gx'=16,'gy'=8] {'gx','gy'}, dimensions={0} | all-to-all | bytes 33792 | tf_op jit(solution)/shard_map/all_to_all | solution.py:144
  304.5 5.7 fusion.2
  312.9 4.8 all-to-all-start.2
  318.4 8.6 %all-to-all-done.2 = f32[128,1,33]{2,1,0:T(1,128)S(1)} async-done(((f32[128,1,33]{2,1,0:T(1,128)}), f32[128,1,33]{2,1,0:T(1,128)S(1)}, u32[]{:S(2)}, u32[]{:S(2)}) %all-to-all-start.2) | async-done | bytes 16928 | tf_op jit(solution)/shard_map/all_to_all | solution.py:144
  328.3 22.1 %scatter_custom_fusion.1 = f32[81920]{0:T(1024)S(1)} fusion(s32[4096]{0:T(1024)} %bitcast.2476, f32[4096]{0:T(1024)} %reshape.27215, f32[]{:T(128)} %constant.105.clone.1), kind=kCustom, calls=%fused_computation.439 | custom fusion | flops 4096 | bytes 328192 | tf_op jit(solution)/shard_map/scatter-add | solution.py:181
  354.8 1.8 copy.965
  356.5 1.7 copy.964
  359.0 12.7 %all-gather.6 = f32[16,2,40,8]{2,3,1,0:T(8,128)S(1)} all-gather(f32[2,2,40,8]{2,3,1,0:T(8,128)S(1)} %pad_maximum_fusion.8), channel_id=8, replica_groups=mesh['gx'=16,'gy'=8] {'gy'}, dimensions={0}, use_global_device_ids=true | all-gather | bytes 46080 | tf_op jit(solution)/shard_map/all_gather | solution.py:128
  376.1 1.3 constant_dynamic-update-slice_fusion.105
  378.0 1.3 constant_dynamic-slice_fusion.5
  379.3 1.4 copy.966
  380.7 2.0 slice_add_fusion.5
  382.7 1.4 copy.967
  384.1 1.3 multiply_multiply_fusion.5
  390.3 1.6 slice_reduce_fusion.2
  393.2 35.7 %all-gather.22.cloned.1.call-done = f32[32,2,40,128]{3,2,1,0:T(8,128)} async-done(((f32[2,2,40,128]{3,2,1,0:T(8,128)}), f32[32,2,40,128]{3,2,1,0:T(8,128)}) %all-gather.22.cloned.1.call-update) | async-done | bytes 1310736 | tf_op jit(solution)/shard_map/all_gather | solution.py:128
  428.9 2.0 constant_dynamic-update-slice_fusion.143
  438.5 42.2 %all-gather.24.cloned.1.call-done = f32[32,2,40,128]{3,2,1,0:T(8,128)} async-done(((f32[2,2,40,128]{3,2,1,0:T(8,128)}), f32[32,2,40,128]{3,2,1,0:T(8,128)}) %all-gather.24.cloned.1.call-update) | async-done | bytes 1310736 | tf_op jit(solution)/shard_map/all_gather | solution.py:128
  480.6 1.9 constant_dynamic-update-slice_fusion.175
  488.7 1.1 copy.979
  489.9 1.1 copy.978
  491.0 13.0 %all-gather.9 = f32[16,2,40,8]{2,3,1,0:T(8,128)S(1)} all-gather(f32[2,2,40,8]{2,3,1,0:T(8,128)S(1)} %pad_maximum_fusion.9), channel_id=11, replica_groups=mesh['gx'=16,'gy'=8] {'gy'}, dimensions={0}, use_global_device_ids=true | all-gather | bytes 46080 | tf_op jit(solution)/shard_map/all_gather | solution.py:128
  510.0 1.9 slice_add_fusion.2
  512.6 1.4 multiply_multiply_fusion.2
  514.0 40.7 %gather_fusion.1 = f32[4096]{0:T(1024)} fusion(f32[81920]{0:T(1024)S(1)} %bitcast.2239, s32[4096]{0:T(1024)} %fusion.126), kind=kCustom, calls=%fused_computation.1.clone | custom fusion | bytes 49152 | tf_op jit(solution)/shard_map/jit(_take)/gather | solution.py:186
  556.2 16.4 %all_to_all.55 = f32[128,1,33]{2,1,0:T(1,128)S(1)} all-to-all(f32[128,1,33]{2,1,0:T(1,128)S(1)} %bitcast.2443), channel_id=1, replica_groups=mesh['gx'=16,'gy'=8] {'gx','gy'}, dimensions={0} | all-to-all | bytes 33792 | tf_op jit(solution)/shard_map/all_to_all | solution.py:144
  574.6 1.7 multiply_reduce_fusion
  577.3 5.7 fusion
  585.7 5.1 all-to-all-start.4
  591.4 8.7 %all-to-all-done.4 = f32[128,1,33]{2,1,0:T(1,128)S(1)} async-done(((f32[128,1,33]{2,1,0:T(1,128)}), f32[128,1,33]{2,1,0:T(1,128)S(1)}, u32[]{:S(2)}, u32[]{:S(2)}) %all-to-all-start.4) | async-done | bytes 16928 | tf_op jit(solution)/shard_map/all_to_all | solution.py:144
  601.5 22.1 %scatter_custom_fusion.2 = f32[81920]{0:T(1024)S(1)} fusion(s32[4096]{0:T(1024)} %bitcast.2477, f32[4096]{0:T(1024)} %reshape.27223, f32[]{:T(128)} %constant.105.clone.1), kind=kCustom, calls=%fused_computation.437 | custom fusion | flops 4096 | bytes 328192 | tf_op jit(solution)/shard_map/scatter-add | solution.py:181
  627.0 12.7 %all-gather.10 = f32[16,2,40,8]{2,3,1,0:T(8,128)S(1)} all-gather(f32[2,2,40,8]{2,3,1,0:T(8,128)S(1)} %pad_maximum_fusion.10), channel_id=12, replica_groups=mesh['gx'=16,'gy'=8] {'gy'}, dimensions={0}, use_global_device_ids=true | all-gather | bytes 46080 | tf_op jit(solution)/shard_map/all_gather | solution.py:128
  644.4 1.6 slice_reduce_fusion
  647.3 36.8 %all-gather.26.cloned.1.call-done = f32[32,2,40,128]{3,2,1,0:T(8,128)} async-done(((f32[2,2,40,128]{3,2,1,0:T(8,128)}), f32[32,2,40,128]{3,2,1,0:T(8,128)}) %all-gather.26.cloned.1.call-update) | async-done | bytes 1310736 | tf_op jit(solution)/shard_map/all_gather | solution.py:128
  684.4 1.8 constant_dynamic-update-slice_fusion.239
  687.6 1.0 multiply_subtract_fusion
  (976 shorter events, 108.2 us)
Async XLA Ops:
  10.3 18.3 %copy-start.40 = (f32[40,8,128]{2,1,0:T(8,128)S(1)}, f32[40,8,128]{2,1,0:T(8,128)}, u32[]{:S(2)}) copy-start(f32[40,8,128]{2,1,0:T(8,128)} %param.10) | copy-start | bytes 491524
  16.8 37.8 %all-to-all-start = ((f32[128,1,32]{2,1,0:T(1,128)}), f32[128,1,32]{2,1,0:T(1,128)}, u32[]{:S(2)}, u32[]{:S(2)}) async-start(f32[128,1,32]{2,1,0:T(1,128)} %bitcast.5), calls=%async_computation | async-start | bytes 131072 | tf_op jit(solution)/shard_map/all_to_all | solution.py:191
  28.5 131.8 %all-gather.18.cloned.1.call-start = ((), (), s32[]{:S(2)}) async-start(), calls=%async_computation.5 | async-start | bytes 1392640 | tf_op jit(solution)/shard_map/all_gather | solution.py:128
  29.7 82.1 %copy-start = (f32[1,40,8,128]{3,2,1,0:T(8,128)}, f32[1,40,8,128]{3,2,1,0:T(8,128)S(1)}, u32[]{:S(2)}) copy-start(f32[1,40,8,128]{3,2,1,0:T(8,128)S(1)} %get-tuple-element.260) | copy-start | bytes 491524
  46.6 62.4 %copy-start.130 = (f32[40,8]{0,1:T(8,128)}, f32[40,8]{0,1:T(8,128)S(1)}, u32[]{:S(2)}) copy-start(f32[40,8]{0,1:T(8,128)S(1)} %get-tuple-element.335) | copy-start | bytes 3844
  46.6 62.4 %copy-start.134 = (f32[40,8]{0,1:T(8,128)}, f32[40,8]{0,1:T(8,128)S(1)}, u32[]{:S(2)}) copy-start(f32[40,8]{0,1:T(8,128)S(1)} %get-tuple-element.348) | copy-start | bytes 3844
  48.4 165.9 %copy-start.6 = (f32[1,40,8,128]{3,2,1,0:T(8,128)}, f32[1,40,8,128]{3,2,1,0:T(8,128)S(1)}, u32[]{:S(2)}) copy-start(f32[1,40,8,128]{3,2,1,0:T(8,128)S(1)} %get-tuple-element.233) | copy-start | bytes 491524
  50.5 115.9 %copy-start.3 = (f32[1,40,8,128]{3,2,1,0:T(8,128)}, f32[1,40,8,128]{3,2,1,0:T(8,128)S(1)}, u32[]{:S(2)}) copy-start(f32[1,40,8,128]{3,2,1,0:T(8,128)S(1)} %get-tuple-element.229) | copy-start | bytes 491524
  52.8 60.6 %copy-start.16 = (f32[40,8,128]{2,0,1:T(8,128)}, f32[40,8,128]{2,0,1:T(8,128)S(1)}, u32[]{:S(2)}) copy-start(f32[40,8,128]{2,0,1:T(8,128)S(1)} %copy.914) | copy-start | bytes 491524
  115.9 94.8 %all-gather.20.cloned.1.call-start = ((), (), s32[]{:S(2)}) async-start(), calls=%async_computation.6 | async-start | bytes 1392640 | tf_op jit(solution)/shard_map/all_gather | solution.py:128
  118.7 44.8 %copy-start.21 = (f32[40,7,128]{2,1,0:T(8,128)}, f32[40,7,128]{2,1,0:T(8,128)S(1)}, u32[]{:S(2)}) copy-start(f32[40,7,128]{2,1,0:T(8,128)S(1)} %slice.2318) | copy-start | bytes 430084
  168.9 41.9 %copy-start.186 = (s32[4096]{0:T(1024)}, s32[4096]{0:T(1024)S(1)}, u32[]{:S(2)}) copy-start(s32[4096]{0:T(1024)S(1)} %reshape_squeeze.10) | copy-start | bytes 49156
  218.1 22.0 %copy-start.28 = (f32[40,8,127]{2,1,0:T(8,128)S(1)}, f32[40,8,127]{2,1,0:T(8,128)}, u32[]{:S(2)}) copy-start(f32[40,8,127]{2,1,0:T(8,128)} %slice.2242) | copy-start | bytes 487684
  312.9 14.1 %all-to-all-start.2 = ((f32[128,1,33]{2,1,0:T(1,128)}), f32[128,1,33]{2,1,0:T(1,128)S(1)}, u32[]{:S(2)}, u32[]{:S(2)}) async-start(f32[128,1,33]{2,1,0:T(1,128)} %bitcast.257), calls=%async_computation.2 | async-start | bytes 131072 | tf_op jit(solution)/shard_map/all_to_all | solution.py:144
  317.7 111.2 %all-gather.22.cloned.1.call-start = ((), (), s32[]{:S(2)}) async-start(), calls=%async_computation.7 | async-start | bytes 1392640 | tf_op jit(solution)/shard_map/all_gather | solution.py:128
  354.7 29.4 %copy-start.1 = (f32[1,40,8,128]{3,2,1,0:T(8,128)S(1)}, f32[1,40,8,128]{3,2,1,0:T(8,128)}, u32[]{:S(2)}) copy-start(f32[1,40,8,128]{3,2,1,0:T(8,128)} %copy-done) | copy-start | bytes 491524
  354.8 29.4 %copy-start.26 = (f32[40,8,128]{2,1,0:T(8,128)S(1)}, f32[40,8,128]{2,1,0:T(8,128)}, u32[]{:S(2)}) copy-start(f32[40,8,128]{2,1,0:T(8,128)} %pad_bitcast_fusion.1) | copy-start | bytes 491524
  386.9 42.0 %copy-start.56 = (f32[40,128]{1,0:T(8,128)S(1)}, f32[40,128]{1,0:T(8,128)}, u32[]{:S(2)}) copy-start(f32[40,128]{1,0:T(8,128)} %copy-done.54) | copy-start | bytes 61444
  387.0 42.0 %copy-start.61 = (f32[40,128]{1,0:T(8,128)S(1)}, f32[40,128]{1,0:T(8,128)}, u32[]{:S(2)}) copy-start(f32[40,128]{1,0:T(8,128)} %copy-done.59) | copy-start | bytes 61444
  387.0 42.0 %copy-start.66 = (f32[40,128]{1,0:T(8,128)S(1)}, f32[40,128]{1,0:T(8,128)}, u32[]{:S(2)}) copy-start(f32[40,128]{1,0:T(8,128)} %copy-done.64) | copy-start | bytes 61444
  387.0 42.0 %copy-start.86 = (f32[40,128]{1,0:T(8,128)S(1)}, f32[40,128]{1,0:T(8,128)}, u32[]{:S(2)}) copy-start(f32[40,128]{1,0:T(8,128)} %copy-done.85) | copy-start | bytes 61444
  389.3 91.4 %all-gather.24.cloned.1.call-start = ((), (), s32[]{:S(2)}) async-start(), calls=%async_computation.8 | async-start | bytes 1392640 | tf_op jit(solution)/shard_map/all_gather | solution.py:128
  487.9 22.0 %copy-start.29 = (f32[40,8,127]{2,1,0:T(8,128)S(1)}, f32[40,8,127]{2,1,0:T(8,128)}, u32[]{:S(2)}) copy-start(f32[40,8,127]{2,1,0:T(8,128)} %slice.2242) | copy-start | bytes 487684
  585.7 14.4 %all-to-all-start.4 = ((f32[128,1,33]{2,1,0:T(1,128)}), f32[128,1,33]{2,1,0:T(1,128)S(1)}, u32[]{:S(2)}, u32[]{:S(2)}) async-start(f32[128,1,33]{2,1,0:T(1,128)} %bitcast.378), calls=%async_computation.4 | async-start | bytes 131072 | tf_op jit(solution)/shard_map/all_to_all | solution.py:144
  590.8 93.2 %all-gather.26.cloned.1.call-start = ((), (), s32[]{:S(2)}) async-start(), calls=%async_computation.9 | async-start | bytes 1392640 | tf_op jit(solution)/shard_map/all_gather | solution.py:128
  642.8 41.3 %copy-start.58 = (f32[40,128]{1,0:T(8,128)S(1)}, f32[40,128]{1,0:T(8,128)}, u32[]{:S(2)}) copy-start(f32[40,128]{1,0:T(8,128)} %copy-done.54) | copy-start | bytes 61444
  642.8 41.3 %copy-start.63 = (f32[40,128]{1,0:T(8,128)S(1)}, f32[40,128]{1,0:T(8,128)}, u32[]{:S(2)}) copy-start(f32[40,128]{1,0:T(8,128)} %copy-done.59) | copy-start | bytes 61444
  642.8 41.3 %copy-start.69 = (f32[40,128]{1,0:T(8,128)S(1)}, f32[40,128]{1,0:T(8,128)}, u32[]{:S(2)}) copy-start(f32[40,128]{1,0:T(8,128)} %copy-done.64) | copy-start | bytes 61444
  642.8 41.3 %copy-start.87 = (f32[40,128]{1,0:T(8,128)S(1)}, f32[40,128]{1,0:T(8,128)}, u32[]{:S(2)}) copy-start(f32[40,128]{1,0:T(8,128)} %copy-done.85) | copy-start | bytes 61444
  642.8 41.3 %copy-start.89 = (f32[40,128]{1,0:T(8,128)S(1)}, f32[40,128]{1,0:T(8,128)}, u32[]{:S(2)}) copy-start(f32[40,128]{1,0:T(8,128)} %copy-done.88) | copy-start | bytes 61444
  642.8 41.3 %copy-start.91 = (f32[40,128]{1,0:T(8,128)S(1)}, f32[40,128]{1,0:T(8,128)}, u32[]{:S(2)}) copy-start(f32[40,128]{1,0:T(8,128)} %copy-done.90) | copy-start | bytes 61444
  642.8 41.3 %copy-start.93 = (f32[40,128]{1,0:T(8,128)S(1)}, f32[40,128]{1,0:T(8,128)}, u32[]{:S(2)}) copy-start(f32[40,128]{1,0:T(8,128)} %copy-done.92) | copy-start | bytes 61444
  642.8 41.3 %copy-start.95 = (f32[40,128]{1,0:T(8,128)S(1)}, f32[40,128]{1,0:T(8,128)}, u32[]{:S(2)}) copy-start(f32[40,128]{1,0:T(8,128)} %copy-done.94) | copy-start | bytes 61444
  642.8 41.3 %copy-start.96 = (f32[40,128]{1,0:T(8,128)S(1)}, f32[40,128]{1,0:T(8,128)}, u32[]{:S(2)}) copy-start(f32[40,128]{1,0:T(8,128)} %get-tuple-element.299) | copy-start | bytes 61444
  642.9 41.3 %copy-start.97 = (f32[40,128]{1,0:T(8,128)S(1)}, f32[40,128]{1,0:T(8,128)}, u32[]{:S(2)}) copy-start(f32[40,128]{1,0:T(8,128)} %get-tuple-element.300) | copy-start | bytes 61444
  642.9 41.3 %copy-start.98 = (f32[40,128]{1,0:T(8,128)S(1)}, f32[40,128]{1,0:T(8,128)}, u32[]{:S(2)}) copy-start(f32[40,128]{1,0:T(8,128)} %get-tuple-element.301) | copy-start | bytes 61444
  642.9 41.3 %copy-start.99 = (f32[40,128]{1,0:T(8,128)S(1)}, f32[40,128]{1,0:T(8,128)}, u32[]{:S(2)}) copy-start(f32[40,128]{1,0:T(8,128)} %get-tuple-element.302) | copy-start | bytes 61444
  642.9 41.3 %copy-start.100 = (f32[40,128]{1,0:T(8,128)S(1)}, f32[40,128]{1,0:T(8,128)}, u32[]{:S(2)}) copy-start(f32[40,128]{1,0:T(8,128)} %get-tuple-element.303) | copy-start | bytes 61444
  642.9 41.3 %copy-start.101 = (f32[40,128]{1,0:T(8,128)S(1)}, f32[40,128]{1,0:T(8,128)}, u32[]{:S(2)}) copy-start(f32[40,128]{1,0:T(8,128)} %get-tuple-element.304) | copy-start | bytes 61444
  642.9 41.3 %copy-start.102 = (f32[40,128]{1,0:T(8,128)S(1)}, f32[40,128]{1,0:T(8,128)}, u32[]{:S(2)}) copy-start(f32[40,128]{1,0:T(8,128)} %get-tuple-element.305) | copy-start | bytes 61444
  642.9 41.3 %copy-start.103 = (f32[40,128]{1,0:T(8,128)S(1)}, f32[40,128]{1,0:T(8,128)}, u32[]{:S(2)}) copy-start(f32[40,128]{1,0:T(8,128)} %get-tuple-element.306) | copy-start | bytes 61444
  642.9 41.3 %copy-start.104 = (f32[40,128]{1,0:T(8,128)S(1)}, f32[40,128]{1,0:T(8,128)}, u32[]{:S(2)}) copy-start(f32[40,128]{1,0:T(8,128)} %get-tuple-element.307) | copy-start | bytes 61444
  642.9 41.3 %copy-start.105 = (f32[40,128]{1,0:T(8,128)S(1)}, f32[40,128]{1,0:T(8,128)}, u32[]{:S(2)}) copy-start(f32[40,128]{1,0:T(8,128)} %get-tuple-element.308) | copy-start | bytes 61444
  642.9 41.3 %copy-start.106 = (f32[40,128]{1,0:T(8,128)S(1)}, f32[40,128]{1,0:T(8,128)}, u32[]{:S(2)}) copy-start(f32[40,128]{1,0:T(8,128)} %get-tuple-element.309) | copy-start | bytes 61444
  643.0 41.3 %copy-start.107 = (f32[40,128]{1,0:T(8,128)S(1)}, f32[40,128]{1,0:T(8,128)}, u32[]{:S(2)}) copy-start(f32[40,128]{1,0:T(8,128)} %get-tuple-element.310) | copy-start | bytes 61444
  643.0 41.3 %copy-start.108 = (f32[40,128]{1,0:T(8,128)S(1)}, f32[40,128]{1,0:T(8,128)}, u32[]{:S(2)}) copy-start(f32[40,128]{1,0:T(8,128)} %get-tuple-element.263) | copy-start | bytes 61444
  643.0 41.3 %copy-start.109 = (f32[40,128]{1,0:T(8,128)S(1)}, f32[40,128]{1,0:T(8,128)}, u32[]{:S(2)}) copy-start(f32[40,128]{1,0:T(8,128)} %get-tuple-element.265) | copy-start | bytes 61444
  643.0 41.3 %copy-start.110 = (f32[40,128]{1,0:T(8,128)S(1)}, f32[40,128]{1,0:T(8,128)}, u32[]{:S(2)}) copy-start(f32[40,128]{1,0:T(8,128)} %get-tuple-element.267) | copy-start | bytes 61444
  643.0 41.3 %copy-start.111 = (f32[40,128]{1,0:T(8,128)S(1)}, f32[40,128]{1,0:T(8,128)}, u32[]{:S(2)}) copy-start(f32[40,128]{1,0:T(8,128)} %get-tuple-element.269) | copy-start | bytes 61444
  643.0 41.3 %copy-start.112 = (f32[40,128]{1,0:T(8,128)S(1)}, f32[40,128]{1,0:T(8,128)}, u32[]{:S(2)}) copy-start(f32[40,128]{1,0:T(8,128)} %get-tuple-element.271) | copy-start | bytes 61444
  643.0 41.3 %copy-start.113 = (f32[40,128]{1,0:T(8,128)S(1)}, f32[40,128]{1,0:T(8,128)}, u32[]{:S(2)}) copy-start(f32[40,128]{1,0:T(8,128)} %get-tuple-element.273) | copy-start | bytes 61444
  643.0 41.3 %copy-start.114 = (f32[40,128]{1,0:T(8,128)S(1)}, f32[40,128]{1,0:T(8,128)}, u32[]{:S(2)}) copy-start(f32[40,128]{1,0:T(8,128)} %get-tuple-element.275) | copy-start | bytes 61444
  643.0 41.3 %copy-start.115 = (f32[40,128]{1,0:T(8,128)S(1)}, f32[40,128]{1,0:T(8,128)}, u32[]{:S(2)}) copy-start(f32[40,128]{1,0:T(8,128)} %get-tuple-element.277) | copy-start | bytes 61444
  643.0 41.3 %copy-start.116 = (f32[40,128]{1,0:T(8,128)S(1)}, f32[40,128]{1,0:T(8,128)}, u32[]{:S(2)}) copy-start(f32[40,128]{1,0:T(8,128)} %get-tuple-element.278) | copy-start | bytes 61444
  643.1 41.3 %copy-start.117 = (f32[40,128]{1,0:T(8,128)S(1)}, f32[40,128]{1,0:T(8,128)}, u32[]{:S(2)}) copy-start(f32[40,128]{1,0:T(8,128)} %get-tuple-element.279) | copy-start | bytes 61444
  643.1 41.3 %copy-start.118 = (f32[40,128]{1,0:T(8,128)S(1)}, f32[40,128]{1,0:T(8,128)}, u32[]{:S(2)}) copy-start(f32[40,128]{1,0:T(8,128)} %get-tuple-element.280) | copy-start | bytes 61444
  643.1 41.3 %copy-start.119 = (f32[40,128]{1,0:T(8,128)S(1)}, f32[40,128]{1,0:T(8,128)}, u32[]{:S(2)}) copy-start(f32[40,128]{1,0:T(8,128)} %get-tuple-element.281) | copy-start | bytes 61444
  643.1 41.3 %copy-start.120 = (f32[40,128]{1,0:T(8,128)S(1)}, f32[40,128]{1,0:T(8,128)}, u32[]{:S(2)}) copy-start(f32[40,128]{1,0:T(8,128)} %multiply_subtract_fusion.3) | copy-start | bytes 61444
  643.1 41.3 %copy-start.121 = (f32[40,128]{1,0:T(8,128)S(1)}, f32[40,128]{1,0:T(8,128)}, u32[]{:S(2)}) copy-start(f32[40,128]{1,0:T(8,128)} %multiply_subtract_fusion.2) | copy-start | bytes 61444
  643.1 41.3 %copy-start.122 = (f32[40,128]{1,0:T(8,128)S(1)}, f32[40,128]{1,0:T(8,128)}, u32[]{:S(2)}) copy-start(f32[40,128]{1,0:T(8,128)} %get-tuple-element.282) | copy-start | bytes 61444
  643.1 41.3 %copy-start.123 = (f32[40,128]{1,0:T(8,128)S(1)}, f32[40,128]{1,0:T(8,128)}, u32[]{:S(2)}) copy-start(f32[40,128]{1,0:T(8,128)} %get-tuple-element.283) | copy-start | bytes 61444
  643.1 41.3 %copy-start.124 = (f32[40,128]{1,0:T(8,128)S(1)}, f32[40,128]{1,0:T(8,128)}, u32[]{:S(2)}) copy-start(f32[40,128]{1,0:T(8,128)} %get-tuple-element.284) | copy-start | bytes 61444
  643.1 41.3 %copy-start.125 = (f32[40,128]{1,0:T(8,128)S(1)}, f32[40,128]{1,0:T(8,128)}, u32[]{:S(2)}) copy-start(f32[40,128]{1,0:T(8,128)} %get-tuple-element.285) | copy-start | bytes 61444
  643.1 41.3 %copy-start.126 = (f32[40,128]{1,0:T(8,128)S(1)}, f32[40,128]{1,0:T(8,128)}, u32[]{:S(2)}) copy-start(f32[40,128]{1,0:T(8,128)} %get-tuple-element.286) | copy-start | bytes 61444
  (137 other events, 1113.6 us)
Sparse Core Ops, SparseCore 0:
  116.0 44.2 all-gather.17
  168.1 42.6 all-gather.19
  389.4 39.4 all-gather.21
  438.0 42.6 all-gather.23
  644.5 39.4 all-gather.25

commit v3 on v2

--- a/solution.py
+++ b/solution.py
@@ -2,6 +2,8 @@
 import jax.numpy as jnp
 from jax import lax
 from jax.sharding import PartitionSpec as P
+from jax.experimental import pallas as pl
+from jax.experimental.pallas import tpu as pltpu
 
 TR = 2
 ITERS = 2
@@ -136,6 +138,85 @@
     return plan["gain_out"] * (forward + next_offset + next_factor * leaving)
 
 
+CHUNK = 512
+
+
+def split_three(values):
+    high = values.astype(jnp.bfloat16)
+    rest = values - high.astype(jnp.float32)
+    middle = rest.astype(jnp.bfloat16)
+    low = (rest - middle.astype(jnp.float32)).astype(jnp.bfloat16)
+    return high, middle, low
+
+
+def pick_kernel(field_ref, rows_ref, lanes_ref, out_ref):
+    field_rows, lanes = field_ref.shape
+    chunk = rows_ref.shape[1]
+    parts = split_three(field_ref[...].T)
+    hot = (
+        lax.broadcasted_iota(jnp.int32, (field_rows, chunk), 0) == rows_ref[...]
+    ).astype(jnp.bfloat16)
+    picked = None
+    for part in parts:
+        term = jnp.dot(part, hot, preferred_element_type=jnp.float32)
+        picked = term if picked is None else picked + term
+    chosen = lax.broadcasted_iota(jnp.int32, (lanes, chunk), 0) == lanes_ref[...]
+    out_ref[...] = jnp.sum(jnp.where(chosen, picked, 0.0), axis=0, keepdims=True)
+
+
+def pick_cells(field_rows, rows, lanes):
+    count = rows.shape[1]
+    return pl.pallas_call(
+        pick_kernel,
+        out_shape=jax.ShapeDtypeStruct((1, count), jnp.float32),
+        grid=(count // CHUNK,),
+        in_specs=[
+            pl.BlockSpec(field_rows.shape, lambda i: (0, 0)),
+            pl.BlockSpec((1, CHUNK), lambda i: (0, i)),
+            pl.BlockSpec((1, CHUNK), lambda i: (0, i)),
+        ],
+        out_specs=pl.BlockSpec((1, CHUNK), lambda i: (0, i)),
+    )(field_rows, rows, lanes)
+
+
+def add_kernel(values_ref, rows_ref, lanes_ref, out_ref):
+    field_rows, lanes = out_ref.shape
+    chunk = rows_ref.shape[1]
+
+    @pl.when(pl.program_id(0) == 0)
+    def _():
+        out_ref[...] = jnp.zeros_like(out_ref)
+
+    chosen = lax.broadcasted_iota(jnp.int32, (lanes, chunk), 0) == lanes_ref[...]
+    placed = jnp.where(chosen, values_ref[...], 0.0)
+    hot = (
+        lax.broadcasted_iota(jnp.int32, (field_rows, chunk), 0) == rows_ref[...]
+    ).astype(jnp.bfloat16)
+    total = None
+    for part in split_three(placed):
+        term = lax.dot_general(
+            hot, part, (((1,), (1,)), ((), ())), preferred_element_type=jnp.float32
+        )
+        total = term if total is None else total + term
+    out_ref[...] += total
+
+
+def add_cells(values, rows, lanes, field_rows, lane_count):
+    count = rows.shape[1]
+    return pl.pallas_call(
+        add_kernel,
+        out_shape=jax.ShapeDtypeStruct((field_rows, lane_count), jnp.float32),
+        grid=(count // CHUNK,),
+        in_specs=[
+            pl.BlockSpec((1, CHUNK), lambda i: (0, i)),
+            pl.BlockSpec((1, CHUNK), lambda i: (0, i)),
+            pl.BlockSpec((1, CHUNK), lambda i: (0, i)),
+        ],
+        out_specs=pl.BlockSpec((field_rows, lane_count), lambda i: (0, 0)),
+        compiler_params=pltpu.CompilerParams(dimension_semantics=("arbitrary",)),
+    )(values, rows, lanes)
+
+
 def exchange(values, partial):
     rows = values.shape[0]
     packed = jnp.concatenate(
@@ -174,18 +255,19 @@
         mixed = jnp.einsum("nij,nj->ni", blocks, packed, precision=lax.Precision.HIGHEST)
         return occupied * mixed.reshape(occupied.shape)
 
+    lane_count = field_shape[-1]
+    field_rows = TR * rate_x.size // lane_count
+    flat_index = cell_index.reshape(1, -1)
+    row_of = flat_index // lane_count
+    lane_of = flat_index % lane_count
+
     def deposit_local(arrived):
-        flat_cells = (
-            jnp.zeros((TR * rate_x.size,), jnp.float32)
-            .at[cell_index.reshape(-1)]
-            .add(arrived.reshape(-1))
-        )
-        return flat_cells.reshape(field_shape)
+        cells = add_cells(arrived.reshape(1, -1), row_of, lane_of, field_rows, lane_count)
+        return cells.reshape(field_shape)
 
     def observe(vector):
-        return jnp.take(vector.reshape(-1), cell_index.reshape(-1), axis=0).reshape(
-            cell_index.shape
-        )
+        picked = pick_cells(vector.reshape(field_rows, lane_count), row_of, lane_of)
+        return picked.reshape(cell_index.shape)
 
     weighted = weigh_obs(innovation[0])
     arrived = lax.all_to_all(weighted, ("gx", "gy"), split_axis=0, concat_axis=0, tiled=True)

time: 706 us -> 759 us (1.075)
  local copies, waits for them, and re-layouts: 163 us -> 215 us
  other arithmetic: 148 us -> 101 us
  Pallas kernels: 0 us -> 35.5 us
    unnamed x564 -> x822, local copies, waits for them, and re-layouts: 33.6 us -> 126 us
    gather x2 -> x0, local copies, waits for them, and re-layouts: 81.4 us -> none  [observe(): jnp.take(vector.reshape(-1), cell_index.reshape(-1), axis=0)]
    scatter-add x3 -> x0, other arithmetic: 67 us -> none  [deposit_local(): flat_cells = jnp.zeros((TR * rate_x.size,), jnp.float32).at[cell_index.re...]
    pallas_call x0 -> x5, Pallas kernels: none -> 35.5 us  [the longest x3 22.1 us: add_cells(): pl.pallas_call(add_kernel, out_shape=jax.ShapeDtypeStruct((field_rows, la...]
    mul x2 -> x16, local copies, waits for them, and re-layouts: 1.66 us -> 14.8 us  [scan_offsets(): level_factor * shift_along(forcing, distance, line_axis, reverse, 0.0)]
    another operation x1 -> x19, local copies, waits for them, and re-layouts: 0.01 us -> 11.7 us  [line_operator(): jnp.stack([lax.index_in_dim(offset, length - 1, line_axis, keepdims=False...]
    dynamic_slice x20 -> x0, local copies, waits for them, and re-layouts: 8.68 us -> none  [the longest x10 5.11 us: carries(): mine_in = lax.dynamic_index_in_dim(jnp.stack(entering), place, 0, False)]
    mul x7 -> x19, local copies, waits for them, and re-layouts: 2.36 us -> 11 us  [line_operator(): return plan['gain_out'] * (forward + next_offset + next_factor * leaving)]
  transfers between devices with their start and end apart: 8 -> 8, of which waited for: 7 -> 7; matrix products, arithmetic and copies ran while one was open for 4% -> 5% of each run, Pallas kernels for 0% -> 0%
where the time goes in v3:
time: 759 us; the launch traced here: 745 us
  local copies, waits for them, and re-layouts  215 us (28%)
  waiting for transfers between devices  189 us (25%)
  blocking collectives  137 us (18%)
  other arithmetic  101 us (13%)
  Pallas kernels  35.5 us (5%)
  between operations  27 us (4%)
  starting transfers between devices  21.7 us (3%)
  matrix products  17 us (2%)
    all_gather x5, waiting for transfers between devices, line_operator(): got = lax.all_gather(mine, plan['axis_name'])  172 us
    unnamed x822, local copies, waits for them, and re-layouts  126 us
    all_gather x5, blocking collectives, line_operator(): got = lax.all_gather(mine, plan['axis_name'])  65.6 us
    all_gather x2, blocking collectives, make_plan(): lax.all_gather(totals, axis_name)  38.9 us
    all_to_all x2, blocking collectives, exchange(): lax.all_to_all(packed, ('gx', 'gy'), split_axis=0, concat_axis=0, tiled=T...  32.9 us
    pallas_call x3, Pallas kernels, add_cells(): pl.pallas_call(add_kernel, out_shape=jax.ShapeDtypeStruct((field_rows, la...  22.1 us
    unnamed x56, other arithmetic  20.6 us
    add x100, other arithmetic, scan_offsets(): forcing + level_factor * shift_along(forcing, distance, line_axis, revers...  18.4 us
  transfers between devices with their start and end apart: 8, of which 7 were waited for; matrix products, arithmetic and copies ran while one was open for 5% of the time, Pallas kernels for 0%

profile of v3, /device:TPU:0, one launch (start us, length us, event | category | flops | bytes accessed | tf_op | source)
XLA Modules:
  0.0 744.5 jit_solution(1336420305358323345)
XLA Ops:
  10.3 5.7 fusion.4
  16.8 11.7 %all-to-all-start = ((f32[128,1,32]{2,1,0:T(1,128)}), f32[128,1,32]{2,1,0:T(1,128)}, u32[]{:S(2)}, u32[]{:S(2)}) async-start(f32[128,1,32]{2,1,0:T(1,128)} %bitcast.4), calls=%async_computation | async-start | bytes 131072 | tf_op jit(solution)/shard_map/all_to_all | solution.py:273
  32.7 13.0 %all-gather.1 = f32[24,1,40,8]{2,3,1,0:T(8,128)S(1)} all-gather(f32[3,1,40,8]{2,3,1,0:T(8,128)S(1)} %pad_maximum_fusion.11), channel_id=3, replica_groups=mesh['gx'=16,'gy'=8] {'gy'}, dimensions={0}, use_global_device_ids=true | all-gather | bytes 34560 | tf_op jit(solution)/shard_map/all_gather | solution.py:71
  72.1 1.6 reduce.17
  74.4 7.4 shard_map.86
  81.8 2.4 copy.651
  102.2 13.2 %all-gather = f32[16,2,40,8]{2,3,1,0:T(8,128)S(1)} all-gather(f32[2,2,40,8]{2,3,1,0:T(8,128)S(1)} %pad_maximum_fusion.6), channel_id=2, replica_groups=mesh['gx'=16,'gy'=8] {'gy'}, dimensions={0}, use_global_device_ids=true | all-gather | bytes 46080 | tf_op jit(solution)/shard_map/all_gather | solution.py:130
  127.4 25.9 %all-gather.2 = f32[48,1,40,128]{3,2,1,0:T(8,128)S(1)} all-gather(f32[3,1,40,128]{3,2,1,0:T(8,128)S(1)} %pad_maximum_fusion.5), channel_id=4, replica_groups=mesh['gx'=16,'gy'=8] {'gx'}, dimensions={0}, use_global_device_ids=true | all-gather | bytes 1044480 | tf_op jit(solution)/shard_map/all_gather | solution.py:71
  154.5 15.1 %all-gather.18.cloned.1.call-done = f32[32,2,40,128]{3,2,1,0:T(8,128)} async-done(((f32[2,2,40,128]{3,2,1,0:T(8,128)}), f32[32,2,40,128]{3,2,1,0:T(8,128)}) %all-gather.18.cloned.1.call-update) | async-done | bytes 1310736 | tf_op jit(solution)/shard_map/all_gather | solution.py:130
  169.5 2.4 constant_dynamic-update-slice_fusion.47
  188.0 1.6 slice_add_fusion.4
  199.3 1.6 copy.715
  200.9 1.6 copy.714
  204.6 42.2 %all-gather.20.cloned.1.call-done = f32[32,2,40,128]{3,2,1,0:T(8,128)} async-done(((f32[2,2,40,128]{3,2,1,0:T(8,128)}), f32[32,2,40,128]{3,2,1,0:T(8,128)}) %all-gather.20.cloned.1.call-update) | async-done | bytes 1310736 | tf_op jit(solution)/shard_map/all_gather | solution.py:130
  246.8 2.6 constant_dynamic-update-slice_fusion.79
  250.3 1.5 copy.717
  263.6 1.7 slice_add_fusion.3
  281.6 13.2 %all-gather.5 = f32[16,2,40,8]{2,3,1,0:T(8,128)S(1)} all-gather(f32[2,2,40,8]{2,3,1,0:T(8,128)S(1)} %pad_maximum_fusion.7), channel_id=7, replica_groups=mesh['gx'=16,'gy'=8] {'gy'}, dimensions={0}, use_global_device_ids=true | all-gather | bytes 46080 | tf_op jit(solution)/shard_map/all_gather | solution.py:130
  297.8 2.4 copy.718
  300.1 6.7 shard_map.87
  308.8 16.4 %all_to_all.54 = f32[128,1,33]{2,1,0:T(1,128)S(1)} all-to-all(f32[128,1,33]{2,1,0:T(1,128)S(1)} %bitcast.2312), channel_id=1, replica_groups=mesh['gx'=16,'gy'=8] {'gx','gy'}, dimensions={0} | all-to-all | bytes 33792 | tf_op jit(solution)/shard_map/all_to_all | solution.py:225
  326.7 5.7 fusion.2
  333.8 2.0 multiply_reduce_fusion.4
  338.6 4.8 all-to-all-start.2
  344.0 8.6 %all-to-all-done.2 = f32[128,1,33]{2,1,0:T(1,128)S(1)} async-done(((f32[128,1,33]{2,1,0:T(1,128)}), f32[128,1,33]{2,1,0:T(1,128)S(1)}, u32[]{:S(2)}, u32[]{:S(2)}) %all-to-all-start.2) | async-done | bytes 16928 | tf_op jit(solution)/shard_map/all_to_all | solution.py:225
  353.3 7.4 shard_map.88
  360.7 2.4 copy.721
  381.2 13.0 %all-gather.6 = f32[16,2,40,8]{2,3,1,0:T(8,128)S(1)} all-gather(f32[2,2,40,8]{2,3,1,0:T(8,128)S(1)} %pad_maximum_fusion.8), channel_id=8, replica_groups=mesh['gx'=16,'gy'=8] {'gy'}, dimensions={0}, use_global_device_ids=true | all-gather | bytes 46080 | tf_op jit(solution)/shard_map/all_gather | solution.py:130
  404.2 1.6 copy.723
  405.8 1.6 copy.722
  409.5 1.5 slice_reduce_fusion.2
  412.3 36.2 %all-gather.22.cloned.1.call-done = f32[32,2,40,128]{3,2,1,0:T(8,128)} async-done(((f32[2,2,40,128]{3,2,1,0:T(8,128)}), f32[32,2,40,128]{3,2,1,0:T(8,128)}) %all-gather.22.cloned.1.call-update) | async-done | bytes 1310736 | tf_op jit(solution)/shard_map/all_gather | solution.py:130
  448.5 2.5 constant_dynamic-update-slice_fusion.143
  452.7 1.5 copy.724
  454.3 2.7 slice_add_fusion.2
  458.4 1.5 copy.725
  460.0 3.2 multiply_reduce_fusion.1
  472.1 1.6 copy.727
  473.7 1.6 copy.726
  477.3 42.2 %all-gather.24.cloned.1.call-done = f32[32,2,40,128]{3,2,1,0:T(8,128)} async-done(((f32[2,2,40,128]{3,2,1,0:T(8,128)}), f32[32,2,40,128]{3,2,1,0:T(8,128)}) %all-gather.24.cloned.1.call-update) | async-done | bytes 1310736 | tf_op jit(solution)/shard_map/all_gather | solution.py:130
  519.5 2.5 constant_dynamic-update-slice_fusion.175
  522.9 1.5 copy.729
  536.9 1.8 slice_add_fusion.1
  554.9 13.5 %all-gather.9 = f32[16,2,40,8]{2,3,1,0:T(8,128)S(1)} all-gather(f32[2,2,40,8]{2,3,1,0:T(8,128)S(1)} %pad_maximum_fusion.9), channel_id=11, replica_groups=mesh['gx'=16,'gy'=8] {'gy'}, dimensions={0}, use_global_device_ids=true | all-gather | bytes 46080 | tf_op jit(solution)/shard_map/all_gather | solution.py:130
  571.3 2.4 copy.730
  573.7 6.7 shard_map.89
  580.4 1.9 reduce.19
  583.8 16.5 %all_to_all.55 = f32[128,1,33]{2,1,0:T(1,128)S(1)} all-to-all(f32[128,1,33]{2,1,0:T(1,128)S(1)} %bitcast.2311), channel_id=1, replica_groups=mesh['gx'=16,'gy'=8] {'gx','gy'}, dimensions={0} | all-to-all | bytes 33792 | tf_op jit(solution)/shard_map/all_to_all | solution.py:225
  602.0 2.2 multiply_reduce_fusion
  604.9 1.5 reshape.27315
  606.5 5.7 fusion
  614.2 2.2 multiply_reduce_fusion.3
  617.6 1.5 concatenate.569
  619.1 4.8 all-to-all-start.4
  624.7 8.4 %all-to-all-done.4 = f32[128,1,33]{2,1,0:T(1,128)S(1)} async-done(((f32[128,1,33]{2,1,0:T(1,128)}), f32[128,1,33]{2,1,0:T(1,128)S(1)}, u32[]{:S(2)}, u32[]{:S(2)}) %all-to-all-start.4) | async-done | bytes 16928 | tf_op jit(solution)/shard_map/all_to_all | solution.py:225
  633.9 7.4 shard_map.90
  641.2 2.4 copy.733
  662.0 12.8 %all-gather.10 = f32[16,2,40,8]{2,3,1,0:T(8,128)S(1)} all-gather(f32[2,2,40,8]{2,3,1,0:T(8,128)S(1)} %pad_maximum_fusion.10), channel_id=12, replica_groups=mesh['gx'=16,'gy'=8] {'gy'}, dimensions={0}, use_global_device_ids=true | all-gather | bytes 46080 | tf_op jit(solution)/shard_map/all_gather | solution.py:130
  686.0 1.6 slice_reduce_fusion
  688.9 36.8 %all-gather.26.cloned.1.call-done = f32[32,2,40,128]{3,2,1,0:T(8,128)} async-done(((f32[2,2,40,128]{3,2,1,0:T(8,128)}), f32[32,2,40,128]{3,2,1,0:T(8,128)}) %all-gather.26.cloned.1.call-update) | async-done | bytes 1310736 | tf_op jit(solution)/shard_map/all_gather | solution.py:130
  725.7 1.9 constant_dynamic-update-slice_fusion.239
  729.2 1.6 slice_add_fusion
  731.0 3.2 multiply_subtract_fusion
  734.2 2.4 copy.738
  (1290 shorter events, 243.5 us)
Async XLA Ops:
  10.3 18.3 %copy-start.124 = (f32[40,8,128]{2,1,0:T(8,128)S(1)}, f32[40,8,128]{2,1,0:T(8,128)}, u32[]{:S(2)}) copy-start(f32[40,8,128]{2,1,0:T(8,128)} %param.8) | copy-start | bytes 491524
  16.8 54.9 %all-to-all-start = ((f32[128,1,32]{2,1,0:T(1,128)}), f32[128,1,32]{2,1,0:T(1,128)}, u32[]{:S(2)}, u32[]{:S(2)}) async-start(f32[128,1,32]{2,1,0:T(1,128)} %bitcast.4), calls=%async_computation | async-start | bytes 131072 | tf_op jit(solution)/shard_map/all_to_all | solution.py:273
  28.5 141.0 %all-gather.18.cloned.1.call-start = ((), (), s32[]{:S(2)}) async-start(), calls=%async_computation.5 | async-start | bytes 1392640 | tf_op jit(solution)/shard_map/all_gather | solution.py:130
  32.1 15.0 %copy-start.315 = (s32[1,128,32]{1,2,0:T(8,128)S(1)}, s32[1,128,32]{1,2,0:T(8,128)}, u32[]{:S(2)}) copy-start(s32[1,128,32]{1,2,0:T(8,128)} %param.10) | copy-start | bytes 49156
  32.1 18.0 %copy-start.130 = (f32[1,40,8,128]{3,2,1,0:T(8,128)}, f32[1,40,8,128]{3,2,1,0:T(8,128)S(1)}, u32[]{:S(2)}) copy-start(f32[1,40,8,128]{3,2,1,0:T(8,128)S(1)} %get-tuple-element.256) | copy-start | bytes 491524
  32.1 17.1 %copy-start.125 = (f32[40,8,128]{2,1,0:T(8,128)S(1)}, f32[40,8,128]{2,1,0:T(8,128)}, u32[]{:S(2)}) copy-start(f32[40,8,128]{2,1,0:T(8,128)} %param.7) | copy-start | bytes 491524
  46.9 68.9 %copy-start.190 = (f32[40,8]{0,1:T(8,128)}, f32[40,8]{0,1:T(8,128)S(1)}, u32[]{:S(2)}) copy-start(f32[40,8]{0,1:T(8,128)S(1)} %get-tuple-element.346) | copy-start | bytes 3844
  46.9 68.9 %copy-start.194 = (f32[40,8]{0,1:T(8,128)}, f32[40,8]{0,1:T(8,128)S(1)}, u32[]{:S(2)}) copy-start(f32[40,8]{0,1:T(8,128)S(1)} %get-tuple-element.359) | copy-start | bytes 3844
  70.4 48.4 %copy-start.7 = (f32[40,8,128]{0,1,2:T(8,128)}, f32[40,8,128]{0,1,2:T(8,128)S(1)}, u32[]{:S(2)}) copy-start(f32[40,8,128]{0,1,2:T(8,128)S(1)} %copy.673) | copy-start | bytes 491524
  70.6 49.8 %copy-start.2 = (f32[40,8,128]{0,1,2:T(8,128)}, f32[40,8,128]{0,1,2:T(8,128)S(1)}, u32[]{:S(2)}) copy-start(f32[40,8,128]{0,1,2:T(8,128)S(1)} %copy.690) | copy-start | bytes 491524
  124.8 121.9 %all-gather.20.cloned.1.call-start = ((), (), s32[]{:S(2)}) async-start(), calls=%async_computation.6 | async-start | bytes 1392640 | tf_op jit(solution)/shard_map/all_gather | solution.py:130
  125.3 62.7 %copy-start.77 = (f32[40,7,128]{0,1,2:T(8,128)}, f32[40,7,128]{0,1,2:T(8,128)S(1)}, u32[]{:S(2)}) copy-start(f32[40,7,128]{0,1,2:T(8,128)S(1)} %copy.752) | copy-start | bytes 430084
  153.4 18.5 %copy-start.176 = (f32[40,128]{1,0:T(8,128)}, f32[40,128]{1,0:T(8,128)S(1)}, u32[]{:S(2)}) copy-start(f32[40,128]{1,0:T(8,128)S(1)} %multiply_subtract_fusion.3) | copy-start | bytes 61444
  153.4 18.5 %copy-start.177 = (f32[40,128]{1,0:T(8,128)}, f32[40,128]{1,0:T(8,128)S(1)}, u32[]{:S(2)}) copy-start(f32[40,128]{1,0:T(8,128)S(1)} %multiply_subtract_fusion.2) | copy-start | bytes 61444
  154.1 17.8 %copy-start.178 = (f32[40,128]{1,0:T(8,128)}, f32[40,128]{1,0:T(8,128)S(1)}, u32[]{:S(2)}) copy-start(f32[40,128]{1,0:T(8,128)S(1)} %get-tuple-element.295) | copy-start | bytes 61444
  154.1 17.8 %copy-start.179 = (f32[40,128]{1,0:T(8,128)}, f32[40,128]{1,0:T(8,128)S(1)}, u32[]{:S(2)}) copy-start(f32[40,128]{1,0:T(8,128)S(1)} %get-tuple-element.296) | copy-start | bytes 61444
  154.2 17.8 %copy-start.134 = (f32[40,128]{1,0:T(8,128)}, f32[40,128]{1,0:T(8,128)S(1)}, u32[]{:S(2)}) copy-start(f32[40,128]{1,0:T(8,128)S(1)} %get-tuple-element.309) | copy-start | bytes 61444
  154.2 17.8 %copy-start.138 = (f32[40,128]{1,0:T(8,128)}, f32[40,128]{1,0:T(8,128)S(1)}, u32[]{:S(2)}) copy-start(f32[40,128]{1,0:T(8,128)S(1)} %get-tuple-element.310) | copy-start | bytes 61444
  154.2 17.8 %copy-start.142 = (f32[40,128]{1,0:T(8,128)}, f32[40,128]{1,0:T(8,128)S(1)}, u32[]{:S(2)}) copy-start(f32[40,128]{1,0:T(8,128)S(1)} %get-tuple-element.311) | copy-start | bytes 61444
  154.2 17.8 %copy-start.146 = (f32[40,128]{1,0:T(8,128)}, f32[40,128]{1,0:T(8,128)S(1)}, u32[]{:S(2)}) copy-start(f32[40,128]{1,0:T(8,128)S(1)} %get-tuple-element.312) | copy-start | bytes 61444
  154.2 17.8 %copy-start.149 = (f32[40,128]{1,0:T(8,128)}, f32[40,128]{1,0:T(8,128)S(1)}, u32[]{:S(2)}) copy-start(f32[40,128]{1,0:T(8,128)S(1)} %get-tuple-element.313) | copy-start | bytes 61444
  154.2 17.8 %copy-start.152 = (f32[40,128]{1,0:T(8,128)}, f32[40,128]{1,0:T(8,128)S(1)}, u32[]{:S(2)}) copy-start(f32[40,128]{1,0:T(8,128)S(1)} %get-tuple-element.314) | copy-start | bytes 61444
  154.2 17.8 %copy-start.155 = (f32[40,128]{1,0:T(8,128)}, f32[40,128]{1,0:T(8,128)S(1)}, u32[]{:S(2)}) copy-start(f32[40,128]{1,0:T(8,128)S(1)} %get-tuple-element.315) | copy-start | bytes 61444
  154.2 17.8 %copy-start.156 = (f32[40,128]{1,0:T(8,128)}, f32[40,128]{1,0:T(8,128)S(1)}, u32[]{:S(2)}) copy-start(f32[40,128]{1,0:T(8,128)S(1)} %get-tuple-element.316) | copy-start | bytes 61444
  154.2 17.8 %copy-start.157 = (f32[40,128]{1,0:T(8,128)}, f32[40,128]{1,0:T(8,128)S(1)}, u32[]{:S(2)}) copy-start(f32[40,128]{1,0:T(8,128)S(1)} %get-tuple-element.317) | copy-start | bytes 61444
  154.3 17.8 %copy-start.158 = (f32[40,128]{1,0:T(8,128)}, f32[40,128]{1,0:T(8,128)S(1)}, u32[]{:S(2)}) copy-start(f32[40,128]{1,0:T(8,128)S(1)} %get-tuple-element.318) | copy-start | bytes 61444
  154.3 17.8 %copy-start.159 = (f32[40,128]{1,0:T(8,128)}, f32[40,128]{1,0:T(8,128)S(1)}, u32[]{:S(2)}) copy-start(f32[40,128]{1,0:T(8,128)S(1)} %get-tuple-element.319) | copy-start | bytes 61444
  154.3 17.8 %copy-start.160 = (f32[40,128]{1,0:T(8,128)}, f32[40,128]{1,0:T(8,128)S(1)}, u32[]{:S(2)}) copy-start(f32[40,128]{1,0:T(8,128)S(1)} %get-tuple-element.320) | copy-start | bytes 61444
  154.3 17.8 %copy-start.161 = (f32[40,128]{1,0:T(8,128)}, f32[40,128]{1,0:T(8,128)S(1)}, u32[]{:S(2)}) copy-start(f32[40,128]{1,0:T(8,128)S(1)} %get-tuple-element.321) | copy-start | bytes 61444
  154.3 17.8 %copy-start.162 = (f32[40,128]{1,0:T(8,128)}, f32[40,128]{1,0:T(8,128)S(1)}, u32[]{:S(2)}) copy-start(f32[40,128]{1,0:T(8,128)S(1)} %get-tuple-element.322) | copy-start | bytes 61444
  154.3 17.8 %copy-start.163 = (f32[40,128]{1,0:T(8,128)}, f32[40,128]{1,0:T(8,128)S(1)}, u32[]{:S(2)}) copy-start(f32[40,128]{1,0:T(8,128)S(1)} %get-tuple-element.323) | copy-start | bytes 61444
  154.4 17.7 %copy-start.164 = (f32[40,128]{1,0:T(8,128)}, f32[40,128]{1,0:T(8,128)S(1)}, u32[]{:S(2)}) copy-start(f32[40,128]{1,0:T(8,128)S(1)} %get-tuple-element.276) | copy-start | bytes 61444
  154.4 17.7 %copy-start.165 = (f32[40,128]{1,0:T(8,128)}, f32[40,128]{1,0:T(8,128)S(1)}, u32[]{:S(2)}) copy-start(f32[40,128]{1,0:T(8,128)S(1)} %get-tuple-element.278) | copy-start | bytes 61444
  154.4 17.7 %copy-start.166 = (f32[40,128]{1,0:T(8,128)}, f32[40,128]{1,0:T(8,128)S(1)}, u32[]{:S(2)}) copy-start(f32[40,128]{1,0:T(8,128)S(1)} %get-tuple-element.280) | copy-start | bytes 61444
  154.4 17.7 %copy-start.167 = (f32[40,128]{1,0:T(8,128)}, f32[40,128]{1,0:T(8,128)S(1)}, u32[]{:S(2)}) copy-start(f32[40,128]{1,0:T(8,128)S(1)} %get-tuple-element.282) | copy-start | bytes 61444
  154.4 17.7 %copy-start.168 = (f32[40,128]{1,0:T(8,128)}, f32[40,128]{1,0:T(8,128)S(1)}, u32[]{:S(2)}) copy-start(f32[40,128]{1,0:T(8,128)S(1)} %get-tuple-element.284) | copy-start | bytes 61444
  154.4 17.7 %copy-start.169 = (f32[40,128]{1,0:T(8,128)}, f32[40,128]{1,0:T(8,128)S(1)}, u32[]{:S(2)}) copy-start(f32[40,128]{1,0:T(8,128)S(1)} %get-tuple-element.286) | copy-start | bytes 61444
  154.4 17.7 %copy-start.170 = (f32[40,128]{1,0:T(8,128)}, f32[40,128]{1,0:T(8,128)S(1)}, u32[]{:S(2)}) copy-start(f32[40,128]{1,0:T(8,128)S(1)} %get-tuple-element.288) | copy-start | bytes 61444
  154.4 17.7 %copy-start.171 = (f32[40,128]{1,0:T(8,128)}, f32[40,128]{1,0:T(8,128)S(1)}, u32[]{:S(2)}) copy-start(f32[40,128]{1,0:T(8,128)S(1)} %get-tuple-element.290) | copy-start | bytes 61444
  154.4 17.7 %copy-start.172 = (f32[40,128]{1,0:T(8,128)}, f32[40,128]{1,0:T(8,128)S(1)}, u32[]{:S(2)}) copy-start(f32[40,128]{1,0:T(8,128)S(1)} %get-tuple-element.291) | copy-start | bytes 61444
  154.4 17.7 %copy-start.173 = (f32[40,128]{1,0:T(8,128)}, f32[40,128]{1,0:T(8,128)S(1)}, u32[]{:S(2)}) copy-start(f32[40,128]{1,0:T(8,128)S(1)} %get-tuple-element.292) | copy-start | bytes 61444
  154.5 17.7 %copy-start.174 = (f32[40,128]{1,0:T(8,128)}, f32[40,128]{1,0:T(8,128)S(1)}, u32[]{:S(2)}) copy-start(f32[40,128]{1,0:T(8,128)S(1)} %get-tuple-element.293) | copy-start | bytes 61444
  154.5 17.7 %copy-start.175 = (f32[40,128]{1,0:T(8,128)}, f32[40,128]{1,0:T(8,128)S(1)}, u32[]{:S(2)}) copy-start(f32[40,128]{1,0:T(8,128)S(1)} %get-tuple-element.294) | copy-start | bytes 61444
  197.4 49.4 %copy-start.135 = (f32[40,128]{1,0:T(8,128)S(1)}, f32[40,128]{1,0:T(8,128)}, u32[]{:S(2)}) copy-start(f32[40,128]{1,0:T(8,128)} %copy-done.134) | copy-start | bytes 61444
  197.4 49.4 %copy-start.139 = (f32[40,128]{1,0:T(8,128)S(1)}, f32[40,128]{1,0:T(8,128)}, u32[]{:S(2)}) copy-start(f32[40,128]{1,0:T(8,128)} %copy-done.138) | copy-start | bytes 61444
  197.4 49.4 %copy-start.143 = (f32[40,128]{1,0:T(8,128)S(1)}, f32[40,128]{1,0:T(8,128)}, u32[]{:S(2)}) copy-start(f32[40,128]{1,0:T(8,128)} %copy-done.142) | copy-start | bytes 61444
  197.4 49.4 %copy-start.147 = (f32[40,128]{1,0:T(8,128)S(1)}, f32[40,128]{1,0:T(8,128)}, u32[]{:S(2)}) copy-start(f32[40,128]{1,0:T(8,128)} %copy-done.146) | copy-start | bytes 61444
  197.4 49.4 %copy-start.150 = (f32[40,128]{1,0:T(8,128)S(1)}, f32[40,128]{1,0:T(8,128)}, u32[]{:S(2)}) copy-start(f32[40,128]{1,0:T(8,128)} %copy-done.149) | copy-start | bytes 61444
  197.4 49.4 %copy-start.153 = (f32[40,128]{1,0:T(8,128)S(1)}, f32[40,128]{1,0:T(8,128)}, u32[]{:S(2)}) copy-start(f32[40,128]{1,0:T(8,128)} %copy-done.152) | copy-start | bytes 61444
  338.6 14.1 %all-to-all-start.2 = ((f32[128,1,33]{2,1,0:T(1,128)}), f32[128,1,33]{2,1,0:T(1,128)S(1)}, u32[]{:S(2)}, u32[]{:S(2)}) async-start(f32[128,1,33]{2,1,0:T(1,128)} %bitcast.2310), calls=%async_computation.2 | async-start | bytes 131072 | tf_op jit(solution)/shard_map/all_to_all | solution.py:225
  343.4 105.1 %all-gather.22.cloned.1.call-start = ((), (), s32[]{:S(2)}) async-start(), calls=%async_computation.7 | async-start | bytes 1392640 | tf_op jit(solution)/shard_map/all_gather | solution.py:130
  402.3 46.2 %copy-start.136 = (f32[40,128]{1,0:T(8,128)S(1)}, f32[40,128]{1,0:T(8,128)}, u32[]{:S(2)}) copy-start(f32[40,128]{1,0:T(8,128)} %copy-done.134) | copy-start | bytes 61444
  402.3 46.2 %copy-start.140 = (f32[40,128]{1,0:T(8,128)S(1)}, f32[40,128]{1,0:T(8,128)}, u32[]{:S(2)}) copy-start(f32[40,128]{1,0:T(8,128)} %copy-done.138) | copy-start | bytes 61444
  402.3 46.2 %copy-start.144 = (f32[40,128]{1,0:T(8,128)S(1)}, f32[40,128]{1,0:T(8,128)}, u32[]{:S(2)}) copy-start(f32[40,128]{1,0:T(8,128)} %copy-done.142) | copy-start | bytes 61444
  408.8 110.7 %all-gather.24.cloned.1.call-start = ((), (), s32[]{:S(2)}) async-start(), calls=%async_computation.8 | async-start | bytes 1392640 | tf_op jit(solution)/shard_map/all_gather | solution.py:130
  554.7 14.0 %copy-start.105 = (f32[40,8,127]{0,1,2:T(8,128)S(1)}, f32[40,8,127]{0,1,2:T(8,128)}, u32[]{:S(2)}) copy-start(f32[40,8,127]{0,1,2:T(8,128)} %copy.751) | copy-start | bytes 487684
  619.1 14.1 %all-to-all-start.4 = ((f32[128,1,33]{2,1,0:T(1,128)}), f32[128,1,33]{2,1,0:T(1,128)S(1)}, u32[]{:S(2)}, u32[]{:S(2)}) async-start(f32[128,1,33]{2,1,0:T(1,128)} %bitcast.377), calls=%async_computation.4 | async-start | bytes 131072 | tf_op jit(solution)/shard_map/all_to_all | solution.py:225
  623.9 101.8 %all-gather.26.cloned.1.call-start = ((), (), s32[]{:S(2)}) async-start(), calls=%async_computation.9 | async-start | bytes 1392640 | tf_op jit(solution)/shard_map/all_gather | solution.py:130
  683.0 42.7 %copy-start.137 = (f32[40,128]{1,0:T(8,128)S(1)}, f32[40,128]{1,0:T(8,128)}, u32[]{:S(2)}) copy-start(f32[40,128]{1,0:T(8,128)} %copy-done.134) | copy-start | bytes 61444
  683.0 42.7 %copy-start.141 = (f32[40,128]{1,0:T(8,128)S(1)}, f32[40,128]{1,0:T(8,128)}, u32[]{:S(2)}) copy-start(f32[40,128]{1,0:T(8,128)} %copy-done.138) | copy-start | bytes 61444
  683.0 42.7 %copy-start.145 = (f32[40,128]{1,0:T(8,128)S(1)}, f32[40,128]{1,0:T(8,128)}, u32[]{:S(2)}) copy-start(f32[40,128]{1,0:T(8,128)} %copy-done.142) | copy-start | bytes 61444
  683.0 42.7 %copy-start.148 = (f32[40,128]{1,0:T(8,128)S(1)}, f32[40,128]{1,0:T(8,128)}, u32[]{:S(2)}) copy-start(f32[40,128]{1,0:T(8,128)} %copy-done.146) | copy-start | bytes 61444
  683.0 42.7 %copy-start.151 = (f32[40,128]{1,0:T(8,128)S(1)}, f32[40,128]{1,0:T(8,128)}, u32[]{:S(2)}) copy-start(f32[40,128]{1,0:T(8,128)} %copy-done.149) | copy-start | bytes 61444
  683.0 42.7 %copy-start.154 = (f32[40,128]{1,0:T(8,128)S(1)}, f32[40,128]{1,0:T(8,128)}, u32[]{:S(2)}) copy-start(f32[40,128]{1,0:T(8,128)} %copy-done.152) | copy-start | bytes 61444
  (269 other events, 1767.6 us)
Sparse Core Ops, SparseCore 0:
  124.9 44.5 all-gather.17
  204.1 42.6 all-gather.19
  409.0 39.4 all-gather.21
  476.9 42.6 all-gather.23
  686.1 39.4 all-gather.25

commit v4 on v2

--- a/solution.py
+++ b/solution.py
@@ -89,9 +89,12 @@
         first = total / (1.0 - product)
     else:
         first = jnp.zeros_like(offsets[0])
+    place = lax.axis_index(axis_name)
     entering = [first]
+    mine_in = first
     for k in range(count - 1):
         entering.append(offsets[k] + factors[k] * entering[k])
+        mine_in = jnp.where(place > k, entering[k + 1], mine_in)
     back_totals = [back_parts[k] + entering[k] * back_gains[k] for k in range(count)]
     if periodic:
         total = back_totals[count - 1]
@@ -99,16 +102,13 @@
         for k in range(count - 2, -1, -1):
             total = back_totals[k] + back_factors[k] * total
             product = product * back_factors[k]
-        last = total / (1.0 - product)
+        leaving = total / (1.0 - product)
     else:
-        last = jnp.zeros_like(offsets[0])
-    leaving = [None] * count
-    leaving[count - 1] = last
+        leaving = jnp.zeros_like(offsets[0])
+    mine_out = leaving
     for k in range(count - 2, -1, -1):
-        leaving[k] = back_totals[k + 1] + back_factors[k + 1] * leaving[k + 1]
-    place = lax.axis_index(axis_name)
-    mine_in = lax.dynamic_index_in_dim(jnp.stack(entering), place, 0, False)
-    mine_out = lax.dynamic_index_in_dim(jnp.stack(leaving), place, 0, False)
+        leaving = back_totals[k + 1] + back_factors[k + 1] * leaving
+        mine_out = jnp.where(place <= k, leaving, mine_out)
     return mine_in, mine_out
 
 

time: 706 us -> 790 us (1.12)
  local copies, waits for them, and re-layouts: 163 us -> 244 us
  blocking collectives: 136 us -> 164 us
  waiting for transfers between devices: 183 us -> 169 us
  starting transfers between devices: 22 us -> 12.1 us
    unnamed x564 -> x790, local copies, waits for them, and re-layouts: 33.6 us -> 97.1 us
    all_to_all x2 -> x4, blocking collectives: 33.2 us -> 60.8 us  [exchange(): lax.all_to_all(packed, ('gx', 'gy'), split_axis=0, concat_axis=0, tiled=T...]
    select_n x0 -> x20, other arithmetic: none -> 19.6 us  [the longest x10 11.7 us: carries(): mine_out = jnp.where(place <= k, leaving, mine_out)]
    unnamed x56 -> x1, other arithmetic: 19.2 us -> 1.32 us
    all_to_all x2 -> x0, waiting for transfers between devices: 17.3 us -> none  [exchange(): lax.all_to_all(packed, ('gx', 'gy'), split_axis=0, concat_axis=0, tiled=T...]
    mul x7 -> x17, local copies, waits for them, and re-layouts: 1.46 us -> 13.9 us  [the longest x7 8.11 us: carries(): leaving = back_totals[k + 1] + back_factors[k + 1] * leaving]
    all_to_all x2 -> x0, starting transfers between devices: 9.87 us -> none  [exchange(): lax.all_to_all(packed, ('gx', 'gy'), split_axis=0, concat_axis=0, tiled=T...]
    mul x1 -> x8, local copies, waits for them, and re-layouts: 0.73 us -> 9.68 us  [carries(): entering[k] * back_gains[k]]
  transfers between devices with their start and end apart: 8 -> 6, of which waited for: 7 -> 5; matrix products, arithmetic and copies ran while one was open for 4% -> 6% of each run, Pallas kernels for 0% -> 0%
where the time goes in v4:
time: 790 us; the launch traced here: 776 us
  local copies, waits for them, and re-layouts  244 us (31%)
  waiting for transfers between devices  169 us (21%)
  blocking collectives  164 us (21%)
  other arithmetic  143 us (18%)
  between operations  27.2 us (3%)
  matrix products  17 us (2%)
  starting transfers between devices  12.1 us (2%)
    all_gather x5, waiting for transfers between devices, line_operator(): got = lax.all_gather(mine, plan['axis_name'])  169 us
    unnamed x790, local copies, waits for them, and re-layouts  97.1 us
    gather x2, local copies, waits for them, and re-layouts, observe(): jnp.take(vector.reshape(-1), cell_index.reshape(-1), axis=0)  81.4 us
    scatter-add x3, other arithmetic, deposit_local(): flat_cells = jnp.zeros((TR * rate_x.size,), jnp.float32).at[cell_index.re...  67 us
    all_gather x5, blocking collectives, line_operator(): got = lax.all_gather(mine, plan['axis_name'])  64.9 us
    all_to_all x4, blocking collectives, exchange(): lax.all_to_all(packed, ('gx', 'gy'), split_axis=0, concat_axis=0, tiled=T...  60.8 us
    all_gather x2, blocking collectives, make_plan(): lax.all_gather(totals, axis_name)  38.7 us
    dot_general x3, matrix products, weigh_obs(): jnp.einsum('nij,nj->ni', blocks, packed, precision=lax.Precision.HIGHEST)  17 us
  transfers between devices with their start and end apart: 6, of which 5 were waited for; matrix products, arithmetic and copies ran while one was open for 6% of the time, Pallas kernels for 0%

profile of v4, /device:TPU:0, one launch (start us, length us, event | category | flops | bytes accessed | tf_op | source)
XLA Modules:
  0.0 776.5 jit_solution(5231210458762329931)
XLA Ops:
  10.3 5.7 fusion.4
  16.8 11.7 %all-to-all-start = ((f32[128,1,32]{2,1,0:T(1,128)}), f32[128,1,32]{2,1,0:T(1,128)}, u32[]{:S(2)}, u32[]{:S(2)}) async-start(f32[128,1,32]{2,1,0:T(1,128)} %bitcast.5), calls=%async_computation | async-start | bytes 131072 | tf_op jit(solution)/shard_map/all_to_all | solution.py:191
  33.8 12.7 %all-gather.1 = f32[24,1,40,8]{2,3,1,0:T(8,128)S(1)} all-gather(f32[3,1,40,8]{2,3,1,0:T(8,128)S(1)} %pad_maximum_fusion.11), channel_id=3, replica_groups=mesh['gx'=16,'gy'=8] {'gy'}, dimensions={0}, use_global_device_ids=true | all-gather | bytes 34560 | tf_op jit(solution)/shard_map/all_gather | solution.py:69
  51.6 1.7 multiply_add_fusion.93
  53.3 1.6 pad_bitcast_fusion.1
  76.3 1.7 slice.2242
  80.3 2.3 reduce.11
  82.5 1.5 reshape.3312
  84.1 22.7 %scatter_custom_fusion = f32[81920]{0:T(1024)} fusion(s32[4096]{0:T(1024)} %bitcast.2067, f32[4096]{0:T(1024)} %reshape.3312, f32[]{:T(128)} %constant.30.clone.1), kind=kCustom, calls=%fused_computation.201 | custom fusion | flops 4096 | bytes 328192 | tf_op jit(solution)/shard_map/scatter-add | solution.py:181
  114.2 1.7 copy.1228
  116.6 13.2 %all-gather = f32[16,2,40,8]{2,3,1,0:T(8,128)S(1)} all-gather(f32[2,2,40,8]{2,3,1,0:T(8,128)S(1)} %pad_maximum_fusion.6), channel_id=2, replica_groups=mesh['gx'=16,'gy'=8] {'gy'}, dimensions={0}, use_global_device_ids=true | all-gather | bytes 46080 | tf_op jit(solution)/shard_map/all_gather | solution.py:128
  130.5 1.4 copy.1404
  131.9 1.4 copy.1405
  137.5 1.4 copy.1409
  140.3 1.4 copy.1411
  141.7 1.4 copy.1412
  145.9 1.4 copy.1415
  158.7 26.0 %all-gather.3 = f32[48,1,40,128]{3,2,1,0:T(8,128)S(1)} all-gather(f32[3,1,40,128]{3,2,1,0:T(8,128)S(1)} %pad_maximum_fusion.5), channel_id=5, replica_groups=mesh['gx'=16,'gy'=8] {'gx'}, dimensions={0}, use_global_device_ids=true | all-gather | bytes 1044480 | tf_op jit(solution)/shard_map/all_gather | solution.py:69
  187.6 13.2 %all-gather.18.cloned.1.call-done = f32[32,2,40,128]{3,2,1,0:T(8,128)} async-done(((f32[2,2,40,128]{3,2,1,0:T(8,128)}), f32[32,2,40,128]{3,2,1,0:T(8,128)}) %all-gather.18.cloned.1.call-update) | async-done | bytes 1310736 | tf_op jit(solution)/shard_map/all_gather | solution.py:128
  201.2 1.5 select_select_fusion.13
  209.9 1.5 reshape_squeeze.10
  212.8 39.9 %all-gather.20.cloned.1.call-done = f32[32,2,40,128]{3,2,1,0:T(8,128)} async-done(((f32[2,2,40,128]{3,2,1,0:T(8,128)}), f32[32,2,40,128]{3,2,1,0:T(8,128)}) %all-gather.20.cloned.1.call-update) | async-done | bytes 1310736 | tf_op jit(solution)/shard_map/all_gather | solution.py:128
  252.7 2.1 select_select_fusion.10
  261.7 1.7 copy.1315
  264.1 13.0 %all-gather.5 = f32[16,2,40,8]{2,3,1,0:T(8,128)S(1)} all-gather(f32[2,2,40,8]{2,3,1,0:T(8,128)S(1)} %pad_maximum_fusion.7), channel_id=7, replica_groups=mesh['gx'=16,'gy'=8] {'gy'}, dimensions={0}, use_global_device_ids=true | all-gather | bytes 46080 | tf_op jit(solution)/shard_map/all_gather | solution.py:128
  277.8 1.4 copy.1421
  280.6 1.4 copy.1423
  284.8 1.4 copy.1426
  293.2 1.4 copy.1432
  301.0 40.7 %gather_fusion = f32[4096]{0:T(1024)} fusion(f32[81920]{0:T(1024)S(1)} %bitcast.1855, s32[4096]{0:T(1024)} %fusion.166), kind=kCustom, calls=%fused_computation.clone | custom fusion | bytes 49152 | tf_op jit(solution)/shard_map/jit(_take)/gather | solution.py:186
  343.7 16.4 %all_to_all.54 = f32[128,1,33]{2,1,0:T(1,128)S(1)} all-to-all(f32[128,1,33]{2,1,0:T(1,128)S(1)} %bitcast.2041), channel_id=1, replica_groups=mesh['gx'=16,'gy'=8] {'gx','gy'}, dimensions={0} | all-to-all | bytes 33792 | tf_op jit(solution)/shard_map/all_to_all | solution.py:144
  360.3 5.7 fusion.2
  368.0 13.9 %all_to_all.55 = f32[128,1,33]{2,1,0:T(1,128)S(1)} all-to-all(f32[128,1,33]{2,1,0:T(1,128)S(1)} %bitcast.2038), channel_id=1, replica_groups=mesh['gx'=16,'gy'=8] {'gx','gy'}, dimensions={0} | all-to-all | bytes 33792 | tf_op jit(solution)/shard_map/all_to_all | solution.py:144
  383.3 22.1 %scatter_custom_fusion.1 = f32[81920]{0:T(1024)S(1)} fusion(s32[4096]{0:T(1024)} %bitcast.2068, f32[4096]{0:T(1024)} %reshape.3320, f32[]{:T(128)} %constant.30.clone.1), kind=kCustom, calls=%fused_computation.199 | custom fusion | flops 4096 | bytes 328192 | tf_op jit(solution)/shard_map/scatter-add | solution.py:181
  409.2 1.7 copy.1333
  411.6 12.7 %all-gather.6 = f32[16,2,40,8]{2,3,1,0:T(8,128)S(1)} all-gather(f32[2,2,40,8]{2,3,1,0:T(8,128)S(1)} %pad_maximum_fusion.8), channel_id=8, replica_groups=mesh['gx'=16,'gy'=8] {'gy'}, dimensions={0}, use_global_device_ids=true | all-gather | bytes 46080 | tf_op jit(solution)/shard_map/all_gather | solution.py:128
  425.0 1.4 copy.1435
  427.8 1.4 copy.1437
  429.2 1.4 copy.1438
  430.6 1.4 copy.1439
  432.0 1.4 copy.1440
  437.6 1.4 copy.1444
  452.7 1.5 slice_reduce_fusion.3
  454.2 1.6 slice_reduce_fusion.2
  457.1 35.0 %all-gather.22.cloned.1.call-done = f32[32,2,40,128]{3,2,1,0:T(8,128)} async-done(((f32[2,2,40,128]{3,2,1,0:T(8,128)}), f32[32,2,40,128]{3,2,1,0:T(8,128)}) %all-gather.22.cloned.1.call-update) | async-done | bytes 1310736 | tf_op jit(solution)/shard_map/all_gather | solution.py:128
  493.5 2.2 select_select_fusion.6
  501.0 42.7 %all-gather.24.cloned.1.call-done = f32[32,2,40,128]{3,2,1,0:T(8,128)} async-done(((f32[2,2,40,128]{3,2,1,0:T(8,128)}), f32[32,2,40,128]{3,2,1,0:T(8,128)}) %all-gather.24.cloned.1.call-update) | async-done | bytes 1310736 | tf_op jit(solution)/shard_map/all_gather | solution.py:128
  543.7 2.1 select_select_fusion.4
  552.7 1.7 copy.1359
  555.1 13.0 %all-gather.9 = f32[16,2,40,8]{2,3,1,0:T(8,128)S(1)} all-gather(f32[2,2,40,8]{2,3,1,0:T(8,128)S(1)} %pad_maximum_fusion.9), channel_id=11, replica_groups=mesh['gx'=16,'gy'=8] {'gy'}, dimensions={0}, use_global_device_ids=true | all-gather | bytes 46080 | tf_op jit(solution)/shard_map/all_gather | solution.py:128
  573.0 1.4 copy.1458
  577.2 1.4 copy.1461
  580.0 1.4 copy.1463
  582.8 1.4 copy.1465
  585.6 1.4 copy.1467
  592.0 40.7 %gather_fusion.1 = f32[4096]{0:T(1024)} fusion(f32[81920]{0:T(1024)S(1)} %bitcast.1854, s32[4096]{0:T(1024)} %fusion.166), kind=kCustom, calls=%fused_computation.1.clone | custom fusion | bytes 49152 | tf_op jit(solution)/shard_map/jit(_take)/gather | solution.py:186
  634.1 16.4 %all_to_all.56 = f32[128,1,33]{2,1,0:T(1,128)S(1)} all-to-all(f32[128,1,33]{2,1,0:T(1,128)S(1)} %bitcast.2039), channel_id=1, replica_groups=mesh['gx'=16,'gy'=8] {'gx','gy'}, dimensions={0} | all-to-all | bytes 33792 | tf_op jit(solution)/shard_map/all_to_all | solution.py:144
  652.6 1.7 multiply_reduce_fusion
  655.3 5.7 fusion
  663.2 13.9 %all_to_all.57 = f32[128,1,33]{2,1,0:T(1,128)S(1)} all-to-all(f32[128,1,33]{2,1,0:T(1,128)S(1)} %bitcast.2040), channel_id=1, replica_groups=mesh['gx'=16,'gy'=8] {'gx','gy'}, dimensions={0} | all-to-all | bytes 33792 | tf_op jit(solution)/shard_map/all_to_all | solution.py:144
  678.4 22.1 %scatter_custom_fusion.2 = f32[81920]{0:T(1024)S(1)} fusion(s32[4096]{0:T(1024)} %bitcast.2069, f32[4096]{0:T(1024)} %reshape.3328, f32[]{:T(128)} %constant.30.clone.1), kind=kCustom, calls=%fused_computation.197 | custom fusion | flops 4096 | bytes 328192 | tf_op jit(solution)/shard_map/scatter-add | solution.py:181
  705.1 12.9 %all-gather.10 = f32[16,2,40,8]{2,3,1,0:T(8,128)S(1)} all-gather(f32[2,2,40,8]{2,3,1,0:T(8,128)S(1)} %pad_maximum_fusion.10), channel_id=12, replica_groups=mesh['gx'=16,'gy'=8] {'gy'}, dimensions={0}, use_global_device_ids=true | all-gather | bytes 46080 | tf_op jit(solution)/shard_map/all_gather | solution.py:128
  727.3 37.8 %all-gather.26.cloned.1.call-done = f32[32,2,40,128]{3,2,1,0:T(8,128)} async-done(((f32[2,2,40,128]{3,2,1,0:T(8,128)}), f32[32,2,40,128]{3,2,1,0:T(8,128)}) %all-gather.26.cloned.1.call-update) | async-done | bytes 1310736 | tf_op jit(solution)/shard_map/all_gather | solution.py:128
  765.3 1.8 select_select_fusion
  (1145 shorter events, 177.9 us)
Async XLA Ops:
  16.8 62.9 %all-to-all-start = ((f32[128,1,32]{2,1,0:T(1,128)}), f32[128,1,32]{2,1,0:T(1,128)}, u32[]{:S(2)}, u32[]{:S(2)}) async-start(f32[128,1,32]{2,1,0:T(1,128)} %bitcast.5), calls=%async_computation | async-start | bytes 131072 | tf_op jit(solution)/shard_map/all_to_all | solution.py:191
  28.5 172.3 %all-gather.18.cloned.1.call-start = ((), (), s32[]{:S(2)}) async-start(), calls=%async_computation.5 | async-start | bytes 1392640 | tf_op jit(solution)/shard_map/all_gather | solution.py:128
  29.9 123.5 %copy-start = (f32[1,40,8,128]{3,2,1,0:T(8,128)}, f32[1,40,8,128]{3,2,1,0:T(8,128)S(1)}, u32[]{:S(2)}) copy-start(f32[1,40,8,128]{3,2,1,0:T(8,128)S(1)} %get-tuple-element.50) | copy-start | bytes 491524
  48.8 206.4 %copy-start.6 = (f32[1,40,8,128]{3,2,1,0:T(8,128)}, f32[1,40,8,128]{3,2,1,0:T(8,128)S(1)}, u32[]{:S(2)}) copy-start(f32[1,40,8,128]{3,2,1,0:T(8,128)S(1)} %get-tuple-element.34) | copy-start | bytes 491524
  53.3 155.1 %copy-start.3 = (f32[1,40,8,128]{3,2,1,0:T(8,128)}, f32[1,40,8,128]{3,2,1,0:T(8,128)S(1)}, u32[]{:S(2)}) copy-start(f32[1,40,8,128]{3,2,1,0:T(8,128)S(1)} %get-tuple-element.30) | copy-start | bytes 491524
  55.0 97.1 %copy-start.119 = (f32[40,8]{1,0:T(8,128)}, f32[40,8]{1,0:T(8,128)S(1)}, u32[]{:S(2)}) copy-start(f32[40,8]{1,0:T(8,128)S(1)} %copy.1238) | copy-start | bytes 3844
  55.1 97.0 %copy-start.124 = (f32[40,8]{1,0:T(8,128)}, f32[40,8]{1,0:T(8,128)S(1)}, u32[]{:S(2)}) copy-start(f32[40,8]{1,0:T(8,128)S(1)} %copy.1240) | copy-start | bytes 3844
  55.1 96.9 %copy-start.129 = (f32[40,8]{1,0:T(8,128)}, f32[40,8]{1,0:T(8,128)S(1)}, u32[]{:S(2)}) copy-start(f32[40,8]{1,0:T(8,128)S(1)} %copy.1242) | copy-start | bytes 3844
  55.2 96.8 %copy-start.134 = (f32[40,8]{1,0:T(8,128)}, f32[40,8]{1,0:T(8,128)S(1)}, u32[]{:S(2)}) copy-start(f32[40,8]{1,0:T(8,128)S(1)} %copy.1244) | copy-start | bytes 3844
  56.0 96.1 %copy-start.139 = (f32[40,8]{1,0:T(8,128)}, f32[40,8]{1,0:T(8,128)S(1)}, u32[]{:S(2)}) copy-start(f32[40,8]{1,0:T(8,128)S(1)} %copy.1246) | copy-start | bytes 3844
  79.7 74.8 %copy-start.11 = (f32[40,8,128]{2,0,1:T(8,128)}, f32[40,8,128]{2,0,1:T(8,128)S(1)}, u32[]{:S(2)}) copy-start(f32[40,8,128]{2,0,1:T(8,128)S(1)} %copy.1271) | copy-start | bytes 491524
  156.3 96.4 %all-gather.20.cloned.1.call-start = ((), (), s32[]{:S(2)}) async-start(), calls=%async_computation.6 | async-start | bytes 1392640 | tf_op jit(solution)/shard_map/all_gather | solution.py:128
  158.0 44.7 %copy-start.27 = (f32[40,7,128]{2,1,0:T(8,128)}, f32[40,7,128]{2,1,0:T(8,128)S(1)}, u32[]{:S(2)}) copy-start(f32[40,7,128]{2,1,0:T(8,128)S(1)} %slice.2318) | copy-start | bytes 430084
  209.8 45.0 %copy-start.64 = (f32[40,128]{1,0:T(8,128)S(1)}, f32[40,128]{1,0:T(8,128)}, u32[]{:S(2)}) copy-start(f32[40,128]{1,0:T(8,128)} %copy-done.63) | copy-start | bytes 61444
  209.8 45.0 %copy-start.69 = (f32[40,128]{1,0:T(8,128)S(1)}, f32[40,128]{1,0:T(8,128)}, u32[]{:S(2)}) copy-start(f32[40,128]{1,0:T(8,128)} %copy-done.68) | copy-start | bytes 61444
  209.8 45.0 %copy-start.74 = (f32[40,128]{1,0:T(8,128)S(1)}, f32[40,128]{1,0:T(8,128)}, u32[]{:S(2)}) copy-start(f32[40,128]{1,0:T(8,128)} %copy-done.73) | copy-start | bytes 61444
  209.8 45.0 %copy-start.79 = (f32[40,128]{1,0:T(8,128)S(1)}, f32[40,128]{1,0:T(8,128)}, u32[]{:S(2)}) copy-start(f32[40,128]{1,0:T(8,128)} %copy-done.78) | copy-start | bytes 61444
  209.8 45.0 %copy-start.84 = (f32[40,128]{1,0:T(8,128)S(1)}, f32[40,128]{1,0:T(8,128)}, u32[]{:S(2)}) copy-start(f32[40,128]{1,0:T(8,128)} %copy-done.83) | copy-start | bytes 61444
  209.8 45.0 %copy-start.89 = (f32[40,128]{1,0:T(8,128)S(1)}, f32[40,128]{1,0:T(8,128)}, u32[]{:S(2)}) copy-start(f32[40,128]{1,0:T(8,128)} %copy-done.88) | copy-start | bytes 61444
  209.8 45.0 %copy-start.94 = (f32[40,128]{1,0:T(8,128)S(1)}, f32[40,128]{1,0:T(8,128)}, u32[]{:S(2)}) copy-start(f32[40,128]{1,0:T(8,128)} %copy-done.93) | copy-start | bytes 61444
  209.8 45.0 %copy-start.99 = (f32[40,128]{1,0:T(8,128)S(1)}, f32[40,128]{1,0:T(8,128)}, u32[]{:S(2)}) copy-start(f32[40,128]{1,0:T(8,128)} %copy-done.98) | copy-start | bytes 61444
  209.9 282.2 %all-gather.22.cloned.1.call-start = ((), (), s32[]{:S(2)}) async-start(), calls=%async_computation.7 | async-start | bytes 1392640 | tf_op jit(solution)/shard_map/all_gather | solution.py:128
  301.0 59.1 %copy-start.351 = (s32[1,128]{1,0:T(1,128)S(1)}, s32[1,128]{1,0:T(1,128)}, u32[]{:S(2)}) copy-start(s32[1,128]{1,0:T(1,128)} %param.13) | copy-start | bytes 1540
  450.1 42.0 %copy-start.65 = (f32[40,128]{1,0:T(8,128)S(1)}, f32[40,128]{1,0:T(8,128)}, u32[]{:S(2)}) copy-start(f32[40,128]{1,0:T(8,128)} %copy-done.63) | copy-start | bytes 61444
  450.1 42.0 %copy-start.70 = (f32[40,128]{1,0:T(8,128)S(1)}, f32[40,128]{1,0:T(8,128)}, u32[]{:S(2)}) copy-start(f32[40,128]{1,0:T(8,128)} %copy-done.68) | copy-start | bytes 61444
  450.1 42.0 %copy-start.75 = (f32[40,128]{1,0:T(8,128)S(1)}, f32[40,128]{1,0:T(8,128)}, u32[]{:S(2)}) copy-start(f32[40,128]{1,0:T(8,128)} %copy-done.73) | copy-start | bytes 61444
  450.1 42.0 %copy-start.80 = (f32[40,128]{1,0:T(8,128)S(1)}, f32[40,128]{1,0:T(8,128)}, u32[]{:S(2)}) copy-start(f32[40,128]{1,0:T(8,128)} %copy-done.78) | copy-start | bytes 61444
  450.1 42.0 %copy-start.85 = (f32[40,128]{1,0:T(8,128)S(1)}, f32[40,128]{1,0:T(8,128)}, u32[]{:S(2)}) copy-start(f32[40,128]{1,0:T(8,128)} %copy-done.83) | copy-start | bytes 61444
  450.1 42.0 %copy-start.90 = (f32[40,128]{1,0:T(8,128)S(1)}, f32[40,128]{1,0:T(8,128)}, u32[]{:S(2)}) copy-start(f32[40,128]{1,0:T(8,128)} %copy-done.88) | copy-start | bytes 61444
  450.2 42.0 %copy-start.95 = (f32[40,128]{1,0:T(8,128)S(1)}, f32[40,128]{1,0:T(8,128)}, u32[]{:S(2)}) copy-start(f32[40,128]{1,0:T(8,128)} %copy-done.93) | copy-start | bytes 61444
  450.2 42.0 %copy-start.100 = (f32[40,128]{1,0:T(8,128)S(1)}, f32[40,128]{1,0:T(8,128)}, u32[]{:S(2)}) copy-start(f32[40,128]{1,0:T(8,128)} %copy-done.98) | copy-start | bytes 61444
  452.4 91.3 %all-gather.24.cloned.1.call-start = ((), (), s32[]{:S(2)}) async-start(), calls=%async_computation.8 | async-start | bytes 1392640 | tf_op jit(solution)/shard_map/all_gather | solution.py:128
  500.2 45.6 %copy-start.66 = (f32[40,128]{1,0:T(8,128)S(1)}, f32[40,128]{1,0:T(8,128)}, u32[]{:S(2)}) copy-start(f32[40,128]{1,0:T(8,128)} %copy-done.63) | copy-start | bytes 61444
  500.2 45.6 %copy-start.71 = (f32[40,128]{1,0:T(8,128)S(1)}, f32[40,128]{1,0:T(8,128)}, u32[]{:S(2)}) copy-start(f32[40,128]{1,0:T(8,128)} %copy-done.68) | copy-start | bytes 61444
  500.2 45.6 %copy-start.76 = (f32[40,128]{1,0:T(8,128)S(1)}, f32[40,128]{1,0:T(8,128)}, u32[]{:S(2)}) copy-start(f32[40,128]{1,0:T(8,128)} %copy-done.73) | copy-start | bytes 61444
  500.2 45.7 %copy-start.81 = (f32[40,128]{1,0:T(8,128)S(1)}, f32[40,128]{1,0:T(8,128)}, u32[]{:S(2)}) copy-start(f32[40,128]{1,0:T(8,128)} %copy-done.78) | copy-start | bytes 61444
  500.3 45.7 %copy-start.86 = (f32[40,128]{1,0:T(8,128)S(1)}, f32[40,128]{1,0:T(8,128)}, u32[]{:S(2)}) copy-start(f32[40,128]{1,0:T(8,128)} %copy-done.83) | copy-start | bytes 61444
  500.3 45.7 %copy-start.91 = (f32[40,128]{1,0:T(8,128)S(1)}, f32[40,128]{1,0:T(8,128)}, u32[]{:S(2)}) copy-start(f32[40,128]{1,0:T(8,128)} %copy-done.88) | copy-start | bytes 61444
  500.3 45.7 %copy-start.96 = (f32[40,128]{1,0:T(8,128)S(1)}, f32[40,128]{1,0:T(8,128)}, u32[]{:S(2)}) copy-start(f32[40,128]{1,0:T(8,128)} %copy-done.93) | copy-start | bytes 61444
  500.3 45.7 %copy-start.101 = (f32[40,128]{1,0:T(8,128)S(1)}, f32[40,128]{1,0:T(8,128)}, u32[]{:S(2)}) copy-start(f32[40,128]{1,0:T(8,128)} %copy-done.98) | copy-start | bytes 61444
  500.9 264.1 %all-gather.26.cloned.1.call-start = ((), (), s32[]{:S(2)}) async-start(), calls=%async_computation.9 | async-start | bytes 1392640 | tf_op jit(solution)/shard_map/all_gather | solution.py:128
  592.0 62.3 %copy-start.352 = (s32[1,128]{1,0:T(1,128)S(1)}, s32[1,128]{1,0:T(1,128)}, u32[]{:S(2)}) copy-start(s32[1,128]{1,0:T(1,128)} %param.13) | copy-start | bytes 1540
  723.7 41.4 %copy-start.67 = (f32[40,128]{1,0:T(8,128)S(1)}, f32[40,128]{1,0:T(8,128)}, u32[]{:S(2)}) copy-start(f32[40,128]{1,0:T(8,128)} %copy-done.63) | copy-start | bytes 61444
  723.7 41.4 %copy-start.72 = (f32[40,128]{1,0:T(8,128)S(1)}, f32[40,128]{1,0:T(8,128)}, u32[]{:S(2)}) copy-start(f32[40,128]{1,0:T(8,128)} %copy-done.68) | copy-start | bytes 61444
  723.7 41.4 %copy-start.77 = (f32[40,128]{1,0:T(8,128)S(1)}, f32[40,128]{1,0:T(8,128)}, u32[]{:S(2)}) copy-start(f32[40,128]{1,0:T(8,128)} %copy-done.73) | copy-start | bytes 61444
  723.7 41.4 %copy-start.82 = (f32[40,128]{1,0:T(8,128)S(1)}, f32[40,128]{1,0:T(8,128)}, u32[]{:S(2)}) copy-start(f32[40,128]{1,0:T(8,128)} %copy-done.78) | copy-start | bytes 61444
  723.7 41.4 %copy-start.87 = (f32[40,128]{1,0:T(8,128)S(1)}, f32[40,128]{1,0:T(8,128)}, u32[]{:S(2)}) copy-start(f32[40,128]{1,0:T(8,128)} %copy-done.83) | copy-start | bytes 61444
  723.7 41.4 %copy-start.92 = (f32[40,128]{1,0:T(8,128)S(1)}, f32[40,128]{1,0:T(8,128)}, u32[]{:S(2)}) copy-start(f32[40,128]{1,0:T(8,128)} %copy-done.88) | copy-start | bytes 61444
  723.7 41.4 %copy-start.97 = (f32[40,128]{1,0:T(8,128)S(1)}, f32[40,128]{1,0:T(8,128)}, u32[]{:S(2)}) copy-start(f32[40,128]{1,0:T(8,128)} %copy-done.93) | copy-start | bytes 61444
  723.7 41.4 %copy-start.102 = (f32[40,128]{1,0:T(8,128)S(1)}, f32[40,128]{1,0:T(8,128)}, u32[]{:S(2)}) copy-start(f32[40,128]{1,0:T(8,128)} %copy-done.98) | copy-start | bytes 61444
  723.7 41.4 %copy-start.106 = (f32[40,128]{1,0:T(8,128)S(1)}, f32[40,128]{1,0:T(8,128)}, u32[]{:S(2)}) copy-start(f32[40,128]{1,0:T(8,128)} %get-tuple-element.80) | copy-start | bytes 61444
  723.8 41.4 %copy-start.110 = (f32[40,128]{1,0:T(8,128)S(1)}, f32[40,128]{1,0:T(8,128)}, u32[]{:S(2)}) copy-start(f32[40,128]{1,0:T(8,128)} %get-tuple-element.81) | copy-start | bytes 61444
  723.8 41.4 %copy-start.114 = (f32[40,128]{1,0:T(8,128)S(1)}, f32[40,128]{1,0:T(8,128)}, u32[]{:S(2)}) copy-start(f32[40,128]{1,0:T(8,128)} %get-tuple-element.82) | copy-start | bytes 61444
  723.8 41.4 %copy-start.118 = (f32[40,128]{1,0:T(8,128)S(1)}, f32[40,128]{1,0:T(8,128)}, u32[]{:S(2)}) copy-start(f32[40,128]{1,0:T(8,128)} %get-tuple-element.83) | copy-start | bytes 61444
  723.8 41.4 %copy-start.171 = (f32[40,128]{1,0:T(8,128)S(1)}, f32[40,128]{1,0:T(8,128)}, u32[]{:S(2)}) copy-start(f32[40,128]{1,0:T(8,128)} %get-tuple-element.84) | copy-start | bytes 61444
  723.8 41.4 %copy-start.173 = (f32[40,128]{1,0:T(8,128)S(1)}, f32[40,128]{1,0:T(8,128)}, u32[]{:S(2)}) copy-start(f32[40,128]{1,0:T(8,128)} %get-tuple-element.85) | copy-start | bytes 61444
  723.8 41.4 %copy-start.175 = (f32[40,128]{1,0:T(8,128)S(1)}, f32[40,128]{1,0:T(8,128)}, u32[]{:S(2)}) copy-start(f32[40,128]{1,0:T(8,128)} %get-tuple-element.86) | copy-start | bytes 61444
  723.8 41.4 %copy-start.177 = (f32[40,128]{1,0:T(8,128)S(1)}, f32[40,128]{1,0:T(8,128)}, u32[]{:S(2)}) copy-start(f32[40,128]{1,0:T(8,128)} %get-tuple-element.87) | copy-start | bytes 61444
  723.8 41.4 %copy-start.179 = (f32[40,128]{1,0:T(8,128)S(1)}, f32[40,128]{1,0:T(8,128)}, u32[]{:S(2)}) copy-start(f32[40,128]{1,0:T(8,128)} %get-tuple-element.88) | copy-start | bytes 61444
  723.8 41.4 %copy-start.181 = (f32[40,128]{1,0:T(8,128)S(1)}, f32[40,128]{1,0:T(8,128)}, u32[]{:S(2)}) copy-start(f32[40,128]{1,0:T(8,128)} %get-tuple-element.89) | copy-start | bytes 61444
  723.8 41.4 %copy-start.183 = (f32[40,128]{1,0:T(8,128)S(1)}, f32[40,128]{1,0:T(8,128)}, u32[]{:S(2)}) copy-start(f32[40,128]{1,0:T(8,128)} %get-tuple-element.90) | copy-start | bytes 61444
  723.9 41.4 %copy-start.185 = (f32[40,128]{1,0:T(8,128)S(1)}, f32[40,128]{1,0:T(8,128)}, u32[]{:S(2)}) copy-start(f32[40,128]{1,0:T(8,128)} %get-tuple-element.91) | copy-start | bytes 61444
  723.9 41.4 %copy-start.187 = (f32[40,128]{1,0:T(8,128)S(1)}, f32[40,128]{1,0:T(8,128)}, u32[]{:S(2)}) copy-start(f32[40,128]{1,0:T(8,128)} %get-tuple-element.92) | copy-start | bytes 61444
  723.9 41.4 %copy-start.189 = (f32[40,128]{1,0:T(8,128)S(1)}, f32[40,128]{1,0:T(8,128)}, u32[]{:S(2)}) copy-start(f32[40,128]{1,0:T(8,128)} %get-tuple-element.93) | copy-start | bytes 61444
  (295 other events, 2335.1 us)
Sparse Core Ops, SparseCore 0:
  156.4 44.4 all-gather.17
  210.0 42.6 all-gather.19
  452.5 39.4 all-gather.21
  501.1 42.6 all-gather.23
  725.5 39.4 all-gather.25

commit v5 on v3

--- a/solution.py
+++ b/solution.py
@@ -262,8 +262,12 @@
     lane_of = flat_index % lane_count
 
     def deposit_local(arrived):
-        cells = add_cells(arrived.reshape(1, -1), row_of, lane_of, field_rows, lane_count)
-        return cells.reshape(field_shape)
+        flat_cells = (
+            jnp.zeros((TR * rate_x.size,), jnp.float32)
+            .at[cell_index.reshape(-1)]
+            .add(arrived.reshape(-1))
+        )
+        return flat_cells.reshape(field_shape)
 
     def observe(vector):
         picked = pick_cells(vector.reshape(field_rows, lane_count), row_of, lane_of)

time: 759 us -> 686 us (0.904)
  local copies, waits for them, and re-layouts: 215 us -> 110 us
  other arithmetic: 101 us -> 167 us
  Pallas kernels: 35.5 us -> 13.4 us
  waiting for transfers between devices: 189 us -> 180 us
    unnamed x822 -> x466, local copies, waits for them, and re-layouts: 126 us -> 36.5 us
    scatter-add x0 -> x3, other arithmetic: none -> 68.2 us  [deposit_local(): flat_cells = jnp.zeros((TR * rate_x.size,), jnp.float32).at[cell_index.re...]
    pallas_call x3 -> x0, Pallas kernels: 22.1 us -> none  [add_cells(): pl.pallas_call(add_kernel, out_shape=jax.ShapeDtypeStruct((field_rows, la...]
    dynamic_slice x0 -> x20, local copies, waits for them, and re-layouts: none -> 15.8 us  [the longest x10 9.64 us: carries(): mine_in = lax.dynamic_index_in_dim(jnp.stack(entering), place, 0, False)]
    mul x16 -> x2, local copies, waits for them, and re-layouts: 14.8 us -> 1.64 us  [scan_offsets(): level_factor * shift_along(forcing, distance, line_axis, reverse, 0.0)]
    another operation x19 -> x1, local copies, waits for them, and re-layouts: 11.7 us -> 0.01 us  [line_operator(): jnp.stack([lax.index_in_dim(offset, length - 1, line_axis, keepdims=False...]
    all_gather x5, waiting for transfers between devices: 172 us -> 163 us  [line_operator(): got = lax.all_gather(mine, plan['axis_name'])]
    mul x19 -> x7, local copies, waits for them, and re-layouts: 11 us -> 2.4 us  [line_operator(): return plan['gain_out'] * (forward + next_offset + next_factor * leaving)]
where the time goes in v5:
time: 686 us; the launch traced here: 674 us
  waiting for transfers between devices  180 us (26%)
  other arithmetic  167 us (24%)
  blocking collectives  136 us (20%)
  local copies, waits for them, and re-layouts  110 us (16%)
  between operations  25.2 us (4%)
  starting transfers between devices  23.7 us (3%)
  matrix products  17 us (2%)
  Pallas kernels  13.4 us (2%)
    all_gather x5, waiting for transfers between devices, line_operator(): got = lax.all_gather(mine, plan['axis_name'])  163 us
    scatter-add x3, other arithmetic, deposit_local(): flat_cells = jnp.zeros((TR * rate_x.size,), jnp.float32).at[cell_index.re...  68.2 us
    all_gather x5, blocking collectives, line_operator(): got = lax.all_gather(mine, plan['axis_name'])  64.7 us
    all_gather x2, blocking collectives, make_plan(): lax.all_gather(totals, axis_name)  38.4 us
    unnamed x466, local copies, waits for them, and re-layouts  36.5 us
    all_to_all x2, blocking collectives, exchange(): lax.all_to_all(packed, ('gx', 'gy'), split_axis=0, concat_axis=0, tiled=T...  33.2 us
    unnamed x56, other arithmetic  22.4 us
    all_to_all x2, waiting for transfers between devices, exchange(): lax.all_to_all(packed, ('gx', 'gy'), split_axis=0, concat_axis=0, tiled=T...  17.3 us
  transfers between devices with their start and end apart: 8, of which 7 were waited for; matrix products, arithmetic and copies ran while one was open for 5% of the time, Pallas kernels for 0%

profile of v5, /device:TPU:0, one launch (start us, length us, event | category | flops | bytes accessed | tf_op | source)
XLA Modules:
  0.0 673.5 jit_solution(4804683499841112424)
XLA Ops:
  10.3 5.7 fusion.4
  16.8 11.7 %all-to-all-start = ((f32[128,1,32]{2,1,0:T(1,128)}), f32[128,1,32]{2,1,0:T(1,128)}, u32[]{:S(2)}, u32[]{:S(2)}) async-start(f32[128,1,32]{2,1,0:T(1,128)} %bitcast.5), calls=%async_computation | async-start | bytes 131072 | tf_op jit(solution)/shard_map/all_to_all | solution.py:277
  33.3 12.7 %all-gather.1 = f32[24,1,40,8]{2,3,1,0:T(8,128)S(1)} all-gather(f32[3,1,40,8]{2,3,1,0:T(8,128)S(1)} %pad_maximum_fusion.11), channel_id=3, replica_groups=mesh['gx'=16,'gy'=8] {'gy'}, dimensions={0}, use_global_device_ids=true | all-gather | bytes 34560 | tf_op jit(solution)/shard_map/all_gather | solution.py:71
  53.7 1.7 slice.2238
  56.0 1.6 reduce.17
  57.6 22.7 %scatter_custom_fusion = f32[81920]{0:T(1024)} fusion(s32[4096]{0:T(1024)} %bitcast.2473, f32[4096]{0:T(1024)S(1)} %reshape.27326, f32[]{:T(128)} %constant.117.clone.1), kind=kCustom, calls=%fused_computation.439 | custom fusion | flops 4096 | bytes 328192 | tf_op jit(solution)/shard_map/scatter-add | solution.py:268
  90.4 1.7 copy.905
  92.9 13.2 %all-gather = f32[16,2,40,8]{2,3,1,0:T(8,128)S(1)} all-gather(f32[2,2,40,8]{2,3,1,0:T(8,128)S(1)} %pad_maximum_fusion.6), channel_id=2, replica_groups=mesh['gx'=16,'gy'=8] {'gy'}, dimensions={0}, use_global_device_ids=true | all-gather | bytes 46080 | tf_op jit(solution)/shard_map/all_gather | solution.py:130
  119.0 1.7 pad_bitcast_fusion
  120.7 25.6 %all-gather.2 = f32[48,1,40,128]{3,2,1,0:T(8,128)S(1)} all-gather(f32[3,1,40,128]{3,2,1,0:T(8,128)S(1)} %pad_maximum_fusion.5), channel_id=4, replica_groups=mesh['gx'=16,'gy'=8] {'gx'}, dimensions={0}, use_global_device_ids=true | all-gather | bytes 1044480 | tf_op jit(solution)/shard_map/all_gather | solution.py:71
  149.8 11.3 %all-gather.18.cloned.1.call-done = f32[32,2,40,128]{3,2,1,0:T(8,128)} async-done(((f32[2,2,40,128]{3,2,1,0:T(8,128)}), f32[32,2,40,128]{3,2,1,0:T(8,128)}) %all-gather.18.cloned.1.call-update) | async-done | bytes 1310736 | tf_op jit(solution)/shard_map/all_gather | solution.py:130
  161.0 1.8 constant_dynamic-update-slice_fusion.47
  168.7 1.5 reshape_squeeze.9
  173.6 37.9 %all-gather.20.cloned.1.call-done = f32[32,2,40,128]{3,2,1,0:T(8,128)} async-done(((f32[2,2,40,128]{3,2,1,0:T(8,128)}), f32[32,2,40,128]{3,2,1,0:T(8,128)}) %all-gather.20.cloned.1.call-update) | async-done | bytes 1310736 | tf_op jit(solution)/shard_map/all_gather | solution.py:130
  211.5 1.9 constant_dynamic-update-slice_fusion.79
  219.6 1.7 copy.959
  221.3 1.7 copy.958
  223.8 13.0 %all-gather.5 = f32[16,2,40,8]{2,3,1,0:T(8,128)S(1)} all-gather(f32[2,2,40,8]{2,3,1,0:T(8,128)S(1)} %pad_maximum_fusion.7), channel_id=7, replica_groups=mesh['gx'=16,'gy'=8] {'gy'}, dimensions={0}, use_global_device_ids=true | all-gather | bytes 46080 | tf_op jit(solution)/shard_map/all_gather | solution.py:130
  245.8 2.0 slice_add_fusion.6
  249.2 2.1 multiply_multiply_fusion.7
  251.3 6.7 shard_map.86
  258.0 1.9 reduce.18
  262.8 16.7 %all_to_all.54 = f32[128,1,33]{2,1,0:T(1,128)S(1)} all-to-all(f32[128,1,33]{2,1,0:T(1,128)S(1)} %bitcast.2442), channel_id=1, replica_groups=mesh['gx'=16,'gy'=8] {'gx','gy'}, dimensions={0} | all-to-all | bytes 33792 | tf_op jit(solution)/shard_map/all_to_all | solution.py:225
  281.5 1.5 reshape.27365
  283.0 5.7 fusion.2
  290.7 2.2 multiply_reduce_fusion.4
  294.1 1.5 concatenate.523
  295.6 5.7 all-to-all-start.2
  301.9 8.6 %all-to-all-done.2 = f32[128,1,33]{2,1,0:T(1,128)} async-done(((f32[128,1,33]{2,1,0:T(1,128)}), f32[128,1,33]{2,1,0:T(1,128)}, u32[]{:S(2)}, u32[]{:S(2)}) %all-to-all-start.2) | async-done | bytes 16928 | tf_op jit(solution)/shard_map/all_to_all | solution.py:225
  310.6 1.5 reshape.27334
  312.1 22.7 %scatter_custom_fusion.1 = f32[81920]{0:T(1024)} fusion(s32[4096]{0:T(1024)} %bitcast.2474, f32[4096]{0:T(1024)} %reshape.27334, f32[]{:T(128)} %constant.117.clone.1), kind=kCustom, calls=%fused_computation.437 | custom fusion | flops 4096 | bytes 328192 | tf_op jit(solution)/shard_map/scatter-add | solution.py:268
  341.0 1.7 copy.966
  342.8 1.7 copy.965
  345.2 12.7 %all-gather.6 = f32[16,2,40,8]{2,3,1,0:T(8,128)S(1)} all-gather(f32[2,2,40,8]{2,3,1,0:T(8,128)S(1)} %pad_maximum_fusion.8), channel_id=8, replica_groups=mesh['gx'=16,'gy'=8] {'gy'}, dimensions={0}, use_global_device_ids=true | all-gather | bytes 46080 | tf_op jit(solution)/shard_map/all_gather | solution.py:130
  367.0 2.0 slice_add_fusion.5
  375.5 1.6 slice_reduce_fusion.3
  377.1 1.5 slice_reduce_fusion.2
  379.9 34.9 %all-gather.22.cloned.1.call-done = f32[32,2,40,128]{3,2,1,0:T(8,128)} async-done(((f32[2,2,40,128]{3,2,1,0:T(8,128)}), f32[32,2,40,128]{3,2,1,0:T(8,128)}) %all-gather.22.cloned.1.call-update) | async-done | bytes 1310736 | tf_op jit(solution)/shard_map/all_gather | solution.py:130
  414.9 1.9 constant_dynamic-update-slice_fusion.143
  424.3 42.2 %all-gather.24.cloned.1.call-done = f32[32,2,40,128]{3,2,1,0:T(8,128)} async-done(((f32[2,2,40,128]{3,2,1,0:T(8,128)}), f32[32,2,40,128]{3,2,1,0:T(8,128)}) %all-gather.24.cloned.1.call-update) | async-done | bytes 1310736 | tf_op jit(solution)/shard_map/all_gather | solution.py:130
  466.4 1.9 constant_dynamic-update-slice_fusion.175
  474.5 1.7 copy.980
  476.2 1.7 copy.979
  478.6 13.0 %all-gather.9 = f32[16,2,40,8]{2,3,1,0:T(8,128)S(1)} all-gather(f32[2,2,40,8]{2,3,1,0:T(8,128)S(1)} %pad_maximum_fusion.9), channel_id=11, replica_groups=mesh['gx'=16,'gy'=8] {'gy'}, dimensions={0}, use_global_device_ids=true | all-gather | bytes 46080 | tf_op jit(solution)/shard_map/all_gather | solution.py:130
  500.6 2.0 slice_add_fusion.2
  504.1 2.1 multiply_multiply_fusion.2
  506.2 6.7 shard_map.87
  512.9 1.9 reduce.19
  516.2 1.5 concatenate.568
  517.7 16.4 %all_to_all.55 = f32[128,1,33]{2,1,0:T(1,128)S(1)} all-to-all(f32[128,1,33]{2,1,0:T(1,128)S(1)} %bitcast.2441), channel_id=1, replica_groups=mesh['gx'=16,'gy'=8] {'gx','gy'}, dimensions={0} | all-to-all | bytes 33792 | tf_op jit(solution)/shard_map/all_to_all | solution.py:225
  536.7 1.7 multiply_reduce_fusion
  538.3 1.6 fusion.19
  539.9 1.5 reshape.27367
  541.5 5.7 fusion
  549.2 2.2 multiply_reduce_fusion.3
  552.6 1.5 concatenate.569
  554.1 5.9 all-to-all-start.4
  560.7 8.6 %all-to-all-done.4 = f32[128,1,33]{2,1,0:T(1,128)} async-done(((f32[128,1,33]{2,1,0:T(1,128)}), f32[128,1,33]{2,1,0:T(1,128)}, u32[]{:S(2)}, u32[]{:S(2)}) %all-to-all-start.4) | async-done | bytes 16928 | tf_op jit(solution)/shard_map/all_to_all | solution.py:225
  569.3 1.5 reshape.27342
  570.9 22.7 %scatter_custom_fusion.2 = f32[81920]{0:T(1024)} fusion(s32[4096]{0:T(1024)} %bitcast.2475, f32[4096]{0:T(1024)} %reshape.27342, f32[]{:T(128)} %constant.117.clone.1), kind=kCustom, calls=%fused_computation.435 | custom fusion | flops 4096 | bytes 328192 | tf_op jit(solution)/shard_map/scatter-add | solution.py:268
  600.0 12.7 %all-gather.10 = f32[16,2,40,8]{2,3,1,0:T(8,128)S(1)} all-gather(f32[2,2,40,8]{2,3,1,0:T(8,128)S(1)} %pad_maximum_fusion.10), channel_id=12, replica_groups=mesh['gx'=16,'gy'=8] {'gy'}, dimensions={0}, use_global_device_ids=true | all-gather | bytes 46080 | tf_op jit(solution)/shard_map/all_gather | solution.py:130
  622.3 1.6 slice_reduce_fusion
  625.2 36.7 %all-gather.26.cloned.1.call-done = f32[32,2,40,128]{3,2,1,0:T(8,128)} async-done(((f32[2,2,40,128]{3,2,1,0:T(8,128)}), f32[32,2,40,128]{3,2,1,0:T(8,128)}) %all-gather.26.cloned.1.call-update) | async-done | bytes 1310736 | tf_op jit(solution)/shard_map/all_gather | solution.py:130
  662.3 1.8 constant_dynamic-update-slice_fusion.239
  (879 shorter events, 144.8 us)
Async XLA Ops:
  10.3 18.3 %copy-start.34 = (f32[40,8,128]{2,1,0:T(8,128)S(1)}, f32[40,8,128]{2,1,0:T(8,128)}, u32[]{:S(2)}) copy-start(f32[40,8,128]{2,1,0:T(8,128)} %param.8) | copy-start | bytes 491524
  16.8 38.7 %all-to-all-start = ((f32[128,1,32]{2,1,0:T(1,128)}), f32[128,1,32]{2,1,0:T(1,128)}, u32[]{:S(2)}, u32[]{:S(2)}) async-start(f32[128,1,32]{2,1,0:T(1,128)} %bitcast.5), calls=%async_computation | async-start | bytes 131072 | tf_op jit(solution)/shard_map/all_to_all | solution.py:277
  28.5 132.5 %all-gather.18.cloned.1.call-start = ((), (), s32[]{:S(2)}) async-start(), calls=%async_computation.5 | async-start | bytes 1392640 | tf_op jit(solution)/shard_map/all_gather | solution.py:130
  47.3 62.6 %copy-start.120 = (f32[40,8]{0,1:T(8,128)}, f32[40,8]{0,1:T(8,128)S(1)}, u32[]{:S(2)}) copy-start(f32[40,8]{0,1:T(8,128)S(1)} %get-tuple-element.334) | copy-start | bytes 3844
  47.3 62.6 %copy-start.122 = (f32[40,8]{0,1:T(8,128)}, f32[40,8]{0,1:T(8,128)S(1)}, u32[]{:S(2)}) copy-start(f32[40,8]{0,1:T(8,128)S(1)} %get-tuple-element.347) | copy-start | bytes 3844
  49.1 69.1 %copy-start = (f32[1,40,8,128]{3,2,1,0:T(8,128)}, f32[1,40,8,128]{3,2,1,0:T(8,128)S(1)}, u32[]{:S(2)}) copy-start(f32[1,40,8,128]{3,2,1,0:T(8,128)S(1)} %get-tuple-element.232) | copy-start | bytes 491524
  53.7 60.5 %copy-start.13 = (f32[40,8,128]{2,0,1:T(8,128)}, f32[40,8,128]{2,0,1:T(8,128)S(1)}, u32[]{:S(2)}) copy-start(f32[40,8,128]{2,0,1:T(8,128)S(1)} %copy.914) | copy-start | bytes 491524
  89.3 17.4 %copy-start.124 = (f32[40,8]{0,1:T(8,128)S(1)}, f32[40,8]{0,1:T(8,128)}, u32[]{:S(2)}) copy-start(f32[40,8]{0,1:T(8,128)} %get-tuple-element.332) | copy-start | bytes 3844
  89.3 17.3 %copy-start.125 = (f32[40,8]{0,1:T(8,128)S(1)}, f32[40,8]{0,1:T(8,128)}, u32[]{:S(2)}) copy-start(f32[40,8]{0,1:T(8,128)} %get-tuple-element.335) | copy-start | bytes 3844
  89.3 17.3 %copy-start.126 = (f32[40,8]{0,1:T(8,128)S(1)}, f32[40,8]{0,1:T(8,128)}, u32[]{:S(2)}) copy-start(f32[40,8]{0,1:T(8,128)} %get-tuple-element.336) | copy-start | bytes 3844
  89.4 17.3 %copy-start.127 = (f32[40,8]{0,1:T(8,128)S(1)}, f32[40,8]{0,1:T(8,128)}, u32[]{:S(2)}) copy-start(f32[40,8]{0,1:T(8,128)} %get-tuple-element.337) | copy-start | bytes 3844
  89.4 17.3 %copy-start.128 = (f32[40,8]{0,1:T(8,128)S(1)}, f32[40,8]{0,1:T(8,128)}, u32[]{:S(2)}) copy-start(f32[40,8]{0,1:T(8,128)} %get-tuple-element.338) | copy-start | bytes 3844
  89.4 17.3 %copy-start.129 = (f32[40,8]{0,1:T(8,128)S(1)}, f32[40,8]{0,1:T(8,128)}, u32[]{:S(2)}) copy-start(f32[40,8]{0,1:T(8,128)} %get-tuple-element.339) | copy-start | bytes 3844
  116.7 94.8 %all-gather.20.cloned.1.call-start = ((), (), s32[]{:S(2)}) async-start(), calls=%async_computation.6 | async-start | bytes 1392640 | tf_op jit(solution)/shard_map/all_gather | solution.py:130
  119.0 45.3 %copy-start.18 = (f32[40,7,128]{2,1,0:T(8,128)}, f32[40,7,128]{2,1,0:T(8,128)S(1)}, u32[]{:S(2)}) copy-start(f32[40,7,128]{2,1,0:T(8,128)S(1)} %slice.2314) | copy-start | bytes 430084
  295.6 14.9 %all-to-all-start.2 = ((f32[128,1,33]{2,1,0:T(1,128)}), f32[128,1,33]{2,1,0:T(1,128)}, u32[]{:S(2)}, u32[]{:S(2)}) async-start(f32[128,1,33]{2,1,0:T(1,128)} %bitcast.2439), calls=%async_computation.2 | async-start | bytes 131072 | tf_op jit(solution)/shard_map/all_to_all | solution.py:225
  301.3 113.6 %all-gather.22.cloned.1.call-start = ((), (), s32[]{:S(2)}) async-start(), calls=%async_computation.7 | async-start | bytes 1392640 | tf_op jit(solution)/shard_map/all_gather | solution.py:130
  375.2 91.2 %all-gather.24.cloned.1.call-start = ((), (), s32[]{:S(2)}) async-start(), calls=%async_computation.8 | async-start | bytes 1392640 | tf_op jit(solution)/shard_map/all_gather | solution.py:130
  554.1 15.2 %all-to-all-start.4 = ((f32[128,1,33]{2,1,0:T(1,128)}), f32[128,1,33]{2,1,0:T(1,128)}, u32[]{:S(2)}, u32[]{:S(2)}) async-start(f32[128,1,33]{2,1,0:T(1,128)} %bitcast.2440), calls=%async_computation.4 | async-start | bytes 131072 | tf_op jit(solution)/shard_map/all_to_all | solution.py:225
  560.1 101.9 %all-gather.26.cloned.1.call-start = ((), (), s32[]{:S(2)}) async-start(), calls=%async_computation.9 | async-start | bytes 1392640 | tf_op jit(solution)/shard_map/all_gather | solution.py:130
  599.0 19.6 %copy-start.24 = (f32[40,8,127]{2,1,0:T(8,128)S(1)}, f32[40,8,127]{2,1,0:T(8,128)}, u32[]{:S(2)}) copy-start(f32[40,8,127]{2,1,0:T(8,128)} %slice.2238) | copy-start | bytes 487684
  599.0 18.1 %copy-start.121 = (f32[40,8]{0,1:T(8,128)S(1)}, f32[40,8]{0,1:T(8,128)}, u32[]{:S(2)}) copy-start(f32[40,8]{0,1:T(8,128)} %copy-done.120) | copy-start | bytes 3844
  599.0 18.1 %copy-start.123 = (f32[40,8]{0,1:T(8,128)S(1)}, f32[40,8]{0,1:T(8,128)}, u32[]{:S(2)}) copy-start(f32[40,8]{0,1:T(8,128)} %copy-done.122) | copy-start | bytes 3844
  599.0 19.8 %copy-start.23 = (f32[40,8,128]{2,1,0:T(8,128)S(1)}, f32[40,8,128]{2,1,0:T(8,128)}, u32[]{:S(2)}) copy-start(f32[40,8,128]{2,1,0:T(8,128)} %pad_bitcast_fusion.1) | copy-start | bytes 491524
  621.1 40.9 %copy-start.50 = (f32[40,128]{1,0:T(8,128)S(1)}, f32[40,128]{1,0:T(8,128)}, u32[]{:S(2)}) copy-start(f32[40,128]{1,0:T(8,128)} %copy-done.46) | copy-start | bytes 61444
  621.1 40.9 %copy-start.55 = (f32[40,128]{1,0:T(8,128)S(1)}, f32[40,128]{1,0:T(8,128)}, u32[]{:S(2)}) copy-start(f32[40,128]{1,0:T(8,128)} %copy-done.51) | copy-start | bytes 61444
  621.1 40.9 %copy-start.60 = (f32[40,128]{1,0:T(8,128)S(1)}, f32[40,128]{1,0:T(8,128)}, u32[]{:S(2)}) copy-start(f32[40,128]{1,0:T(8,128)} %copy-done.56) | copy-start | bytes 61444
  621.1 40.9 %copy-start.77 = (f32[40,128]{1,0:T(8,128)S(1)}, f32[40,128]{1,0:T(8,128)}, u32[]{:S(2)}) copy-start(f32[40,128]{1,0:T(8,128)} %copy-done.76) | copy-start | bytes 61444
  621.1 40.9 %copy-start.79 = (f32[40,128]{1,0:T(8,128)S(1)}, f32[40,128]{1,0:T(8,128)}, u32[]{:S(2)}) copy-start(f32[40,128]{1,0:T(8,128)} %copy-done.78) | copy-start | bytes 61444
  621.1 40.9 %copy-start.81 = (f32[40,128]{1,0:T(8,128)S(1)}, f32[40,128]{1,0:T(8,128)}, u32[]{:S(2)}) copy-start(f32[40,128]{1,0:T(8,128)} %copy-done.80) | copy-start | bytes 61444
  621.1 40.9 %copy-start.83 = (f32[40,128]{1,0:T(8,128)S(1)}, f32[40,128]{1,0:T(8,128)}, u32[]{:S(2)}) copy-start(f32[40,128]{1,0:T(8,128)} %copy-done.82) | copy-start | bytes 61444
  621.1 40.9 %copy-start.85 = (f32[40,128]{1,0:T(8,128)S(1)}, f32[40,128]{1,0:T(8,128)}, u32[]{:S(2)}) copy-start(f32[40,128]{1,0:T(8,128)} %copy-done.84) | copy-start | bytes 61444
  621.1 40.9 %copy-start.86 = (f32[40,128]{1,0:T(8,128)S(1)}, f32[40,128]{1,0:T(8,128)}, u32[]{:S(2)}) copy-start(f32[40,128]{1,0:T(8,128)} %get-tuple-element.298) | copy-start | bytes 61444
  621.1 40.9 %copy-start.87 = (f32[40,128]{1,0:T(8,128)S(1)}, f32[40,128]{1,0:T(8,128)}, u32[]{:S(2)}) copy-start(f32[40,128]{1,0:T(8,128)} %get-tuple-element.299) | copy-start | bytes 61444
  621.2 40.9 %copy-start.88 = (f32[40,128]{1,0:T(8,128)S(1)}, f32[40,128]{1,0:T(8,128)}, u32[]{:S(2)}) copy-start(f32[40,128]{1,0:T(8,128)} %get-tuple-element.300) | copy-start | bytes 61444
  621.2 40.9 %copy-start.89 = (f32[40,128]{1,0:T(8,128)S(1)}, f32[40,128]{1,0:T(8,128)}, u32[]{:S(2)}) copy-start(f32[40,128]{1,0:T(8,128)} %get-tuple-element.301) | copy-start | bytes 61444
  621.2 40.9 %copy-start.90 = (f32[40,128]{1,0:T(8,128)S(1)}, f32[40,128]{1,0:T(8,128)}, u32[]{:S(2)}) copy-start(f32[40,128]{1,0:T(8,128)} %get-tuple-element.302) | copy-start | bytes 61444
  621.2 40.9 %copy-start.91 = (f32[40,128]{1,0:T(8,128)S(1)}, f32[40,128]{1,0:T(8,128)}, u32[]{:S(2)}) copy-start(f32[40,128]{1,0:T(8,128)} %get-tuple-element.303) | copy-start | bytes 61444
  621.2 40.9 %copy-start.92 = (f32[40,128]{1,0:T(8,128)S(1)}, f32[40,128]{1,0:T(8,128)}, u32[]{:S(2)}) copy-start(f32[40,128]{1,0:T(8,128)} %get-tuple-element.304) | copy-start | bytes 61444
  621.2 40.9 %copy-start.93 = (f32[40,128]{1,0:T(8,128)S(1)}, f32[40,128]{1,0:T(8,128)}, u32[]{:S(2)}) copy-start(f32[40,128]{1,0:T(8,128)} %get-tuple-element.305) | copy-start | bytes 61444
  621.2 40.9 %copy-start.94 = (f32[40,128]{1,0:T(8,128)S(1)}, f32[40,128]{1,0:T(8,128)}, u32[]{:S(2)}) copy-start(f32[40,128]{1,0:T(8,128)} %get-tuple-element.306) | copy-start | bytes 61444
  621.2 40.9 %copy-start.95 = (f32[40,128]{1,0:T(8,128)S(1)}, f32[40,128]{1,0:T(8,128)}, u32[]{:S(2)}) copy-start(f32[40,128]{1,0:T(8,128)} %get-tuple-element.307) | copy-start | bytes 61444
  621.2 40.9 %copy-start.96 = (f32[40,128]{1,0:T(8,128)S(1)}, f32[40,128]{1,0:T(8,128)}, u32[]{:S(2)}) copy-start(f32[40,128]{1,0:T(8,128)} %get-tuple-element.308) | copy-start | bytes 61444
  621.2 40.9 %copy-start.97 = (f32[40,128]{1,0:T(8,128)S(1)}, f32[40,128]{1,0:T(8,128)}, u32[]{:S(2)}) copy-start(f32[40,128]{1,0:T(8,128)} %get-tuple-element.309) | copy-start | bytes 61444
  621.3 40.9 %copy-start.98 = (f32[40,128]{1,0:T(8,128)S(1)}, f32[40,128]{1,0:T(8,128)}, u32[]{:S(2)}) copy-start(f32[40,128]{1,0:T(8,128)} %get-tuple-element.262) | copy-start | bytes 61444
  621.3 40.9 %copy-start.99 = (f32[40,128]{1,0:T(8,128)S(1)}, f32[40,128]{1,0:T(8,128)}, u32[]{:S(2)}) copy-start(f32[40,128]{1,0:T(8,128)} %get-tuple-element.264) | copy-start | bytes 61444
  621.3 40.9 %copy-start.100 = (f32[40,128]{1,0:T(8,128)S(1)}, f32[40,128]{1,0:T(8,128)}, u32[]{:S(2)}) copy-start(f32[40,128]{1,0:T(8,128)} %get-tuple-element.266) | copy-start | bytes 61444
  621.3 40.9 %copy-start.101 = (f32[40,128]{1,0:T(8,128)S(1)}, f32[40,128]{1,0:T(8,128)}, u32[]{:S(2)}) copy-start(f32[40,128]{1,0:T(8,128)} %get-tuple-element.268) | copy-start | bytes 61444
  621.3 40.9 %copy-start.102 = (f32[40,128]{1,0:T(8,128)S(1)}, f32[40,128]{1,0:T(8,128)}, u32[]{:S(2)}) copy-start(f32[40,128]{1,0:T(8,128)} %get-tuple-element.270) | copy-start | bytes 61444
  621.3 40.9 %copy-start.103 = (f32[40,128]{1,0:T(8,128)S(1)}, f32[40,128]{1,0:T(8,128)}, u32[]{:S(2)}) copy-start(f32[40,128]{1,0:T(8,128)} %get-tuple-element.272) | copy-start | bytes 61444
  621.3 40.9 %copy-start.104 = (f32[40,128]{1,0:T(8,128)S(1)}, f32[40,128]{1,0:T(8,128)}, u32[]{:S(2)}) copy-start(f32[40,128]{1,0:T(8,128)} %get-tuple-element.274) | copy-start | bytes 61444
  621.3 40.9 %copy-start.105 = (f32[40,128]{1,0:T(8,128)S(1)}, f32[40,128]{1,0:T(8,128)}, u32[]{:S(2)}) copy-start(f32[40,128]{1,0:T(8,128)} %get-tuple-element.276) | copy-start | bytes 61444
  621.3 40.9 %copy-start.106 = (f32[40,128]{1,0:T(8,128)S(1)}, f32[40,128]{1,0:T(8,128)}, u32[]{:S(2)}) copy-start(f32[40,128]{1,0:T(8,128)} %get-tuple-element.277) | copy-start | bytes 61444
  621.3 40.9 %copy-start.107 = (f32[40,128]{1,0:T(8,128)S(1)}, f32[40,128]{1,0:T(8,128)}, u32[]{:S(2)}) copy-start(f32[40,128]{1,0:T(8,128)} %get-tuple-element.278) | copy-start | bytes 61444
  621.4 40.9 %copy-start.108 = (f32[40,128]{1,0:T(8,128)S(1)}, f32[40,128]{1,0:T(8,128)}, u32[]{:S(2)}) copy-start(f32[40,128]{1,0:T(8,128)} %get-tuple-element.279) | copy-start | bytes 61444
  621.4 40.9 %copy-start.109 = (f32[40,128]{1,0:T(8,128)S(1)}, f32[40,128]{1,0:T(8,128)}, u32[]{:S(2)}) copy-start(f32[40,128]{1,0:T(8,128)} %get-tuple-element.280) | copy-start | bytes 61444
  621.4 40.9 %copy-start.110 = (f32[40,128]{1,0:T(8,128)S(1)}, f32[40,128]{1,0:T(8,128)}, u32[]{:S(2)}) copy-start(f32[40,128]{1,0:T(8,128)} %multiply_subtract_fusion.3) | copy-start | bytes 61444
  621.4 40.9 %copy-start.111 = (f32[40,128]{1,0:T(8,128)S(1)}, f32[40,128]{1,0:T(8,128)}, u32[]{:S(2)}) copy-start(f32[40,128]{1,0:T(8,128)} %multiply_subtract_fusion.2) | copy-start | bytes 61444
  621.4 40.9 %copy-start.112 = (f32[40,128]{1,0:T(8,128)S(1)}, f32[40,128]{1,0:T(8,128)}, u32[]{:S(2)}) copy-start(f32[40,128]{1,0:T(8,128)} %get-tuple-element.281) | copy-start | bytes 61444
  621.4 40.9 %copy-start.113 = (f32[40,128]{1,0:T(8,128)S(1)}, f32[40,128]{1,0:T(8,128)}, u32[]{:S(2)}) copy-start(f32[40,128]{1,0:T(8,128)} %get-tuple-element.282) | copy-start | bytes 61444
  621.4 40.9 %copy-start.114 = (f32[40,128]{1,0:T(8,128)S(1)}, f32[40,128]{1,0:T(8,128)}, u32[]{:S(2)}) copy-start(f32[40,128]{1,0:T(8,128)} %get-tuple-element.283) | copy-start | bytes 61444
  621.4 40.9 %copy-start.115 = (f32[40,128]{1,0:T(8,128)S(1)}, f32[40,128]{1,0:T(8,128)}, u32[]{:S(2)}) copy-start(f32[40,128]{1,0:T(8,128)} %get-tuple-element.284) | copy-start | bytes 61444
  621.4 40.9 %copy-start.116 = (f32[40,128]{1,0:T(8,128)S(1)}, f32[40,128]{1,0:T(8,128)}, u32[]{:S(2)}) copy-start(f32[40,128]{1,0:T(8,128)} %get-tuple-element.285) | copy-start | bytes 61444
  621.4 40.9 %copy-start.117 = (f32[40,128]{1,0:T(8,128)S(1)}, f32[40,128]{1,0:T(8,128)}, u32[]{:S(2)}) copy-start(f32[40,128]{1,0:T(8,128)} %get-tuple-element.286) | copy-start | bytes 61444
  (88 other events, 420.7 us)
Sparse Core Ops, SparseCore 0:
  116.8 44.1 all-gather.17
  168.8 42.6 all-gather.19
  375.4 39.4 all-gather.21
  423.8 42.6 all-gather.23
  622.4 39.4 all-gather.25

commit v6 on v5

--- a/solution.py
+++ b/solution.py
@@ -59,7 +59,20 @@
             lax.index_in_dim(back_of_prefix, 0, line_axis, keepdims=False),
         ]
     )
+    rate_totals = lax.all_gather(totals, axis_name)
+    count = rate_totals.shape[0]
+    basis = jnp.arange(2 * count, dtype=jnp.int32).reshape(2 * count, 1, 1, 1)
+    unit_in, unit_out = carries(
+        [(basis == k).astype(jnp.float32) for k in range(count)],
+        [(basis == count + k).astype(jnp.float32) for k in range(count)],
+        rate_totals,
+        periodic,
+        axis_name,
+    )
     return dict(
+        entering_weights=unit_in[:count],
+        leaving_weights=unit_out[:count],
+        leaving_back_weights=unit_out[count:],
         retention=retention,
         gain=scaling * weight,
         gain_out=weight * scaling,
@@ -68,17 +81,14 @@
         prefix=prefix,
         suffix=suffix,
         back_of_prefix=back_of_prefix,
-        rate_totals=lax.all_gather(totals, axis_name),
         axis_name=axis_name,
         periodic=periodic,
         line_axis=line_axis,
     )
 
 
-def carries(got, rate_totals, periodic, axis_name):
-    count = got.shape[0]
-    offsets = [got[k, 0] for k in range(count)]
-    back_parts = [got[k, 1] for k in range(count)]
+def carries(offsets, back_parts, rate_totals, periodic, axis_name):
+    count = len(offsets)
     factors = [rate_totals[k, 0] for k in range(count)]
     back_factors = [rate_totals[k, 1] for k in range(count)]
     back_gains = [rate_totals[k, 2] for k in range(count)]
@@ -90,7 +100,7 @@
             product = product * factors[k]
         first = total / (1.0 - product)
     else:
-        first = jnp.zeros_like(offsets[0])
+        first = jnp.zeros_like(offsets[0] * factors[0])
     entering = [first]
     for k in range(count - 1):
         entering.append(offsets[k] + factors[k] * entering[k])
@@ -103,7 +113,7 @@
             product = product * back_factors[k]
         last = total / (1.0 - product)
     else:
-        last = jnp.zeros_like(offsets[0])
+        last = jnp.zeros_like(offsets[0] * factors[0])
     leaving = [None] * count
     leaving[count - 1] = last
     for k in range(count - 2, -1, -1):
@@ -128,7 +138,10 @@
         ]
     )
     got = lax.all_gather(mine, plan["axis_name"])
-    entering, leaving = carries(got, plan["rate_totals"], plan["periodic"], plan["axis_name"])
+    entering = jnp.sum(plan["entering_weights"] * got[:, 0], axis=0)
+    leaving = jnp.sum(
+        plan["leaving_weights"] * got[:, 0] + plan["leaving_back_weights"] * got[:, 1], axis=0
+    )
     entering = jnp.expand_dims(entering, line_axis)
     leaving = jnp.expand_dims(leaving, line_axis)
     forward = offset + plan["prefix"] * entering

time: 686 us -> 812 us (1.18)
  other arithmetic: 167 us -> 307 us
  blocking collectives: 136 us -> 164 us
  local copies, waits for them, and re-layouts: 110 us -> 92.1 us
  starting transfers between devices: 23.7 us -> 12.1 us
    unnamed x56 -> x43, other arithmetic: 22.4 us -> 115 us
    all_to_all x2 -> x4, blocking collectives: 33.2 us -> 61.2 us  [exchange(): lax.all_to_all(packed, ('gx', 'gy'), split_axis=0, concat_axis=0, tiled=T...]
    unnamed x466 -> x237, local copies, waits for them, and re-layouts: 36.5 us -> 17.4 us
    all_to_all x2 -> x0, waiting for transfers between devices: 17.3 us -> none  [exchange(): lax.all_to_all(packed, ('gx', 'gy'), split_axis=0, concat_axis=0, tiled=T...]
    dynamic_slice x20 -> x0, local copies, waits for them, and re-layouts: 15.8 us -> none  [the longest x10 9.64 us: carries(): mine_in = lax.dynamic_index_in_dim(jnp.stack(entering), place, 0, False)]
    reduce_sum x0 -> x10, other arithmetic: none -> 12.7 us  [line_operator(): jnp.sum(plan['leaving_weights'] * got[:, 0] + plan['leaving_back_weights'...]
    all_to_all x2 -> x0, starting transfers between devices: 11.6 us -> none  [exchange(): lax.all_to_all(packed, ('gx', 'gy'), split_axis=0, concat_axis=0, tiled=T...]
    reduce_sum x0 -> x10, local copies, waits for them, and re-layouts: none -> 10.6 us  [the longest x5 6.39 us: line_operator(): entering = jnp.sum(plan['entering_weights'] * got[:, 0], axis=0)]
  transfers between devices with their start and end apart: 8 -> 6, of which waited for: 7 -> 5; matrix products, arithmetic and copies ran while one was open for 5% -> 21% of each run, Pallas kernels for 0% -> 0%
where the time goes in v6:
time: 812 us; the launch traced here: 802 us
  other arithmetic  307 us (38%)
  waiting for transfers between devices  172 us (21%)
  blocking collectives  164 us (20%)
  local copies, waits for them, and re-layouts  92.1 us (11%)
  between operations  23.6 us (3%)
  matrix products  17 us (2%)
  Pallas kernels  13.3 us (2%)
  starting transfers between devices  12.1 us (1%)
    all_gather x5, waiting for transfers between devices, line_operator(): got = lax.all_gather(mine, plan['axis_name'])  172 us
    unnamed x43, other arithmetic  115 us
    scatter-add x3, other arithmetic, deposit_local(): flat_cells = jnp.zeros((TR * rate_x.size,), jnp.float32).at[cell_index.re...  68.5 us
    all_gather x5, blocking collectives, line_operator(): got = lax.all_gather(mine, plan['axis_name'])  64.7 us
    all_to_all x4, blocking collectives, exchange(): lax.all_to_all(packed, ('gx', 'gy'), split_axis=0, concat_axis=0, tiled=T...  61.2 us
    all_gather x2, blocking collectives, make_plan(): rate_totals = lax.all_gather(totals, axis_name)  38.5 us
    add x100, other arithmetic, scan_offsets(): forcing + level_factor * shift_along(forcing, distance, line_axis, revers...  21.5 us
    unnamed x237, local copies, waits for them, and re-layouts  17.4 us
  transfers between devices with their start and end apart: 6, of which 5 were waited for; matrix products, arithmetic and copies ran while one was open for 21% of the time, Pallas kernels for 0%

profile of v6, /device:TPU:0, one launch (start us, length us, event | category | flops | bytes accessed | tf_op | source)
XLA Modules:
  0.0 801.6 jit_solution(16194828641097083558)
XLA Ops:
  10.3 5.7 fusion.4
  17.4 11.7 %all-to-all-start = ((f32[128,1,32]{2,1,0:T(1,128)}), f32[128,1,32]{2,1,0:T(1,128)}, u32[]{:S(2)}, u32[]{:S(2)}) async-start(f32[128,1,32]{2,1,0:T(1,128)} %bitcast.5), calls=%async_computation | async-start | bytes 131072 | tf_op jit(solution)/shard_map/all_to_all | solution.py:290
  36.2 25.3 %all-gather.2 = f32[48,1,40,128]{3,2,1,0:T(8,128)S(1)} all-gather(f32[3,1,40,128]{3,2,1,0:T(8,128)S(1)} %pad_maximum_fusion.5), channel_id=4, replica_groups=mesh['gx'=16,'gy'=8] {'gx'}, dimensions={0}, use_global_device_ids=true | all-gather | bytes 1044480 | tf_op jit(solution)/shard_map/all_gather | solution.py:62
  76.7 13.2 %all-gather = f32[24,1,40,8]{2,3,1,0:T(8,128)S(1)} all-gather(f32[3,1,40,8]{2,3,1,0:T(8,128)S(1)} %pad_maximum_fusion.11), channel_id=2, replica_groups=mesh['gx'=16,'gy'=8] {'gy'}, dimensions={0}, use_global_device_ids=true | all-gather | bytes 34560 | tf_op jit(solution)/shard_map/all_gather | solution.py:62
  94.7 2.1 constant_dynamic-update-slice_fusion.20
  96.7 2.2 fusion.23
  99.0 2.3 constant_dynamic-update-slice_fusion.19
  101.3 2.2 fusion.24
  103.5 2.3 constant_dynamic-update-slice_fusion.18
  105.8 2.4 fusion.25
  108.3 2.7 constant_dynamic-update-slice_fusion.17
  111.0 2.4 fusion.26
  113.4 2.5 constant_dynamic-update-slice_fusion.16
  116.0 2.6 fusion.27
  118.6 2.7 constant_dynamic-update-slice_fusion.15
  121.3 2.7 fusion.28
  124.0 3.2 fusion.36
  127.2 4.0 copy-done.103
  131.2 5.3 add_dynamic-update-slice_fusion
  136.5 6.8 constant_dynamic-update-slice_fusion.29
  143.3 6.3 fusion.35
  150.0 6.0 constant_dynamic-update-slice_fusion.28
  156.0 5.3 fusion.34
  161.3 5.2 constant_dynamic-update-slice_fusion.27
  166.5 4.6 fusion.33
  171.0 4.7 constant_dynamic-update-slice_fusion.26
  175.7 3.9 fusion.32
  179.6 3.4 constant_dynamic-update-slice_fusion.25
  183.0 3.1 fusion.31
  210.5 2.2 reduce.17
  214.3 22.9 %scatter_custom_fusion = f32[81920]{0:T(1024)} fusion(s32[4096]{0:T(1024)} %bitcast.832, f32[4096]{0:T(1024)} %reshape.2005, f32[]{:T(128)} %constant.42.clone.1), kind=kCustom, calls=%fused_computation.295 | custom fusion | flops 4096 | bytes 328192 | tf_op jit(solution)/shard_map/scatter-add | solution.py:281
  246.1 12.7 %all-gather.1 = f32[16,2,40,8]{2,3,1,0:T(8,128)S(1)} all-gather(f32[2,2,40,8]{2,3,1,0:T(8,128)S(1)} %pad_maximum_fusion.6), channel_id=3, replica_groups=mesh['gx'=16,'gy'=8] {'gy'}, dimensions={0}, use_global_device_ids=true | all-gather | bytes 46080 | tf_op jit(solution)/shard_map/all_gather | solution.py:140
  271.3 3.6 fusion.21
  280.4 4.3 constant_dynamic-update-slice_fusion.24
  284.6 4.1 fusion.30
  288.7 3.9 constant_dynamic-update-slice_fusion.23
  292.6 3.6 fusion.29
  298.3 14.8 %all-gather.18.cloned.1.call-done = f32[32,2,40,128]{3,2,1,0:T(8,128)} async-done(((f32[2,2,40,128]{3,2,1,0:T(8,128)}), f32[32,2,40,128]{3,2,1,0:T(8,128)}) %all-gather.18.cloned.1.call-update) | async-done | bytes 1310736 | tf_op jit(solution)/shard_map/all_gather | solution.py:140
  327.5 41.3 %all-gather.20.cloned.1.call-done = f32[32,2,40,128]{3,2,1,0:T(8,128)} async-done(((f32[2,2,40,128]{3,2,1,0:T(8,128)}), f32[32,2,40,128]{3,2,1,0:T(8,128)}) %all-gather.20.cloned.1.call-update) | async-done | bytes 1310736 | tf_op jit(solution)/shard_map/all_gather | solution.py:140
  380.5 13.4 %all-gather.5 = f32[16,2,40,8]{2,3,1,0:T(8,128)S(1)} all-gather(f32[2,2,40,8]{2,3,1,0:T(8,128)S(1)} %pad_maximum_fusion.7), channel_id=7, replica_groups=mesh['gx'=16,'gy'=8] {'gy'}, dimensions={0}, use_global_device_ids=true | all-gather | bytes 46080 | tf_op jit(solution)/shard_map/all_gather | solution.py:140
  395.4 2.0 slice_add_fusion.6
  398.1 2.2 multiply_multiply_fusion.7
  400.2 6.7 shard_map.86
  410.3 16.4 %all_to_all.54 = f32[128,1,33]{2,1,0:T(1,128)S(1)} all-to-all(f32[128,1,33]{2,1,0:T(1,128)S(1)} %bitcast.806), channel_id=1, replica_groups=mesh['gx'=16,'gy'=8] {'gx','gy'}, dimensions={0} | all-to-all | bytes 33792 | tf_op jit(solution)/shard_map/all_to_all | solution.py:238
  429.0 5.7 fusion.2
  436.8 2.1 multiply_reduce_fusion.12
  441.0 14.4 %all_to_all.55 = f32[128,1,33]{2,1,0:T(1,128)} all-to-all(f32[128,1,33]{2,1,0:T(1,128)S(1)} %bitcast.803), channel_id=1, replica_groups=mesh['gx'=16,'gy'=8] {'gx','gy'}, dimensions={0} | all-to-all | bytes 33792 | tf_op jit(solution)/shard_map/all_to_all | solution.py:238
  457.0 22.7 %scatter_custom_fusion.1 = f32[81920]{0:T(1024)} fusion(s32[4096]{0:T(1024)} %bitcast.833, f32[4096]{0:T(1024)} %reshape.2013, f32[]{:T(128)} %constant.42.clone.1), kind=kCustom, calls=%fused_computation.293 | custom fusion | flops 4096 | bytes 328192 | tf_op jit(solution)/shard_map/scatter-add | solution.py:281
  489.6 12.7 %all-gather.6 = f32[16,2,40,8]{2,3,1,0:T(8,128)S(1)} all-gather(f32[2,2,40,8]{2,3,1,0:T(8,128)S(1)} %pad_maximum_fusion.8), channel_id=8, replica_groups=mesh['gx'=16,'gy'=8] {'gy'}, dimensions={0}, use_global_device_ids=true | all-gather | bytes 46080 | tf_op jit(solution)/shard_map/all_gather | solution.py:140
  505.2 2.0 slice_add_fusion.5
  517.5 35.8 %all-gather.22.cloned.1.call-done = f32[32,2,40,128]{3,2,1,0:T(8,128)} async-done(((f32[2,2,40,128]{3,2,1,0:T(8,128)}), f32[32,2,40,128]{3,2,1,0:T(8,128)}) %all-gather.22.cloned.1.call-update) | async-done | bytes 1310736 | tf_op jit(solution)/shard_map/all_gather | solution.py:140
  562.0 42.7 %all-gather.24.cloned.1.call-done = f32[32,2,40,128]{3,2,1,0:T(8,128)} async-done(((f32[2,2,40,128]{3,2,1,0:T(8,128)}), f32[32,2,40,128]{3,2,1,0:T(8,128)}) %all-gather.24.cloned.1.call-update) | async-done | bytes 1310736 | tf_op jit(solution)/shard_map/all_gather | solution.py:140
  616.4 13.0 %all-gather.9 = f32[16,2,40,8]{2,3,1,0:T(8,128)S(1)} all-gather(f32[2,2,40,8]{2,3,1,0:T(8,128)S(1)} %pad_maximum_fusion.9), channel_id=11, replica_groups=mesh['gx'=16,'gy'=8] {'gy'}, dimensions={0}, use_global_device_ids=true | all-gather | bytes 46080 | tf_op jit(solution)/shard_map/all_gather | solution.py:140
  632.3 2.0 slice_add_fusion.2
  635.0 2.2 multiply_multiply_fusion.2
  637.1 6.6 shard_map.87
  648.7 16.4 %all_to_all.56 = f32[128,1,33]{2,1,0:T(1,128)S(1)} all-to-all(f32[128,1,33]{2,1,0:T(1,128)S(1)} %bitcast.804), channel_id=1, replica_groups=mesh['gx'=16,'gy'=8] {'gx','gy'}, dimensions={0} | all-to-all | bytes 33792 | tf_op jit(solution)/shard_map/all_to_all | solution.py:238
  672.4 5.7 fusion
  680.2 2.3 multiply_reduce_fusion.9
  684.5 13.9 %all_to_all.57 = f32[128,1,33]{2,1,0:T(1,128)S(1)} all-to-all(f32[128,1,33]{2,1,0:T(1,128)S(1)} %bitcast.805), channel_id=1, replica_groups=mesh['gx'=16,'gy'=8] {'gx','gy'}, dimensions={0} | all-to-all | bytes 33792 | tf_op jit(solution)/shard_map/all_to_all | solution.py:238
  699.1 22.9 %scatter_custom_fusion.2 = f32[81920]{0:T(1024)} fusion(s32[4096]{0:T(1024)} %bitcast.834, f32[4096]{0:T(1024)} %reshape.2021, f32[]{:T(128)} %constant.42.clone.1), kind=kCustom, calls=%fused_computation.291 | custom fusion | flops 4096 | bytes 328192 | tf_op jit(solution)/shard_map/scatter-add | solution.py:281
  732.1 12.7 %all-gather.10 = f32[16,2,40,8]{2,3,1,0:T(8,128)S(1)} all-gather(f32[2,2,40,8]{2,3,1,0:T(8,128)S(1)} %pad_maximum_fusion.10), channel_id=12, replica_groups=mesh['gx'=16,'gy'=8] {'gy'}, dimensions={0}, use_global_device_ids=true | all-gather | bytes 46080 | tf_op jit(solution)/shard_map/all_gather | solution.py:140
  746.9 2.0 slice_add_fusion.1
  754.8 37.5 %all-gather.26.cloned.1.call-done = f32[32,2,40,128]{3,2,1,0:T(8,128)} async-done(((f32[2,2,40,128]{3,2,1,0:T(8,128)}), f32[32,2,40,128]{3,2,1,0:T(8,128)}) %all-gather.26.cloned.1.call-update) | async-done | bytes 1310736 | tf_op jit(solution)/shard_map/all_gather | solution.py:140
  (641 shorter events, 201.6 us)
Async XLA Ops:
  7.2 65.1 %copy-start.41 = (f32[40,8,128]{2,1,0:T(8,128)S(1)}, f32[40,8,128]{2,1,0:T(8,128)}, u32[]{:S(2)}) copy-start(f32[40,8,128]{2,1,0:T(8,128)} %param.8) | copy-start | bytes 491524
  17.4 192.6 %all-to-all-start = ((f32[128,1,32]{2,1,0:T(1,128)}), f32[128,1,32]{2,1,0:T(1,128)}, u32[]{:S(2)}, u32[]{:S(2)}) async-start(f32[128,1,32]{2,1,0:T(1,128)} %bitcast.5), calls=%async_computation | async-start | bytes 131072 | tf_op jit(solution)/shard_map/all_to_all | solution.py:290
  29.1 283.9 %all-gather.18.cloned.1.call-start = ((), (), s32[]{:S(2)}) async-start(), calls=%async_computation.5 | async-start | bytes 1392640 | tf_op jit(solution)/shard_map/all_gather | solution.py:140
  35.4 37.4 %copy-start.24 = (f32[1,40,8,128]{3,2,1,0:T(8,128)}, f32[1,40,8,128]{3,2,1,0:T(8,128)S(1)}, u32[]{:S(2)}) copy-start(f32[1,40,8,128]{3,2,1,0:T(8,128)S(1)} %get-tuple-element.51) | copy-start | bytes 491524
  62.8 120.2 %copy-start.86 = (f32[32]{0:T(128)}, f32[32]{0:T(128)S(1)}, u32[]{:S(2)}) copy-start(f32[32]{0:T(128)S(1)} %get-tuple-element.194) | copy-start | bytes 388
  74.3 167.7 %copy-start = (f32[1,40,8,128]{3,2,1,0:T(8,128)}, f32[1,40,8,128]{3,2,1,0:T(8,128)S(1)}, u32[]{:S(2)}) copy-start(f32[1,40,8,128]{3,2,1,0:T(8,128)S(1)} %get-tuple-element.65) | copy-start | bytes 491524
  74.6 167.7 %copy-start.5 = (f32[1,40,8,128]{3,2,1,0:T(8,128)}, f32[1,40,8,128]{3,2,1,0:T(8,128)S(1)}, u32[]{:S(2)}) copy-start(f32[1,40,8,128]{3,2,1,0:T(8,128)S(1)} %get-tuple-element.63) | copy-start | bytes 491524
  75.6 51.5 %copy-start.64 = (f32[1,40,8,128]{3,2,1,0:T(8,128)}, f32[1,40,8,128]{3,2,1,0:T(8,128)S(1)}, u32[]{:S(2)}) copy-start(f32[1,40,8,128]{3,2,1,0:T(8,128)S(1)} %get-tuple-element.58) | copy-start | bytes 491524
  92.4 57.2 %copy-start.42 = (f32[40,128]{1,0:T(8,128)S(1)}, f32[40,128]{1,0:T(8,128)}, u32[]{:S(2)}) copy-start(f32[40,128]{1,0:T(8,128)} %get-tuple-element.96) | copy-start | bytes 61444
  92.4 57.2 %copy-start.43 = (f32[40,128]{1,0:T(8,128)S(1)}, f32[40,128]{1,0:T(8,128)}, u32[]{:S(2)}) copy-start(f32[40,128]{1,0:T(8,128)} %get-tuple-element.85) | copy-start | bytes 61444
  92.4 57.2 %copy-start.44 = (f32[40,128]{1,0:T(8,128)S(1)}, f32[40,128]{1,0:T(8,128)}, u32[]{:S(2)}) copy-start(f32[40,128]{1,0:T(8,128)} %get-tuple-element.97) | copy-start | bytes 61444
  92.4 57.2 %copy-start.45 = (f32[40,128]{1,0:T(8,128)S(1)}, f32[40,128]{1,0:T(8,128)}, u32[]{:S(2)}) copy-start(f32[40,128]{1,0:T(8,128)} %get-tuple-element.83) | copy-start | bytes 61444
  92.5 57.2 %copy-start.50 = (f32[40,128]{1,0:T(8,128)S(1)}, f32[40,128]{1,0:T(8,128)}, u32[]{:S(2)}) copy-start(f32[40,128]{1,0:T(8,128)} %get-tuple-element.98) | copy-start | bytes 61444
  92.5 57.2 %copy-start.51 = (f32[40,128]{1,0:T(8,128)S(1)}, f32[40,128]{1,0:T(8,128)}, u32[]{:S(2)}) copy-start(f32[40,128]{1,0:T(8,128)} %get-tuple-element.81) | copy-start | bytes 61444
  92.5 57.2 %copy-start.53 = (f32[40,128]{1,0:T(8,128)S(1)}, f32[40,128]{1,0:T(8,128)}, u32[]{:S(2)}) copy-start(f32[40,128]{1,0:T(8,128)} %get-tuple-element.93) | copy-start | bytes 61444
  92.5 57.2 %copy-start.54 = (f32[40,128]{1,0:T(8,128)S(1)}, f32[40,128]{1,0:T(8,128)}, u32[]{:S(2)}) copy-start(f32[40,128]{1,0:T(8,128)} %get-tuple-element.79) | copy-start | bytes 61444
  92.5 57.2 %copy-start.55 = (f32[40,128]{1,0:T(8,128)S(1)}, f32[40,128]{1,0:T(8,128)}, u32[]{:S(2)}) copy-start(f32[40,128]{1,0:T(8,128)} %get-tuple-element.99) | copy-start | bytes 61444
  92.5 57.2 %copy-start.56 = (f32[40,128]{1,0:T(8,128)S(1)}, f32[40,128]{1,0:T(8,128)}, u32[]{:S(2)}) copy-start(f32[40,128]{1,0:T(8,128)} %get-tuple-element.92) | copy-start | bytes 61444
  92.5 57.2 %copy-start.58 = (f32[40,128]{1,0:T(8,128)S(1)}, f32[40,128]{1,0:T(8,128)}, u32[]{:S(2)}) copy-start(f32[40,128]{1,0:T(8,128)} %get-tuple-element.100) | copy-start | bytes 61444
  92.5 57.2 %copy-start.59 = (f32[40,128]{1,0:T(8,128)S(1)}, f32[40,128]{1,0:T(8,128)}, u32[]{:S(2)}) copy-start(f32[40,128]{1,0:T(8,128)} %get-tuple-element.84) | copy-start | bytes 61444
  92.5 57.2 %copy-start.65 = (f32[40,128]{1,0:T(8,128)S(1)}, f32[40,128]{1,0:T(8,128)}, u32[]{:S(2)}) copy-start(f32[40,128]{1,0:T(8,128)} %get-tuple-element.101) | copy-start | bytes 61444
  92.5 57.2 %copy-start.66 = (f32[40,128]{1,0:T(8,128)S(1)}, f32[40,128]{1,0:T(8,128)}, u32[]{:S(2)}) copy-start(f32[40,128]{1,0:T(8,128)} %get-tuple-element.88) | copy-start | bytes 61444
  92.6 57.2 %copy-start.73 = (f32[40,128]{1,0:T(8,128)S(1)}, f32[40,128]{1,0:T(8,128)}, u32[]{:S(2)}) copy-start(f32[40,128]{1,0:T(8,128)} %get-tuple-element.102) | copy-start | bytes 61444
  92.6 57.2 %copy-start.74 = (f32[40,128]{1,0:T(8,128)S(1)}, f32[40,128]{1,0:T(8,128)}, u32[]{:S(2)}) copy-start(f32[40,128]{1,0:T(8,128)} %get-tuple-element.80) | copy-start | bytes 61444
  92.6 57.2 %copy-start.79 = (f32[40,128]{1,0:T(8,128)S(1)}, f32[40,128]{1,0:T(8,128)}, u32[]{:S(2)}) copy-start(f32[40,128]{1,0:T(8,128)} %get-tuple-element.103) | copy-start | bytes 61444
  92.6 57.2 %copy-start.80 = (f32[40,128]{1,0:T(8,128)S(1)}, f32[40,128]{1,0:T(8,128)}, u32[]{:S(2)}) copy-start(f32[40,128]{1,0:T(8,128)} %get-tuple-element.78) | copy-start | bytes 61444
  92.6 57.2 %copy-start.84 = (f32[40,128]{1,0:T(8,128)S(1)}, f32[40,128]{1,0:T(8,128)}, u32[]{:S(2)}) copy-start(f32[40,128]{1,0:T(8,128)} %get-tuple-element.104) | copy-start | bytes 61444
  92.6 57.2 %copy-start.85 = (f32[40,128]{1,0:T(8,128)S(1)}, f32[40,128]{1,0:T(8,128)}, u32[]{:S(2)}) copy-start(f32[40,128]{1,0:T(8,128)} %get-tuple-element.82) | copy-start | bytes 61444
  92.6 57.2 %copy-start.87 = (f32[32]{0:T(128)S(1)}, f32[32]{0:T(128)}, u32[]{:S(2)}) copy-start(f32[32]{0:T(128)} %get-tuple-element.195) | copy-start | bytes 388
  92.6 57.2 %copy-start.88 = (f32[32]{0:T(128)S(1)}, f32[32]{0:T(128)}, u32[]{:S(2)}) copy-start(f32[32]{0:T(128)} %get-tuple-element.196) | copy-start | bytes 388
  92.6 57.2 %copy-start.89 = (f32[32]{0:T(128)S(1)}, f32[32]{0:T(128)}, u32[]{:S(2)}) copy-start(f32[32]{0:T(128)} %get-tuple-element.197) | copy-start | bytes 388
  92.6 57.2 %copy-start.90 = (f32[32]{0:T(128)S(1)}, f32[32]{0:T(128)}, u32[]{:S(2)}) copy-start(f32[32]{0:T(128)} %get-tuple-element.198) | copy-start | bytes 388
  92.7 57.2 %copy-start.91 = (f32[32]{0:T(128)S(1)}, f32[32]{0:T(128)}, u32[]{:S(2)}) copy-start(f32[32]{0:T(128)} %get-tuple-element.199) | copy-start | bytes 388
  92.7 57.2 %copy-start.92 = (f32[32]{0:T(128)S(1)}, f32[32]{0:T(128)}, u32[]{:S(2)}) copy-start(f32[32]{0:T(128)} %get-tuple-element.200) | copy-start | bytes 388
  92.7 57.2 %copy-start.93 = (f32[32]{0:T(128)S(1)}, f32[32]{0:T(128)}, u32[]{:S(2)}) copy-start(f32[32]{0:T(128)} %get-tuple-element.201) | copy-start | bytes 388
  92.7 57.2 %copy-start.94 = (f32[32]{0:T(128)S(1)}, f32[32]{0:T(128)}, u32[]{:S(2)}) copy-start(f32[32]{0:T(128)} %get-tuple-element.202) | copy-start | bytes 388
  92.7 57.2 %copy-start.95 = (f32[32]{0:T(128)S(1)}, f32[32]{0:T(128)}, u32[]{:S(2)}) copy-start(f32[32]{0:T(128)} %get-tuple-element.203) | copy-start | bytes 388
  92.7 57.2 %copy-start.96 = (f32[32]{0:T(128)S(1)}, f32[32]{0:T(128)}, u32[]{:S(2)}) copy-start(f32[32]{0:T(128)} %get-tuple-element.204) | copy-start | bytes 388
  92.7 57.2 %copy-start.97 = (f32[32]{0:T(128)S(1)}, f32[32]{0:T(128)}, u32[]{:S(2)}) copy-start(f32[32]{0:T(128)} %get-tuple-element.205) | copy-start | bytes 388
  92.7 57.2 %copy-start.98 = (f32[32]{0:T(128)S(1)}, f32[32]{0:T(128)}, u32[]{:S(2)}) copy-start(f32[32]{0:T(128)} %get-tuple-element.206) | copy-start | bytes 388
  92.7 57.2 %copy-start.99 = (f32[32]{0:T(128)S(1)}, f32[32]{0:T(128)}, u32[]{:S(2)}) copy-start(f32[32]{0:T(128)} %get-tuple-element.207) | copy-start | bytes 388
  92.7 57.2 %copy-start.101 = (f32[32]{0:T(128)S(1)}, f32[32]{0:T(128)}, u32[]{:S(2)}) copy-start(f32[32]{0:T(128)} %get-tuple-element.177) | copy-start | bytes 388
  92.8 57.2 %copy-start.102 = (f32[32]{0:T(128)S(1)}, f32[32]{0:T(128)}, u32[]{:S(2)}) copy-start(f32[32]{0:T(128)} %get-tuple-element.178) | copy-start | bytes 388
  92.8 57.2 %copy-start.104 = (f32[32]{0:T(128)S(1)}, f32[32]{0:T(128)}, u32[]{:S(2)}) copy-start(f32[32]{0:T(128)} %get-tuple-element.179) | copy-start | bytes 388
  92.8 57.2 %copy-start.105 = (f32[32]{0:T(128)S(1)}, f32[32]{0:T(128)}, u32[]{:S(2)}) copy-start(f32[32]{0:T(128)} %get-tuple-element.180) | copy-start | bytes 388
  92.8 57.2 %copy-start.106 = (f32[32]{0:T(128)S(1)}, f32[32]{0:T(128)}, u32[]{:S(2)}) copy-start(f32[32]{0:T(128)} %get-tuple-element.181) | copy-start | bytes 388
  92.8 57.2 %copy-start.107 = (f32[32]{0:T(128)S(1)}, f32[32]{0:T(128)}, u32[]{:S(2)}) copy-start(f32[32]{0:T(128)} %get-tuple-element.182) | copy-start | bytes 388
  92.8 57.2 %copy-start.108 = (f32[32]{0:T(128)S(1)}, f32[32]{0:T(128)}, u32[]{:S(2)}) copy-start(f32[32]{0:T(128)} %get-tuple-element.183) | copy-start | bytes 388
  271.3 97.5 %all-gather.20.cloned.1.call-start = ((), (), s32[]{:S(2)}) async-start(), calls=%async_computation.6 | async-start | bytes 1392640 | tf_op jit(solution)/shard_map/all_gather | solution.py:140
  296.2 29.8 %copy-start.81 = (s32[1,128,32]{2,1,0:T(8,128)S(1)}, s32[1,128,32]{2,1,0:T(8,128)}, u32[]{:S(2)}) copy-start(s32[1,128,32]{2,1,0:T(8,128)} %copy.1002) | copy-start | bytes 49156
  326.0 227.3 %all-gather.22.cloned.1.call-start = ((), (), s32[]{:S(2)}) async-start(), calls=%async_computation.7 | async-start | bytes 1392640 | tf_op jit(solution)/shard_map/all_gather | solution.py:140
  372.8 21.2 %copy-start.67 = (f32[8,40,8]{1,2,0:T(8,128)S(1)}, f32[8,40,8]{1,2,0:T(8,128)}, u32[]{:S(2)}) copy-start(f32[8,40,8]{1,2,0:T(8,128)} %dynamic-slice_bitcast_fusion.5) | copy-start | bytes 30724
  373.5 53.3 %copy-start.110 = (s32[1,128]{1,0:T(1,128)S(1)}, s32[1,128]{1,0:T(1,128)}, u32[]{:S(2)}) copy-start(s32[1,128]{1,0:T(1,128)} %param.11) | copy-start | bytes 1540
  513.8 90.9 %all-gather.24.cloned.1.call-start = ((), (), s32[]{:S(2)}) async-start(), calls=%async_computation.8 | async-start | bytes 1392640 | tf_op jit(solution)/shard_map/all_gather | solution.py:140
  562.0 230.3 %all-gather.26.cloned.1.call-start = ((), (), s32[]{:S(2)}) async-start(), calls=%async_computation.9 | async-start | bytes 1392640 | tf_op jit(solution)/shard_map/all_gather | solution.py:140
  698.5 25.9 %copy-start.82 = (f32[128,1,33]{2,1,0:T(1,128)}, f32[128,1,33]{2,1,0:T(1,128)S(1)}, u32[]{:S(2)}) copy-start(f32[128,1,33]{2,1,0:T(1,128)S(1)} %all_to_all.57) | copy-start | bytes 50692
  724.7 24.9 %copy-start.23 = (f32[1,40,8,128]{3,2,1,0:T(8,128)S(1)}, f32[1,40,8,128]{3,2,1,0:T(8,128)}, u32[]{:S(2)}) copy-start(f32[1,40,8,128]{3,2,1,0:T(8,128)} %copy-done.22) | copy-start | bytes 491524
  725.2 26.0 %copy-start.35 = (f32[40,8,128]{2,0,1:T(8,128)S(1)}, f32[40,8,128]{2,0,1:T(8,128)}, u32[]{:S(2)}) copy-start(f32[40,8,128]{2,0,1:T(8,128)} %copy.1014) | copy-start | bytes 491524
  725.4 26.0 %copy-start.32 = (f32[40,8,128]{2,0,1:T(8,128)S(1)}, f32[40,8,128]{2,0,1:T(8,128)}, u32[]{:S(2)}) copy-start(f32[40,8,128]{2,0,1:T(8,128)} %copy.1017) | copy-start | bytes 491524
  726.9 24.9 %copy-start.27 = (f32[1,40,8,128]{3,2,1,0:T(8,128)S(1)}, f32[1,40,8,128]{3,2,1,0:T(8,128)}, u32[]{:S(2)}) copy-start(f32[1,40,8,128]{3,2,1,0:T(8,128)} %copy-done.24) | copy-start | bytes 491524
  727.5 66.2 %copy-start.34 = (f32[40,7,128]{2,1,0:T(8,128)S(1)}, f32[40,7,128]{2,1,0:T(8,128)}, u32[]{:S(2)}) copy-start(f32[40,7,128]{2,1,0:T(8,128)} %slice.1211) | copy-start | bytes 430084
  727.6 66.2 %copy-start.29 = (f32[1,40,8,128]{3,2,1,0:T(8,128)S(1)}, f32[1,40,8,128]{3,2,1,0:T(8,128)}, u32[]{:S(2)}) copy-start(f32[1,40,8,128]{3,2,1,0:T(8,128)} %copy-done.28) | copy-start | bytes 491524
  727.6 66.2 %copy-start.31 = (f32[2,40,8,128]{3,2,1,0:T(8,128)S(1)}, f32[2,40,8,128]{3,2,1,0:T(8,128)}, u32[]{:S(2)}) copy-start(f32[2,40,8,128]{3,2,1,0:T(8,128)} %copy-done.30) | copy-start | bytes 983044
  727.6 66.2 %copy-start.33 = (f32[40,8,128]{2,1,0:T(8,128)S(1)}, f32[40,8,128]{2,1,0:T(8,128)}, u32[]{:S(2)}) copy-start(f32[40,8,128]{2,1,0:T(8,128)} %pad_bitcast_fusion) | copy-start | bytes 491524
  (53 other events, 263.2 us)
Sparse Core Ops, SparseCore 0:
  271.4 41.5 all-gather.17
  326.1 42.6 all-gather.19
  513.9 39.3 all-gather.21
  562.1 42.6 all-gather.23
  752.7 39.4 all-gather.25

commit v7 on v5

--- a/solution.py
+++ b/solution.py
@@ -68,7 +68,8 @@
         prefix=prefix,
         suffix=suffix,
         back_of_prefix=back_of_prefix,
-        rate_totals=lax.all_gather(totals, axis_name),
+        rate_totals=lax.all_gather(totals, axis_name) if periodic else None,
+        totals=totals,
         axis_name=axis_name,
         periodic=periodic,
         line_axis=line_axis,
@@ -127,7 +128,13 @@
             lax.index_in_dim(back_offset, 0, line_axis, keepdims=False),
         ]
     )
-    got = lax.all_gather(mine, plan["axis_name"])
+    if plan["rate_totals"] is None:
+        rate_part = jnp.broadcast_to(plan["totals"], (3,) + mine.shape[1:])
+        both = lax.all_gather(jnp.concatenate([mine, rate_part]), plan["axis_name"])
+        got = both[:, :2]
+        plan["rate_totals"] = both[:, 2:, :1]
+    else:
+        got = lax.all_gather(mine, plan["axis_name"])
     entering, leaving = carries(got, plan["rate_totals"], plan["periodic"], plan["axis_name"])
     entering = jnp.expand_dims(entering, line_axis)
     leaving = jnp.expand_dims(leaving, line_axis)

time: 686 us -> 671 us (0.978)
  blocking collectives: 136 us -> 124 us
    all_gather x0 -> x1, blocking collectives: none -> 13.4 us  [line_operator(): both = lax.all_gather(jnp.concatenate([mine, rate_part]), plan['axis_name'])]
    all_gather x5 -> x4, blocking collectives: 64.7 us -> 51.5 us  [line_operator(): got = lax.all_gather(mine, plan['axis_name'])]
    all_gather x2 -> x1, blocking collectives: 38.4 us -> 25.7 us  [make_plan(): lax.all_gather(totals, axis_name)]
    unnamed x466 -> x472, local copies, waits for them, and re-layouts: 36.5 us -> 34.1 us
where the time goes in v7:
time: 671 us; the launch traced here: 659 us
  waiting for transfers between devices  181 us (27%)
  other arithmetic  166 us (25%)
  blocking collectives  124 us (18%)
  local copies, waits for them, and re-layouts  110 us (16%)
  between operations  25.2 us (4%)
  starting transfers between devices  23.7 us (4%)
  matrix products  17 us (3%)
  Pallas kernels  13.4 us (2%)
    all_gather x5, waiting for transfers between devices, line_operator(): got = lax.all_gather(mine, plan['axis_name'])  163 us
    scatter-add x3, other arithmetic, deposit_local(): flat_cells = jnp.zeros((TR * rate_x.size,), jnp.float32).at[cell_index.re...  68.2 us
    all_gather x4, blocking collectives, line_operator(): got = lax.all_gather(mine, plan['axis_name'])  51.5 us
    unnamed x472, local copies, waits for them, and re-layouts  34.1 us
    all_to_all x2, blocking collectives, exchange(): lax.all_to_all(packed, ('gx', 'gy'), split_axis=0, concat_axis=0, tiled=T...  33.2 us
    all_gather x1, blocking collectives, make_plan(): lax.all_gather(totals, axis_name)  25.7 us
    unnamed x56, other arithmetic  21.3 us
    add x100, other arithmetic, scan_offsets(): forcing + level_factor * shift_along(forcing, distance, line_axis, revers...  17.5 us
  transfers between devices with their start and end apart: 8, of which 7 were waited for; matrix products, arithmetic and copies ran while one was open for 5% of the time, Pallas kernels for 0%

profile of v7, /device:TPU:0, one launch (start us, length us, event | category | flops | bytes accessed | tf_op | source)
XLA Modules:
  0.0 659.0 jit_solution(13150415036278327112)
XLA Ops:
  10.3 5.7 fusion.4
  16.8 11.7 %all-to-all-start = ((f32[128,1,32]{2,1,0:T(1,128)}), f32[128,1,32]{2,1,0:T(1,128)}, u32[]{:S(2)}, u32[]{:S(2)}) async-start(f32[128,1,32]{2,1,0:T(1,128)} %bitcast.5), calls=%async_computation | async-start | bytes 131072 | tf_op jit(solution)/shard_map/all_to_all | solution.py:284
  37.5 1.6 pad_bitcast_fusion.1
  40.1 1.7 multiply_add_fusion.93
  44.1 1.7 slice.2275
  46.4 1.6 reduce.17
  48.1 22.7 %scatter_custom_fusion = f32[81920]{0:T(1024)} fusion(s32[4096]{0:T(1024)} %bitcast.2474, f32[4096]{0:T(1024)S(1)} %reshape.27326, f32[]{:T(128)} %constant.117.clone.1), kind=kCustom, calls=%fused_computation.439 | custom fusion | flops 4096 | bytes 328192 | tf_op jit(solution)/shard_map/scatter-add | solution.py:275
  81.9 13.4 %all-gather = f32[40,2,40,8]{2,3,1,0:T(8,128)S(1)} all-gather(f32[5,2,40,8]{2,3,1,0:T(8,128)S(1)} %pad_maximum_fusion.6), channel_id=2, replica_groups=mesh['gx'=16,'gy'=8] {'gy'}, dimensions={0}, use_global_device_ids=true | all-gather | bytes 115200 | tf_op jit(solution)/shard_map/all_gather | solution.py:133
  103.9 1.7 pad_bitcast_fusion
  105.5 25.7 %all-gather.1 = f32[48,1,40,128]{3,2,1,0:T(8,128)S(1)} all-gather(f32[3,1,40,128]{3,2,1,0:T(8,128)S(1)} %pad_maximum_fusion.5), channel_id=3, replica_groups=mesh['gx'=16,'gy'=8] {'gx'}, dimensions={0}, use_global_device_ids=true | all-gather | bytes 1044480 | tf_op jit(solution)/shard_map/all_gather | solution.py:71
  134.7 11.4 %all-gather.17.cloned.1.call-done = f32[32,2,40,128]{3,2,1,0:T(8,128)} async-done(((f32[2,2,40,128]{3,2,1,0:T(8,128)}), f32[32,2,40,128]{3,2,1,0:T(8,128)}) %all-gather.17.cloned.1.call-update) | async-done | bytes 1310736 | tf_op jit(solution)/shard_map/all_gather | solution.py:137
  146.0 1.8 constant_dynamic-update-slice_fusion.47
  153.7 1.5 reshape_squeeze.9
  158.6 37.9 %all-gather.19.cloned.1.call-done = f32[32,2,40,128]{3,2,1,0:T(8,128)} async-done(((f32[2,2,40,128]{3,2,1,0:T(8,128)}), f32[32,2,40,128]{3,2,1,0:T(8,128)}) %all-gather.19.cloned.1.call-update) | async-done | bytes 1310736 | tf_op jit(solution)/shard_map/all_gather | solution.py:137
  196.5 1.9 constant_dynamic-update-slice_fusion.79
  204.6 1.7 copy.920
  206.3 1.7 copy.919
  208.8 13.0 %all-gather.4 = f32[16,2,40,8]{2,3,1,0:T(8,128)S(1)} all-gather(f32[2,2,40,8]{2,3,1,0:T(8,128)S(1)} %pad_maximum_fusion.7), channel_id=6, replica_groups=mesh['gx'=16,'gy'=8] {'gy'}, dimensions={0}, use_global_device_ids=true | all-gather | bytes 46080 | tf_op jit(solution)/shard_map/all_gather | solution.py:137
  230.8 2.0 slice_add_fusion.6
  234.2 2.1 multiply_multiply_fusion.7
  236.3 6.7 %shard_map.86 = f32[1,4096]{1,0:T(1,128)} custom-call(f32[640,128]{1,0:T(8,128)} %bitcast.2408, s32[1,4096]{1,0:T(1,128)} %and_select_fusion.1.rows_ref, s32[1,4096]{1,0:T(1,128)} %get-tuple-element.148.lanes_ref), custom_call_target="tpu_custom_call" | custom-call | tf_op jit(solution)/shard_map/pallas_call | solution.py:176
  243.0 2.0 reduce.18
  247.9 16.7 %all_to_all.54 = f32[128,1,33]{2,1,0:T(1,128)S(1)} all-to-all(f32[128,1,33]{2,1,0:T(1,128)S(1)} %bitcast.2443), channel_id=1, replica_groups=mesh['gx'=16,'gy'=8] {'gx','gy'}, dimensions={0} | all-to-all | bytes 33792 | tf_op jit(solution)/shard_map/all_to_all | solution.py:232
  266.6 1.5 reshape.27364
  268.1 5.7 fusion.2
  275.9 2.2 multiply_reduce_fusion.4
  279.3 1.5 concatenate.527
  280.8 5.7 all-to-all-start.2
  287.2 8.6 %all-to-all-done.2 = f32[128,1,33]{2,1,0:T(1,128)} async-done(((f32[128,1,33]{2,1,0:T(1,128)}), f32[128,1,33]{2,1,0:T(1,128)}, u32[]{:S(2)}, u32[]{:S(2)}) %all-to-all-start.2) | async-done | bytes 16928 | tf_op jit(solution)/shard_map/all_to_all | solution.py:232
  295.8 1.5 reshape.27334
  297.3 22.7 %scatter_custom_fusion.1 = f32[81920]{0:T(1024)} fusion(s32[4096]{0:T(1024)} %bitcast.2475, f32[4096]{0:T(1024)} %reshape.27334, f32[]{:T(128)} %constant.117.clone.1), kind=kCustom, calls=%fused_computation.437 | custom fusion | flops 4096 | bytes 328192 | tf_op jit(solution)/shard_map/scatter-add | solution.py:275
  326.3 1.7 copy.927
  328.0 1.7 copy.926
  330.5 12.7 %all-gather.5 = f32[16,2,40,8]{2,3,1,0:T(8,128)S(1)} all-gather(f32[2,2,40,8]{2,3,1,0:T(8,128)S(1)} %pad_maximum_fusion.8), channel_id=7, replica_groups=mesh['gx'=16,'gy'=8] {'gy'}, dimensions={0}, use_global_device_ids=true | all-gather | bytes 46080 | tf_op jit(solution)/shard_map/all_gather | solution.py:137
  352.2 2.0 slice_add_fusion.5
  360.8 1.5 slice_reduce_fusion.3
  362.3 1.5 slice_reduce_fusion.2
  365.0 35.1 %all-gather.21.cloned.1.call-done = f32[32,2,40,128]{3,2,1,0:T(8,128)} async-done(((f32[2,2,40,128]{3,2,1,0:T(8,128)}), f32[32,2,40,128]{3,2,1,0:T(8,128)}) %all-gather.21.cloned.1.call-update) | async-done | bytes 1310736 | tf_op jit(solution)/shard_map/all_gather | solution.py:137
  400.2 1.9 constant_dynamic-update-slice_fusion.143
  409.6 42.2 %all-gather.23.cloned.1.call-done = f32[32,2,40,128]{3,2,1,0:T(8,128)} async-done(((f32[2,2,40,128]{3,2,1,0:T(8,128)}), f32[32,2,40,128]{3,2,1,0:T(8,128)}) %all-gather.23.cloned.1.call-update) | async-done | bytes 1310736 | tf_op jit(solution)/shard_map/all_gather | solution.py:137
  451.8 1.9 constant_dynamic-update-slice_fusion.175
  459.8 1.7 copy.941
  461.5 1.7 copy.940
  464.0 13.0 %all-gather.8 = f32[16,2,40,8]{2,3,1,0:T(8,128)S(1)} all-gather(f32[2,2,40,8]{2,3,1,0:T(8,128)S(1)} %pad_maximum_fusion.9), channel_id=10, replica_groups=mesh['gx'=16,'gy'=8] {'gy'}, dimensions={0}, use_global_device_ids=true | all-gather | bytes 46080 | tf_op jit(solution)/shard_map/all_gather | solution.py:137
  486.0 2.0 slice_add_fusion.2
  489.4 2.1 multiply_multiply_fusion.2
  491.5 6.7 %shard_map.87 = f32[1,4096]{1,0:T(1,128)} custom-call(f32[640,128]{1,0:T(8,128)} %bitcast.2407, s32[1,4096]{1,0:T(1,128)} %and_select_fusion.1.rows_ref, s32[1,4096]{1,0:T(1,128)} %get-tuple-element.148.lanes_ref), custom_call_target="tpu_custom_call" | custom-call | tf_op jit(solution)/shard_map/pallas_call | solution.py:176
  498.2 2.0 reduce.19
  501.6 1.5 concatenate.572
  503.2 16.4 %all_to_all.55 = f32[128,1,33]{2,1,0:T(1,128)S(1)} all-to-all(f32[128,1,33]{2,1,0:T(1,128)S(1)} %bitcast.2442), channel_id=1, replica_groups=mesh['gx'=16,'gy'=8] {'gx','gy'}, dimensions={0} | all-to-all | bytes 33792 | tf_op jit(solution)/shard_map/all_to_all | solution.py:232
  522.2 1.7 multiply_reduce_fusion
  523.8 1.6 fusion.19
  525.4 1.5 reshape.27366
  527.0 5.7 fusion
  534.7 2.3 multiply_reduce_fusion.3
  538.1 1.5 concatenate.573
  539.6 5.9 all-to-all-start.4
  546.2 8.6 %all-to-all-done.4 = f32[128,1,33]{2,1,0:T(1,128)} async-done(((f32[128,1,33]{2,1,0:T(1,128)}), f32[128,1,33]{2,1,0:T(1,128)}, u32[]{:S(2)}, u32[]{:S(2)}) %all-to-all-start.4) | async-done | bytes 16928 | tf_op jit(solution)/shard_map/all_to_all | solution.py:232
  554.8 1.5 reshape.27342
  556.3 22.7 %scatter_custom_fusion.2 = f32[81920]{0:T(1024)} fusion(s32[4096]{0:T(1024)} %bitcast.2476, f32[4096]{0:T(1024)} %reshape.27342, f32[]{:T(128)} %constant.117.clone.1), kind=kCustom, calls=%fused_computation.435 | custom fusion | flops 4096 | bytes 328192 | tf_op jit(solution)/shard_map/scatter-add | solution.py:275
  585.5 12.7 %all-gather.9 = f32[16,2,40,8]{2,3,1,0:T(8,128)S(1)} all-gather(f32[2,2,40,8]{2,3,1,0:T(8,128)S(1)} %pad_maximum_fusion.10), channel_id=11, replica_groups=mesh['gx'=16,'gy'=8] {'gy'}, dimensions={0}, use_global_device_ids=true | all-gather | bytes 46080 | tf_op jit(solution)/shard_map/all_gather | solution.py:137
  607.8 1.6 slice_reduce_fusion
  610.8 36.7 %all-gather.25.cloned.1.call-done = f32[32,2,40,128]{3,2,1,0:T(8,128)} async-done(((f32[2,2,40,128]{3,2,1,0:T(8,128)}), f32[32,2,40,128]{3,2,1,0:T(8,128)}) %all-gather.25.cloned.1.call-update) | async-done | bytes 1310736 | tf_op jit(solution)/shard_map/all_gather | solution.py:137
  647.8 1.8 constant_dynamic-update-slice_fusion.239
  (885 shorter events, 140.8 us)
Async XLA Ops:
  10.3 18.3 %copy-start.143 = (s32[1,128,32]{1,2,0:T(8,128)S(1)}, s32[1,128,32]{1,2,0:T(8,128)}, u32[]{:S(2)}) copy-start(s32[1,128,32]{1,2,0:T(8,128)} %param.10) | copy-start | bytes 49156
  10.3 19.6 %copy-start.34 = (f32[40,8,128]{2,1,0:T(8,128)S(1)}, f32[40,8,128]{2,1,0:T(8,128)}, u32[]{:S(2)}) copy-start(f32[40,8,128]{2,1,0:T(8,128)} %param.7) | copy-start | bytes 491524
  16.8 29.0 %all-to-all-start = ((f32[128,1,32]{2,1,0:T(1,128)}), f32[128,1,32]{2,1,0:T(1,128)}, u32[]{:S(2)}, u32[]{:S(2)}) async-start(f32[128,1,32]{2,1,0:T(1,128)} %bitcast.5), calls=%async_computation | async-start | bytes 131072 | tf_op jit(solution)/shard_map/all_to_all | solution.py:284
  28.5 117.5 %all-gather.17.cloned.1.call-start = ((), (), s32[]{:S(2)}) async-start(), calls=%async_computation.5 | async-start | bytes 1392640 | tf_op jit(solution)/shard_map/all_gather | solution.py:137
  30.3 72.7 %copy-start = (f32[1,40,8,128]{3,2,1,0:T(8,128)}, f32[1,40,8,128]{3,2,1,0:T(8,128)S(1)}, u32[]{:S(2)}) copy-start(f32[1,40,8,128]{3,2,1,0:T(8,128)S(1)} %get-tuple-element.232) | copy-start | bytes 491524
  44.1 55.1 %copy-start.8 = (f32[40,8,128]{2,0,1:T(8,128)}, f32[40,8,128]{2,0,1:T(8,128)S(1)}, u32[]{:S(2)}) copy-start(f32[40,8,128]{2,0,1:T(8,128)S(1)} %copy.875) | copy-start | bytes 491524
  79.8 15.7 %copy-start.145 = (f32[8,2,40,8]{2,3,1,0:T(8,128)S(1)}, f32[8,2,40,8]{2,3,1,0:T(8,128)}, u32[]{:S(2)}) copy-start(f32[8,2,40,8]{2,3,1,0:T(8,128)} %constant_dynamic-update-slice_fusion.7) | copy-start | bytes 61444
  101.6 94.9 %all-gather.19.cloned.1.call-start = ((), (), s32[]{:S(2)}) async-start(), calls=%async_computation.6 | async-start | bytes 1392640 | tf_op jit(solution)/shard_map/all_gather | solution.py:137
  103.8 45.5 %copy-start.19 = (f32[40,7,128]{2,1,0:T(8,128)}, f32[40,7,128]{2,1,0:T(8,128)S(1)}, u32[]{:S(2)}) copy-start(f32[40,7,128]{2,1,0:T(8,128)S(1)} %slice.2351) | copy-start | bytes 430084
  133.2 15.3 %copy-start.58 = (f32[40,128]{1,0:T(8,128)}, f32[40,128]{1,0:T(8,128)S(1)}, u32[]{:S(2)}) copy-start(f32[40,128]{1,0:T(8,128)S(1)} %get-tuple-element.292) | copy-start | bytes 61444
  133.9 14.0 %copy-start.79 = (f32[40,128]{1,0:T(8,128)}, f32[40,128]{1,0:T(8,128)S(1)}, u32[]{:S(2)}) copy-start(f32[40,128]{1,0:T(8,128)S(1)} %get-tuple-element.293) | copy-start | bytes 61444
  133.9 14.0 %copy-start.81 = (f32[40,128]{1,0:T(8,128)}, f32[40,128]{1,0:T(8,128)S(1)}, u32[]{:S(2)}) copy-start(f32[40,128]{1,0:T(8,128)S(1)} %get-tuple-element.294) | copy-start | bytes 61444
  133.9 14.0 %copy-start.83 = (f32[40,128]{1,0:T(8,128)}, f32[40,128]{1,0:T(8,128)S(1)}, u32[]{:S(2)}) copy-start(f32[40,128]{1,0:T(8,128)S(1)} %get-tuple-element.295) | copy-start | bytes 61444
  133.9 14.0 %copy-start.85 = (f32[40,128]{1,0:T(8,128)}, f32[40,128]{1,0:T(8,128)S(1)}, u32[]{:S(2)}) copy-start(f32[40,128]{1,0:T(8,128)S(1)} %get-tuple-element.296) | copy-start | bytes 61444
  133.9 14.0 %copy-start.87 = (f32[40,128]{1,0:T(8,128)}, f32[40,128]{1,0:T(8,128)S(1)}, u32[]{:S(2)}) copy-start(f32[40,128]{1,0:T(8,128)S(1)} %get-tuple-element.297) | copy-start | bytes 61444
  280.8 15.0 %all-to-all-start.2 = ((f32[128,1,33]{2,1,0:T(1,128)}), f32[128,1,33]{2,1,0:T(1,128)}, u32[]{:S(2)}, u32[]{:S(2)}) async-start(f32[128,1,33]{2,1,0:T(1,128)} %bitcast.2440), calls=%async_computation.2 | async-start | bytes 131072 | tf_op jit(solution)/shard_map/all_to_all | solution.py:232
  286.5 113.6 %all-gather.21.cloned.1.call-start = ((), (), s32[]{:S(2)}) async-start(), calls=%async_computation.7 | async-start | bytes 1392640 | tf_op jit(solution)/shard_map/all_gather | solution.py:137
  360.5 91.3 %all-gather.23.cloned.1.call-start = ((), (), s32[]{:S(2)}) async-start(), calls=%async_computation.8 | async-start | bytes 1392640 | tf_op jit(solution)/shard_map/all_gather | solution.py:137
  539.6 15.2 %all-to-all-start.4 = ((f32[128,1,33]{2,1,0:T(1,128)}), f32[128,1,33]{2,1,0:T(1,128)}, u32[]{:S(2)}, u32[]{:S(2)}) async-start(f32[128,1,33]{2,1,0:T(1,128)} %bitcast.2441), calls=%async_computation.4 | async-start | bytes 131072 | tf_op jit(solution)/shard_map/all_to_all | solution.py:232
  545.6 101.9 %all-gather.25.cloned.1.call-start = ((), (), s32[]{:S(2)}) async-start(), calls=%async_computation.9 | async-start | bytes 1392640 | tf_op jit(solution)/shard_map/all_gather | solution.py:137
  584.5 19.6 %copy-start.24 = (f32[40,8,127]{2,1,0:T(8,128)S(1)}, f32[40,8,127]{2,1,0:T(8,128)}, u32[]{:S(2)}) copy-start(f32[40,8,127]{2,1,0:T(8,128)} %slice.2275) | copy-start | bytes 487684
  584.5 18.1 %copy-start.123 = (f32[40,8]{0,1:T(8,128)S(1)}, f32[40,8]{0,1:T(8,128)}, u32[]{:S(2)}) copy-start(f32[40,8]{0,1:T(8,128)} %copy-done.122) | copy-start | bytes 3844
  584.5 18.1 %copy-start.125 = (f32[40,8]{0,1:T(8,128)S(1)}, f32[40,8]{0,1:T(8,128)}, u32[]{:S(2)}) copy-start(f32[40,8]{0,1:T(8,128)} %copy-done.124) | copy-start | bytes 3844
  584.5 19.8 %copy-start.18 = (f32[40,8,128]{2,1,0:T(8,128)S(1)}, f32[40,8,128]{2,1,0:T(8,128)}, u32[]{:S(2)}) copy-start(f32[40,8,128]{2,1,0:T(8,128)} %pad_bitcast_fusion.1) | copy-start | bytes 491524
  606.5 40.9 %copy-start.52 = (f32[40,128]{1,0:T(8,128)S(1)}, f32[40,128]{1,0:T(8,128)}, u32[]{:S(2)}) copy-start(f32[40,128]{1,0:T(8,128)} %copy-done.48) | copy-start | bytes 61444
  606.6 40.9 %copy-start.57 = (f32[40,128]{1,0:T(8,128)S(1)}, f32[40,128]{1,0:T(8,128)}, u32[]{:S(2)}) copy-start(f32[40,128]{1,0:T(8,128)} %copy-done.53) | copy-start | bytes 61444
  606.6 40.9 %copy-start.62 = (f32[40,128]{1,0:T(8,128)S(1)}, f32[40,128]{1,0:T(8,128)}, u32[]{:S(2)}) copy-start(f32[40,128]{1,0:T(8,128)} %copy-done.58) | copy-start | bytes 61444
  606.6 40.9 %copy-start.80 = (f32[40,128]{1,0:T(8,128)S(1)}, f32[40,128]{1,0:T(8,128)}, u32[]{:S(2)}) copy-start(f32[40,128]{1,0:T(8,128)} %copy-done.79) | copy-start | bytes 61444
  606.6 40.9 %copy-start.82 = (f32[40,128]{1,0:T(8,128)S(1)}, f32[40,128]{1,0:T(8,128)}, u32[]{:S(2)}) copy-start(f32[40,128]{1,0:T(8,128)} %copy-done.81) | copy-start | bytes 61444
  606.6 40.9 %copy-start.84 = (f32[40,128]{1,0:T(8,128)S(1)}, f32[40,128]{1,0:T(8,128)}, u32[]{:S(2)}) copy-start(f32[40,128]{1,0:T(8,128)} %copy-done.83) | copy-start | bytes 61444
  606.6 40.9 %copy-start.86 = (f32[40,128]{1,0:T(8,128)S(1)}, f32[40,128]{1,0:T(8,128)}, u32[]{:S(2)}) copy-start(f32[40,128]{1,0:T(8,128)} %copy-done.85) | copy-start | bytes 61444
  606.6 40.9 %copy-start.88 = (f32[40,128]{1,0:T(8,128)S(1)}, f32[40,128]{1,0:T(8,128)}, u32[]{:S(2)}) copy-start(f32[40,128]{1,0:T(8,128)} %copy-done.87) | copy-start | bytes 61444
  606.6 40.9 %copy-start.89 = (f32[40,128]{1,0:T(8,128)S(1)}, f32[40,128]{1,0:T(8,128)}, u32[]{:S(2)}) copy-start(f32[40,128]{1,0:T(8,128)} %get-tuple-element.298) | copy-start | bytes 61444
  606.6 40.9 %copy-start.90 = (f32[40,128]{1,0:T(8,128)S(1)}, f32[40,128]{1,0:T(8,128)}, u32[]{:S(2)}) copy-start(f32[40,128]{1,0:T(8,128)} %get-tuple-element.299) | copy-start | bytes 61444
  606.6 40.9 %copy-start.91 = (f32[40,128]{1,0:T(8,128)S(1)}, f32[40,128]{1,0:T(8,128)}, u32[]{:S(2)}) copy-start(f32[40,128]{1,0:T(8,128)} %get-tuple-element.300) | copy-start | bytes 61444
  606.7 40.9 %copy-start.92 = (f32[40,128]{1,0:T(8,128)S(1)}, f32[40,128]{1,0:T(8,128)}, u32[]{:S(2)}) copy-start(f32[40,128]{1,0:T(8,128)} %get-tuple-element.301) | copy-start | bytes 61444
  606.7 40.9 %copy-start.93 = (f32[40,128]{1,0:T(8,128)S(1)}, f32[40,128]{1,0:T(8,128)}, u32[]{:S(2)}) copy-start(f32[40,128]{1,0:T(8,128)} %get-tuple-element.302) | copy-start | bytes 61444
  606.7 40.9 %copy-start.94 = (f32[40,128]{1,0:T(8,128)S(1)}, f32[40,128]{1,0:T(8,128)}, u32[]{:S(2)}) copy-start(f32[40,128]{1,0:T(8,128)} %get-tuple-element.303) | copy-start | bytes 61444
  606.7 40.9 %copy-start.95 = (f32[40,128]{1,0:T(8,128)S(1)}, f32[40,128]{1,0:T(8,128)}, u32[]{:S(2)}) copy-start(f32[40,128]{1,0:T(8,128)} %get-tuple-element.304) | copy-start | bytes 61444
  606.7 40.9 %copy-start.96 = (f32[40,128]{1,0:T(8,128)S(1)}, f32[40,128]{1,0:T(8,128)}, u32[]{:S(2)}) copy-start(f32[40,128]{1,0:T(8,128)} %get-tuple-element.305) | copy-start | bytes 61444
  606.7 40.9 %copy-start.97 = (f32[40,128]{1,0:T(8,128)S(1)}, f32[40,128]{1,0:T(8,128)}, u32[]{:S(2)}) copy-start(f32[40,128]{1,0:T(8,128)} %get-tuple-element.306) | copy-start | bytes 61444
  606.7 40.9 %copy-start.98 = (f32[40,128]{1,0:T(8,128)S(1)}, f32[40,128]{1,0:T(8,128)}, u32[]{:S(2)}) copy-start(f32[40,128]{1,0:T(8,128)} %get-tuple-element.307) | copy-start | bytes 61444
  606.7 40.9 %copy-start.99 = (f32[40,128]{1,0:T(8,128)S(1)}, f32[40,128]{1,0:T(8,128)}, u32[]{:S(2)}) copy-start(f32[40,128]{1,0:T(8,128)} %get-tuple-element.308) | copy-start | bytes 61444
  606.7 40.9 %copy-start.100 = (f32[40,128]{1,0:T(8,128)S(1)}, f32[40,128]{1,0:T(8,128)}, u32[]{:S(2)}) copy-start(f32[40,128]{1,0:T(8,128)} %get-tuple-element.309) | copy-start | bytes 61444
  606.7 40.9 %copy-start.101 = (f32[40,128]{1,0:T(8,128)S(1)}, f32[40,128]{1,0:T(8,128)}, u32[]{:S(2)}) copy-start(f32[40,128]{1,0:T(8,128)} %get-tuple-element.262) | copy-start | bytes 61444
  606.8 40.9 %copy-start.102 = (f32[40,128]{1,0:T(8,128)S(1)}, f32[40,128]{1,0:T(8,128)}, u32[]{:S(2)}) copy-start(f32[40,128]{1,0:T(8,128)} %get-tuple-element.264) | copy-start | bytes 61444
  606.8 40.9 %copy-start.103 = (f32[40,128]{1,0:T(8,128)S(1)}, f32[40,128]{1,0:T(8,128)}, u32[]{:S(2)}) copy-start(f32[40,128]{1,0:T(8,128)} %get-tuple-element.266) | copy-start | bytes 61444
  606.8 40.9 %copy-start.104 = (f32[40,128]{1,0:T(8,128)S(1)}, f32[40,128]{1,0:T(8,128)}, u32[]{:S(2)}) copy-start(f32[40,128]{1,0:T(8,128)} %get-tuple-element.268) | copy-start | bytes 61444
  606.8 40.9 %copy-start.105 = (f32[40,128]{1,0:T(8,128)S(1)}, f32[40,128]{1,0:T(8,128)}, u32[]{:S(2)}) copy-start(f32[40,128]{1,0:T(8,128)} %get-tuple-element.270) | copy-start | bytes 61444
  606.8 40.9 %copy-start.106 = (f32[40,128]{1,0:T(8,128)S(1)}, f32[40,128]{1,0:T(8,128)}, u32[]{:S(2)}) copy-start(f32[40,128]{1,0:T(8,128)} %get-tuple-element.272) | copy-start | bytes 61444
  606.8 40.9 %copy-start.107 = (f32[40,128]{1,0:T(8,128)S(1)}, f32[40,128]{1,0:T(8,128)}, u32[]{:S(2)}) copy-start(f32[40,128]{1,0:T(8,128)} %get-tuple-element.274) | copy-start | bytes 61444
  606.8 40.9 %copy-start.108 = (f32[40,128]{1,0:T(8,128)S(1)}, f32[40,128]{1,0:T(8,128)}, u32[]{:S(2)}) copy-start(f32[40,128]{1,0:T(8,128)} %get-tuple-element.276) | copy-start | bytes 61444
  606.8 40.9 %copy-start.109 = (f32[40,128]{1,0:T(8,128)S(1)}, f32[40,128]{1,0:T(8,128)}, u32[]{:S(2)}) copy-start(f32[40,128]{1,0:T(8,128)} %get-tuple-element.277) | copy-start | bytes 61444
  606.8 40.9 %copy-start.110 = (f32[40,128]{1,0:T(8,128)S(1)}, f32[40,128]{1,0:T(8,128)}, u32[]{:S(2)}) copy-start(f32[40,128]{1,0:T(8,128)} %get-tuple-element.278) | copy-start | bytes 61444
  606.8 40.9 %copy-start.111 = (f32[40,128]{1,0:T(8,128)S(1)}, f32[40,128]{1,0:T(8,128)}, u32[]{:S(2)}) copy-start(f32[40,128]{1,0:T(8,128)} %get-tuple-element.279) | copy-start | bytes 61444
  606.9 40.9 %copy-start.112 = (f32[40,128]{1,0:T(8,128)S(1)}, f32[40,128]{1,0:T(8,128)}, u32[]{:S(2)}) copy-start(f32[40,128]{1,0:T(8,128)} %get-tuple-element.280) | copy-start | bytes 61444
  606.9 40.9 %copy-start.113 = (f32[40,128]{1,0:T(8,128)S(1)}, f32[40,128]{1,0:T(8,128)}, u32[]{:S(2)}) copy-start(f32[40,128]{1,0:T(8,128)} %multiply_subtract_fusion.3) | copy-start | bytes 61444
  606.9 40.9 %copy-start.114 = (f32[40,128]{1,0:T(8,128)S(1)}, f32[40,128]{1,0:T(8,128)}, u32[]{:S(2)}) copy-start(f32[40,128]{1,0:T(8,128)} %multiply_subtract_fusion.2) | copy-start | bytes 61444
  606.9 40.9 %copy-start.115 = (f32[40,128]{1,0:T(8,128)S(1)}, f32[40,128]{1,0:T(8,128)}, u32[]{:S(2)}) copy-start(f32[40,128]{1,0:T(8,128)} %get-tuple-element.281) | copy-start | bytes 61444
  606.9 40.9 %copy-start.116 = (f32[40,128]{1,0:T(8,128)S(1)}, f32[40,128]{1,0:T(8,128)}, u32[]{:S(2)}) copy-start(f32[40,128]{1,0:T(8,128)} %get-tuple-element.282) | copy-start | bytes 61444
  606.9 40.9 %copy-start.117 = (f32[40,128]{1,0:T(8,128)S(1)}, f32[40,128]{1,0:T(8,128)}, u32[]{:S(2)}) copy-start(f32[40,128]{1,0:T(8,128)} %get-tuple-element.283) | copy-start | bytes 61444
  606.9 40.9 %copy-start.118 = (f32[40,128]{1,0:T(8,128)S(1)}, f32[40,128]{1,0:T(8,128)}, u32[]{:S(2)}) copy-start(f32[40,128]{1,0:T(8,128)} %get-tuple-element.284) | copy-start | bytes 61444
  606.9 40.9 %copy-start.119 = (f32[40,128]{1,0:T(8,128)S(1)}, f32[40,128]{1,0:T(8,128)}, u32[]{:S(2)}) copy-start(f32[40,128]{1,0:T(8,128)} %get-tuple-element.285) | copy-start | bytes 61444
  606.9 40.9 %copy-start.120 = (f32[40,128]{1,0:T(8,128)S(1)}, f32[40,128]{1,0:T(8,128)}, u32[]{:S(2)}) copy-start(f32[40,128]{1,0:T(8,128)} %get-tuple-element.286) | copy-start | bytes 61444
  (91 other events, 135.7 us)
Sparse Core Ops, SparseCore 0:
  101.7 44.3 all-gather.16
  153.8 42.6 all-gather.18
  360.6 39.4 all-gather.20
  409.1 42.6 all-gather.22
  607.9 39.4 all-gather.24

commit v8 on v7

--- a/solution.py
+++ b/solution.py
@@ -68,7 +68,7 @@
         prefix=prefix,
         suffix=suffix,
         back_of_prefix=back_of_prefix,
-        rate_totals=lax.all_gather(totals, axis_name) if periodic else None,
+        rate_totals=None,
         totals=totals,
         axis_name=axis_name,
         periodic=periodic,
@@ -128,7 +128,15 @@
             lax.index_in_dim(back_offset, 0, line_axis, keepdims=False),
         ]
     )
-    if plan["rate_totals"] is None:
+    if plan["rate_totals"] is None and plan["periodic"]:
+        rate_part = plan["totals"].reshape((-1,) + plan["totals"].shape[2:])
+        both = lax.all_gather(
+            jnp.concatenate([mine.reshape((-1,) + mine.shape[2:]), rate_part]), plan["axis_name"]
+        )
+        split = mine.shape[0] * mine.shape[1]
+        got = both[:, :split].reshape((both.shape[0],) + mine.shape)
+        plan["rate_totals"] = both[:, split:].reshape((both.shape[0],) + plan["totals"].shape)
+    elif plan["rate_totals"] is None:
         rate_part = jnp.broadcast_to(plan["totals"], (3,) + mine.shape[1:])
         both = lax.all_gather(jnp.concatenate([mine, rate_part]), plan["axis_name"])
         got = both[:, :2]

time: 671 us -> 679 us (1.012)
  waiting for transfers between devices: 181 us -> 212 us
  blocking collectives: 124 us -> 98.1 us
    all_gather x0 -> x1, waiting for transfers between devices: none -> 42.6 us  [line_operator(): lax.all_gather(jnp.concatenate([mine.reshape((-1,) + mine.shape[2:]), rat...]
    all_gather x1 -> x0, blocking collectives: 25.7 us -> none  [make_plan(): lax.all_gather(totals, axis_name)]
    all_gather x5 -> x4, waiting for transfers between devices: 163 us -> 152 us  [line_operator(): got = lax.all_gather(mine, plan['axis_name'])]
    unnamed x472 -> x544, local copies, waits for them, and re-layouts: 34.1 us -> 39.7 us
  transfers between devices with their start and end apart: 8 -> 8, of which waited for: 7 -> 7; matrix products, arithmetic and copies ran while one was open for 5% -> 4% of each run, Pallas kernels for 0% -> 0%
where the time goes in v8:
time: 679 us; the launch traced here: 667 us
  waiting for transfers between devices  212 us (31%)
  other arithmetic  162 us (24%)
  local copies, waits for them, and re-layouts  116 us (17%)
  blocking collectives  98.1 us (14%)
  between operations  25.9 us (4%)
  starting transfers between devices  23.2 us (3%)
  matrix products  17 us (3%)
  Pallas kernels  13.4 us (2%)
    all_gather x4, waiting for transfers between devices, line_operator(): got = lax.all_gather(mine, plan['axis_name'])  152 us
    scatter-add x3, other arithmetic, deposit_local(): flat_cells = jnp.zeros((TR * rate_x.size,), jnp.float32).at[cell_index.re...  68.2 us
    all_gather x4, blocking collectives, line_operator(): got = lax.all_gather(mine, plan['axis_name'])  51.5 us
    all_gather x1, waiting for transfers between devices, line_operator(): lax.all_gather(jnp.concatenate([mine.reshape((-1,) + mine.shape[2:]), rat...  42.6 us
    unnamed x544, local copies, waits for them, and re-layouts  39.7 us
    all_to_all x2, blocking collectives, exchange(): lax.all_to_all(packed, ('gx', 'gy'), split_axis=0, concat_axis=0, tiled=T...  33.2 us
    unnamed x56, other arithmetic  21.8 us
    all_to_all x2, waiting for transfers between devices, exchange(): lax.all_to_all(packed, ('gx', 'gy'), split_axis=0, concat_axis=0, tiled=T...  17.2 us
  transfers between devices with their start and end apart: 8, of which 7 were waited for; matrix products, arithmetic and copies ran while one was open for 4% of the time, Pallas kernels for 0%

profile of v8, /device:TPU:0, one launch (start us, length us, event | category | flops | bytes accessed | tf_op | source)
XLA Modules:
  0.0 667.3 jit_solution(10775242498663501490)
XLA Ops:
  10.3 5.7 fusion.4
  16.8 11.2 %all-to-all-start = ((f32[128,1,32]{2,1,0:T(1,128)}), f32[128,1,32]{2,1,0:T(1,128)S(1)}, u32[]{:S(2)}, u32[]{:S(2)}) async-start(f32[128,1,32]{2,1,0:T(1,128)} %bitcast.5), calls=%async_computation | async-start | bytes 131072 | tf_op jit(solution)/shard_map/all_to_all | solution.py:292
  35.1 1.7 slice.2283
  39.7 1.7 reduce.17
  41.5 22.7 %scatter_custom_fusion = f32[81920]{0:T(1024)} fusion(s32[4096]{0:T(1024)} %bitcast.2477, f32[4096]{0:T(1024)S(1)} %reshape.27342, f32[]{:T(128)} %constant.117.clone.1), kind=kCustom, calls=%fused_computation.441 | custom fusion | flops 4096 | bytes 328192 | tf_op jit(solution)/shard_map/scatter-add | solution.py:283
  72.8 13.4 %all-gather = f32[40,2,40,8]{2,3,1,0:T(8,128)S(1)} all-gather(f32[5,2,40,8]{2,3,1,0:T(8,128)S(1)} %pad_maximum_fusion.6), channel_id=2, replica_groups=mesh['gx'=16,'gy'=8] {'gy'}, dimensions={0}, use_global_device_ids=true | all-gather | bytes 115200 | tf_op jit(solution)/shard_map/all_gather | solution.py:141
  101.0 1.7 pad_bitcast_fusion
  102.7 42.6 %all-gather.16.cloned.1.call-done = f32[112,40,128]{2,1,0:T(8,128)} async-done(((f32[7,40,128]{2,1,0:T(8,128)}), f32[112,40,128]{2,1,0:T(8,128)}) %all-gather.16.cloned.1.call-update) | async-done | bytes 2293776 | tf_op jit(solution)/shard_map/all_gather | solution.py:133
  156.1 1.5 reshape_squeeze.9
  161.0 37.9 %all-gather.18.cloned.1.call-done = f32[32,2,40,128]{3,2,1,0:T(8,128)} async-done(((f32[2,2,40,128]{3,2,1,0:T(8,128)}), f32[32,2,40,128]{3,2,1,0:T(8,128)}) %all-gather.18.cloned.1.call-update) | async-done | bytes 1310736 | tf_op jit(solution)/shard_map/all_gather | solution.py:145
  198.9 1.9 constant_dynamic-update-slice_fusion.79
  207.0 1.7 copy.729
  208.7 1.7 copy.728
  211.2 13.0 %all-gather.3 = f32[16,2,40,8]{2,3,1,0:T(8,128)S(1)} all-gather(f32[2,2,40,8]{2,3,1,0:T(8,128)S(1)} %pad_maximum_fusion.7), channel_id=5, replica_groups=mesh['gx'=16,'gy'=8] {'gy'}, dimensions={0}, use_global_device_ids=true | all-gather | bytes 46080 | tf_op jit(solution)/shard_map/all_gather | solution.py:145
  233.2 2.0 slice_add_fusion.6
  238.5 2.1 multiply_multiply_fusion.7
  240.6 6.7 %shard_map.86 = f32[1,4096]{1,0:T(1,128)} custom-call(f32[640,128]{1,0:T(8,128)} %bitcast.2410, s32[1,4096]{1,0:T(1,128)} %and_select_fusion.1.rows_ref, s32[1,4096]{1,0:T(1,128)} %get-tuple-element.148.lanes_ref), custom_call_target="tpu_custom_call" | custom-call | tf_op jit(solution)/shard_map/pallas_call | solution.py:184
  247.3 2.0 reduce.18
  249.3 1.4 reshape.27327
  250.7 1.5 concatenate.530
  252.3 16.7 %all_to_all.54 = f32[128,1,33]{2,1,0:T(1,128)S(1)} all-to-all(f32[128,1,33]{2,1,0:T(1,128)S(1)} %bitcast.2446), channel_id=1, replica_groups=mesh['gx'=16,'gy'=8] {'gx','gy'}, dimensions={0} | all-to-all | bytes 33792 | tf_op jit(solution)/shard_map/all_to_all | solution.py:240
  271.0 1.5 reshape.27379
  272.5 5.7 fusion.2
  278.8 1.4 reshape.27329
  280.2 2.2 multiply_reduce_fusion.4
  283.8 1.5 concatenate.531
  285.3 5.7 all-to-all-start.2
  291.6 8.6 %all-to-all-done.2 = f32[128,1,33]{2,1,0:T(1,128)} async-done(((f32[128,1,33]{2,1,0:T(1,128)}), f32[128,1,33]{2,1,0:T(1,128)}, u32[]{:S(2)}, u32[]{:S(2)}) %all-to-all-start.2) | async-done | bytes 16928 | tf_op jit(solution)/shard_map/all_to_all | solution.py:240
  300.2 1.5 reshape.27350
  301.7 22.7 %scatter_custom_fusion.1 = f32[81920]{0:T(1024)} fusion(s32[4096]{0:T(1024)} %bitcast.2478, f32[4096]{0:T(1024)} %reshape.27350, f32[]{:T(128)} %constant.117.clone.1), kind=kCustom, calls=%fused_computation.439 | custom fusion | flops 4096 | bytes 328192 | tf_op jit(solution)/shard_map/scatter-add | solution.py:283
  330.6 1.7 copy.736
  332.4 1.7 copy.735
  334.8 12.7 %all-gather.4 = f32[16,2,40,8]{2,3,1,0:T(8,128)S(1)} all-gather(f32[2,2,40,8]{2,3,1,0:T(8,128)S(1)} %pad_maximum_fusion.8), channel_id=6, replica_groups=mesh['gx'=16,'gy'=8] {'gy'}, dimensions={0}, use_global_device_ids=true | all-gather | bytes 46080 | tf_op jit(solution)/shard_map/all_gather | solution.py:145
  356.6 2.0 slice_add_fusion.5
  361.9 1.4 multiply_multiply_fusion.5
  367.0 1.6 slice_reduce_fusion.3
  368.6 1.6 slice_reduce_fusion.2
  371.5 34.8 %all-gather.20.cloned.1.call-done = f32[32,2,40,128]{3,2,1,0:T(8,128)} async-done(((f32[2,2,40,128]{3,2,1,0:T(8,128)}), f32[32,2,40,128]{3,2,1,0:T(8,128)}) %all-gather.20.cloned.1.call-update) | async-done | bytes 1310736 | tf_op jit(solution)/shard_map/all_gather | solution.py:145
  406.3 1.9 constant_dynamic-update-slice_fusion.143
  416.1 42.2 %all-gather.22.cloned.1.call-done = f32[32,2,40,128]{3,2,1,0:T(8,128)} async-done(((f32[2,2,40,128]{3,2,1,0:T(8,128)}), f32[32,2,40,128]{3,2,1,0:T(8,128)}) %all-gather.22.cloned.1.call-update) | async-done | bytes 1310736 | tf_op jit(solution)/shard_map/all_gather | solution.py:145
  458.2 1.9 constant_dynamic-update-slice_fusion.175
  466.2 1.7 copy.750
  468.0 1.7 copy.749
  470.4 13.0 %all-gather.7 = f32[16,2,40,8]{2,3,1,0:T(8,128)S(1)} all-gather(f32[2,2,40,8]{2,3,1,0:T(8,128)S(1)} %pad_maximum_fusion.9), channel_id=9, replica_groups=mesh['gx'=16,'gy'=8] {'gy'}, dimensions={0}, use_global_device_ids=true | all-gather | bytes 46080 | tf_op jit(solution)/shard_map/all_gather | solution.py:145
  492.5 2.0 slice_add_fusion.2
  497.7 2.1 multiply_multiply_fusion.2
  499.8 6.7 %shard_map.87 = f32[1,4096]{1,0:T(1,128)} custom-call(f32[640,128]{1,0:T(8,128)} %bitcast.2409, s32[1,4096]{1,0:T(1,128)} %and_select_fusion.1.rows_ref, s32[1,4096]{1,0:T(1,128)} %get-tuple-element.148.lanes_ref), custom_call_target="tpu_custom_call" | custom-call | tf_op jit(solution)/shard_map/pallas_call | solution.py:184
  506.5 2.0 reduce.19
  508.6 1.4 reshape.27333
  511.4 16.4 %all_to_all.55 = f32[128,1,33]{2,1,0:T(1,128)S(1)} all-to-all(f32[128,1,33]{2,1,0:T(1,128)S(1)} %bitcast.2445), channel_id=1, replica_groups=mesh['gx'=16,'gy'=8] {'gx','gy'}, dimensions={0} | all-to-all | bytes 33792 | tf_op jit(solution)/shard_map/all_to_all | solution.py:240
  530.4 1.7 multiply_reduce_fusion
  532.0 1.6 fusion.19
  533.6 1.5 reshape.27381
  535.2 5.7 fusion
  542.9 2.3 multiply_reduce_fusion.3
  546.5 1.5 concatenate.577
  547.9 5.9 all-to-all-start.4
  554.5 8.6 %all-to-all-done.4 = f32[128,1,33]{2,1,0:T(1,128)} async-done(((f32[128,1,33]{2,1,0:T(1,128)}), f32[128,1,33]{2,1,0:T(1,128)}, u32[]{:S(2)}, u32[]{:S(2)}) %all-to-all-start.4) | async-done | bytes 16928 | tf_op jit(solution)/shard_map/all_to_all | solution.py:240
  563.2 1.5 reshape.27358
  564.7 22.7 %scatter_custom_fusion.2 = f32[81920]{0:T(1024)} fusion(s32[4096]{0:T(1024)} %bitcast.2479, f32[4096]{0:T(1024)} %reshape.27358, f32[]{:T(128)} %constant.117.clone.1), kind=kCustom, calls=%fused_computation.437 | custom fusion | flops 4096 | bytes 328192 | tf_op jit(solution)/shard_map/scatter-add | solution.py:283
  593.8 12.7 %all-gather.8 = f32[16,2,40,8]{2,3,1,0:T(8,128)S(1)} all-gather(f32[2,2,40,8]{2,3,1,0:T(8,128)S(1)} %pad_maximum_fusion.10), channel_id=10, replica_groups=mesh['gx'=16,'gy'=8] {'gy'}, dimensions={0}, use_global_device_ids=true | all-gather | bytes 46080 | tf_op jit(solution)/shard_map/all_gather | solution.py:145
  616.1 1.6 slice_reduce_fusion
  618.9 36.9 %all-gather.24.cloned.1.call-done = f32[32,2,40,128]{3,2,1,0:T(8,128)} async-done(((f32[2,2,40,128]{3,2,1,0:T(8,128)}), f32[32,2,40,128]{3,2,1,0:T(8,128)}) %all-gather.24.cloned.1.call-update) | async-done | bytes 1310736 | tf_op jit(solution)/shard_map/all_gather | solution.py:145
  656.1 1.8 constant_dynamic-update-slice_fusion.239
  (959 shorter events, 142.9 us)
Async XLA Ops:
  10.3 5.8 copy-start.177
  10.3 17.8 %copy-start.35 = (f32[40,8,128]{2,1,0:T(8,128)S(1)}, f32[40,8,128]{2,1,0:T(8,128)}, u32[]{:S(2)}) copy-start(f32[40,8,128]{2,1,0:T(8,128)} %param.8) | copy-start | bytes 491524
  16.8 21.7 %all-to-all-start = ((f32[128,1,32]{2,1,0:T(1,128)}), f32[128,1,32]{2,1,0:T(1,128)S(1)}, u32[]{:S(2)}, u32[]{:S(2)}) async-start(f32[128,1,32]{2,1,0:T(1,128)} %bitcast.5), calls=%async_computation | async-start | bytes 131072 | tf_op jit(solution)/shard_map/all_to_all | solution.py:292
  28.0 117.3 %all-gather.16.cloned.1.call-start = ((), (), s32[]{:S(2)}) async-start(), calls=%async_computation.5 | async-start | bytes 2437120 | tf_op jit(solution)/shard_map/all_gather | solution.py:133
  32.5 62.3 %copy-start.18 = (f32[40,8,128]{2,1,0:T(8,128)}, f32[40,8,128]{2,1,0:T(8,128)S(1)}, u32[]{:S(2)}) copy-start(f32[40,8,128]{2,1,0:T(8,128)S(1)} %pad_bitcast_fusion.1) | copy-start | bytes 491524
  38.4 58.0 %copy-start.8 = (f32[40,8,128]{2,0,1:T(8,128)}, f32[40,8,128]{2,0,1:T(8,128)S(1)}, u32[]{:S(2)}) copy-start(f32[40,8,128]{2,0,1:T(8,128)S(1)} %copy.684) | copy-start | bytes 491524
  86.2 6.4 copy-start.169
  86.2 6.4 copy-start.170
  86.3 6.4 copy-start.171
  86.3 6.4 copy-start.172
  86.3 6.4 copy-start.173
  86.3 6.4 copy-start.174
  86.3 9.7 %copy-start.153 = (f32[40,8]{0,1:T(8,128)}, f32[40,8]{0,1:T(8,128)S(1)}, u32[]{:S(2)}) copy-start(f32[40,8]{0,1:T(8,128)S(1)} %get-tuple-element.323) | copy-start | bytes 3844
  86.3 9.7 %copy-start.155 = (f32[40,8]{0,1:T(8,128)}, f32[40,8]{0,1:T(8,128)S(1)}, u32[]{:S(2)}) copy-start(f32[40,8]{0,1:T(8,128)S(1)} %get-tuple-element.326) | copy-start | bytes 3844
  86.3 6.3 copy-start.175
  98.9 100.0 %all-gather.18.cloned.1.call-start = ((), (), s32[]{:S(2)}) async-start(), calls=%async_computation.6 | async-start | bytes 1392640 | tf_op jit(solution)/shard_map/all_gather | solution.py:145
  101.0 49.9 %copy-start.20 = (f32[40,7,128]{2,1,0:T(8,128)}, f32[40,7,128]{2,1,0:T(8,128)S(1)}, u32[]{:S(2)}) copy-start(f32[40,7,128]{2,1,0:T(8,128)S(1)} %slice.2361) | copy-start | bytes 430084
  285.3 14.9 %all-to-all-start.2 = ((f32[128,1,33]{2,1,0:T(1,128)}), f32[128,1,33]{2,1,0:T(1,128)}, u32[]{:S(2)}, u32[]{:S(2)}) async-start(f32[128,1,33]{2,1,0:T(1,128)} %bitcast.2443), calls=%async_computation.2 | async-start | bytes 131072 | tf_op jit(solution)/shard_map/all_to_all | solution.py:240
  290.9 115.3 %all-gather.20.cloned.1.call-start = ((), (), s32[]{:S(2)}) async-start(), calls=%async_computation.7 | async-start | bytes 1392640 | tf_op jit(solution)/shard_map/all_gather | solution.py:145
  366.7 91.5 %all-gather.22.cloned.1.call-start = ((), (), s32[]{:S(2)}) async-start(), calls=%async_computation.8 | async-start | bytes 1392640 | tf_op jit(solution)/shard_map/all_gather | solution.py:145
  547.9 15.2 %all-to-all-start.4 = ((f32[128,1,33]{2,1,0:T(1,128)}), f32[128,1,33]{2,1,0:T(1,128)}, u32[]{:S(2)}, u32[]{:S(2)}) async-start(f32[128,1,33]{2,1,0:T(1,128)} %bitcast.2444), calls=%async_computation.4 | async-start | bytes 131072 | tf_op jit(solution)/shard_map/all_to_all | solution.py:240
  553.9 101.9 %all-gather.24.cloned.1.call-start = ((), (), s32[]{:S(2)}) async-start(), calls=%async_computation.9 | async-start | bytes 1392640 | tf_op jit(solution)/shard_map/all_gather | solution.py:145
  592.8 19.6 %copy-start.25 = (f32[40,8,127]{2,1,0:T(8,128)S(1)}, f32[40,8,127]{2,1,0:T(8,128)}, u32[]{:S(2)}) copy-start(f32[40,8,127]{2,1,0:T(8,128)} %slice.2283) | copy-start | bytes 487684
  592.9 18.1 %copy-start.154 = (f32[40,8]{0,1:T(8,128)S(1)}, f32[40,8]{0,1:T(8,128)}, u32[]{:S(2)}) copy-start(f32[40,8]{0,1:T(8,128)} %copy-done.153) | copy-start | bytes 3844
  592.9 18.1 %copy-start.156 = (f32[40,8]{0,1:T(8,128)S(1)}, f32[40,8]{0,1:T(8,128)}, u32[]{:S(2)}) copy-start(f32[40,8]{0,1:T(8,128)} %copy-done.155) | copy-start | bytes 3844
  592.9 19.8 %copy-start.19 = (f32[40,8,128]{2,1,0:T(8,128)S(1)}, f32[40,8,128]{2,1,0:T(8,128)}, u32[]{:S(2)}) copy-start(f32[40,8,128]{2,1,0:T(8,128)} %copy-done.18) | copy-start | bytes 491524
  614.9 40.9 %copy-start.52 = (f32[40,128]{1,0:T(8,128)S(1)}, f32[40,128]{1,0:T(8,128)}, u32[]{:S(2)}) copy-start(f32[40,128]{1,0:T(8,128)} %copy-done.48) | copy-start | bytes 61444
  614.9 40.9 %copy-start.57 = (f32[40,128]{1,0:T(8,128)S(1)}, f32[40,128]{1,0:T(8,128)}, u32[]{:S(2)}) copy-start(f32[40,128]{1,0:T(8,128)} %copy-done.53) | copy-start | bytes 61444
  614.9 40.9 %copy-start.62 = (f32[40,128]{1,0:T(8,128)S(1)}, f32[40,128]{1,0:T(8,128)}, u32[]{:S(2)}) copy-start(f32[40,128]{1,0:T(8,128)} %copy-done.58) | copy-start | bytes 61444
  614.9 40.9 %copy-start.83 = (f32[40,128]{1,0:T(8,128)S(1)}, f32[40,128]{1,0:T(8,128)}, u32[]{:S(2)}) copy-start(f32[40,128]{1,0:T(8,128)} %copy-done.82) | copy-start | bytes 61444
  614.9 40.8 %copy-start.85 = (f32[40,128]{1,0:T(8,128)S(1)}, f32[40,128]{1,0:T(8,128)}, u32[]{:S(2)}) copy-start(f32[40,128]{1,0:T(8,128)} %copy-done.84) | copy-start | bytes 61444
  614.9 40.8 %copy-start.87 = (f32[40,128]{1,0:T(8,128)S(1)}, f32[40,128]{1,0:T(8,128)}, u32[]{:S(2)}) copy-start(f32[40,128]{1,0:T(8,128)} %copy-done.86) | copy-start | bytes 61444
  615.0 40.8 %copy-start.89 = (f32[40,128]{1,0:T(8,128)S(1)}, f32[40,128]{1,0:T(8,128)}, u32[]{:S(2)}) copy-start(f32[40,128]{1,0:T(8,128)} %copy-done.88) | copy-start | bytes 61444
  615.0 40.8 %copy-start.91 = (f32[40,128]{1,0:T(8,128)S(1)}, f32[40,128]{1,0:T(8,128)}, u32[]{:S(2)}) copy-start(f32[40,128]{1,0:T(8,128)} %copy-done.90) | copy-start | bytes 61444
  615.0 40.8 %copy-start.93 = (f32[40,128]{1,0:T(8,128)S(1)}, f32[40,128]{1,0:T(8,128)}, u32[]{:S(2)}) copy-start(f32[40,128]{1,0:T(8,128)} %copy-done.92) | copy-start | bytes 61444
  615.0 40.8 %copy-start.95 = (f32[40,128]{1,0:T(8,128)S(1)}, f32[40,128]{1,0:T(8,128)}, u32[]{:S(2)}) copy-start(f32[40,128]{1,0:T(8,128)} %copy-done.94) | copy-start | bytes 61444
  615.0 40.8 %copy-start.97 = (f32[40,128]{1,0:T(8,128)S(1)}, f32[40,128]{1,0:T(8,128)}, u32[]{:S(2)}) copy-start(f32[40,128]{1,0:T(8,128)} %copy-done.96) | copy-start | bytes 61444
  615.0 40.8 %copy-start.99 = (f32[40,128]{1,0:T(8,128)S(1)}, f32[40,128]{1,0:T(8,128)}, u32[]{:S(2)}) copy-start(f32[40,128]{1,0:T(8,128)} %copy-done.98) | copy-start | bytes 61444
  615.0 40.8 %copy-start.101 = (f32[40,128]{1,0:T(8,128)S(1)}, f32[40,128]{1,0:T(8,128)}, u32[]{:S(2)}) copy-start(f32[40,128]{1,0:T(8,128)} %copy-done.100) | copy-start | bytes 61444
  615.0 40.8 %copy-start.103 = (f32[40,128]{1,0:T(8,128)S(1)}, f32[40,128]{1,0:T(8,128)}, u32[]{:S(2)}) copy-start(f32[40,128]{1,0:T(8,128)} %copy-done.102) | copy-start | bytes 61444
  615.0 40.8 %copy-start.105 = (f32[40,128]{1,0:T(8,128)S(1)}, f32[40,128]{1,0:T(8,128)}, u32[]{:S(2)}) copy-start(f32[40,128]{1,0:T(8,128)} %copy-done.104) | copy-start | bytes 61444
  615.0 40.8 %copy-start.107 = (f32[40,128]{1,0:T(8,128)S(1)}, f32[40,128]{1,0:T(8,128)}, u32[]{:S(2)}) copy-start(f32[40,128]{1,0:T(8,128)} %copy-done.106) | copy-start | bytes 61444
  615.1 40.8 %copy-start.109 = (f32[40,128]{1,0:T(8,128)S(1)}, f32[40,128]{1,0:T(8,128)}, u32[]{:S(2)}) copy-start(f32[40,128]{1,0:T(8,128)} %copy-done.108) | copy-start | bytes 61444
  615.1 40.8 %copy-start.111 = (f32[40,128]{1,0:T(8,128)S(1)}, f32[40,128]{1,0:T(8,128)}, u32[]{:S(2)}) copy-start(f32[40,128]{1,0:T(8,128)} %copy-done.110) | copy-start | bytes 61444
  615.1 40.8 %copy-start.113 = (f32[40,128]{1,0:T(8,128)S(1)}, f32[40,128]{1,0:T(8,128)}, u32[]{:S(2)}) copy-start(f32[40,128]{1,0:T(8,128)} %copy-done.112) | copy-start | bytes 61444
  615.1 40.8 %copy-start.115 = (f32[40,128]{1,0:T(8,128)S(1)}, f32[40,128]{1,0:T(8,128)}, u32[]{:S(2)}) copy-start(f32[40,128]{1,0:T(8,128)} %copy-done.114) | copy-start | bytes 61444
  615.1 40.8 %copy-start.117 = (f32[40,128]{1,0:T(8,128)S(1)}, f32[40,128]{1,0:T(8,128)}, u32[]{:S(2)}) copy-start(f32[40,128]{1,0:T(8,128)} %copy-done.116) | copy-start | bytes 61444
  615.1 40.8 %copy-start.119 = (f32[40,128]{1,0:T(8,128)S(1)}, f32[40,128]{1,0:T(8,128)}, u32[]{:S(2)}) copy-start(f32[40,128]{1,0:T(8,128)} %copy-done.118) | copy-start | bytes 61444
  615.1 40.8 %copy-start.121 = (f32[40,128]{1,0:T(8,128)S(1)}, f32[40,128]{1,0:T(8,128)}, u32[]{:S(2)}) copy-start(f32[40,128]{1,0:T(8,128)} %copy-done.120) | copy-start | bytes 61444
  615.1 40.8 %copy-start.123 = (f32[40,128]{1,0:T(8,128)S(1)}, f32[40,128]{1,0:T(8,128)}, u32[]{:S(2)}) copy-start(f32[40,128]{1,0:T(8,128)} %copy-done.122) | copy-start | bytes 61444
  615.1 40.8 %copy-start.125 = (f32[40,128]{1,0:T(8,128)S(1)}, f32[40,128]{1,0:T(8,128)}, u32[]{:S(2)}) copy-start(f32[40,128]{1,0:T(8,128)} %copy-done.124) | copy-start | bytes 61444
  615.1 40.8 %copy-start.127 = (f32[40,128]{1,0:T(8,128)S(1)}, f32[40,128]{1,0:T(8,128)}, u32[]{:S(2)}) copy-start(f32[40,128]{1,0:T(8,128)} %copy-done.126) | copy-start | bytes 61444
  615.2 40.8 %copy-start.129 = (f32[40,128]{1,0:T(8,128)S(1)}, f32[40,128]{1,0:T(8,128)}, u32[]{:S(2)}) copy-start(f32[40,128]{1,0:T(8,128)} %copy-done.128) | copy-start | bytes 61444
  615.2 40.8 %copy-start.131 = (f32[40,128]{1,0:T(8,128)S(1)}, f32[40,128]{1,0:T(8,128)}, u32[]{:S(2)}) copy-start(f32[40,128]{1,0:T(8,128)} %copy-done.130) | copy-start | bytes 61444
  615.2 40.8 %copy-start.133 = (f32[40,128]{1,0:T(8,128)S(1)}, f32[40,128]{1,0:T(8,128)}, u32[]{:S(2)}) copy-start(f32[40,128]{1,0:T(8,128)} %copy-done.132) | copy-start | bytes 61444
  615.2 40.8 %copy-start.135 = (f32[40,128]{1,0:T(8,128)S(1)}, f32[40,128]{1,0:T(8,128)}, u32[]{:S(2)}) copy-start(f32[40,128]{1,0:T(8,128)} %copy-done.134) | copy-start | bytes 61444
  615.2 40.8 %copy-start.137 = (f32[40,128]{1,0:T(8,128)S(1)}, f32[40,128]{1,0:T(8,128)}, u32[]{:S(2)}) copy-start(f32[40,128]{1,0:T(8,128)} %copy-done.136) | copy-start | bytes 61444
  615.2 40.8 %copy-start.139 = (f32[40,128]{1,0:T(8,128)S(1)}, f32[40,128]{1,0:T(8,128)}, u32[]{:S(2)}) copy-start(f32[40,128]{1,0:T(8,128)} %copy-done.138) | copy-start | bytes 61444
  615.2 40.8 %copy-start.141 = (f32[40,128]{1,0:T(8,128)S(1)}, f32[40,128]{1,0:T(8,128)}, u32[]{:S(2)}) copy-start(f32[40,128]{1,0:T(8,128)} %copy-done.140) | copy-start | bytes 61444
  615.2 40.8 %copy-start.143 = (f32[40,128]{1,0:T(8,128)S(1)}, f32[40,128]{1,0:T(8,128)}, u32[]{:S(2)}) copy-start(f32[40,128]{1,0:T(8,128)} %copy-done.142) | copy-start | bytes 61444
  615.2 40.8 %copy-start.145 = (f32[40,128]{1,0:T(8,128)S(1)}, f32[40,128]{1,0:T(8,128)}, u32[]{:S(2)}) copy-start(f32[40,128]{1,0:T(8,128)} %copy-done.144) | copy-start | bytes 61444
  615.2 40.8 %copy-start.147 = (f32[40,128]{1,0:T(8,128)S(1)}, f32[40,128]{1,0:T(8,128)}, u32[]{:S(2)}) copy-start(f32[40,128]{1,0:T(8,128)} %copy-done.146) | copy-start | bytes 61444
  615.3 40.8 %copy-start.149 = (f32[40,128]{1,0:T(8,128)S(1)}, f32[40,128]{1,0:T(8,128)}, u32[]{:S(2)}) copy-start(f32[40,128]{1,0:T(8,128)} %copy-done.148) | copy-start | bytes 61444
  615.3 40.8 %copy-start.151 = (f32[40,128]{1,0:T(8,128)S(1)}, f32[40,128]{1,0:T(8,128)}, u32[]{:S(2)}) copy-start(f32[40,128]{1,0:T(8,128)} %copy-done.150) | copy-start | bytes 61444
  (127 other events, 214.3 us)
Sparse Core Ops, SparseCore 0:
  99.0 46.2 all-gather.15
  156.2 42.5 all-gather.17
  366.9 39.3 all-gather.19
  415.6 42.6 all-gather.21
  616.3 39.4 all-gather.23

commit v9 on v7

--- a/solution.py
+++ b/solution.py
@@ -145,7 +145,7 @@
     return plan["gain_out"] * (forward + next_offset + next_factor * leaving)
 
 
-CHUNK = 512
+CHUNK = 4096
 
 
 def split_three(values):

time: 671 us -> 667 us (level)
  no operation moved by 1% of the time
where the time goes in v9:
time: 667 us; the launch traced here: 655 us
  waiting for transfers between devices  181 us (27%)
  other arithmetic  166 us (25%)
  blocking collectives  124 us (19%)
  local copies, waits for them, and re-layouts  110 us (16%)
  between operations  25.2 us (4%)
  starting transfers between devices  23.3 us (3%)
  matrix products  17 us (3%)
  Pallas kernels  9.57 us (1%)
    all_gather x5, waiting for transfers between devices, line_operator(): got = lax.all_gather(mine, plan['axis_name'])  163 us
    scatter-add x3, other arithmetic, deposit_local(): flat_cells = jnp.zeros((TR * rate_x.size,), jnp.float32).at[cell_index.re...  68.6 us
    all_gather x4, blocking collectives, line_operator(): got = lax.all_gather(mine, plan['axis_name'])  52.2 us
    unnamed x472, local copies, waits for them, and re-layouts  34.1 us
    all_to_all x2, blocking collectives, exchange(): lax.all_to_all(packed, ('gx', 'gy'), split_axis=0, concat_axis=0, tiled=T...  32.9 us
    all_gather x1, blocking collectives, make_plan(): lax.all_gather(totals, axis_name)  25.7 us
    unnamed x56, other arithmetic  21.3 us
    add x100, other arithmetic, scan_offsets(): forcing + level_factor * shift_along(forcing, distance, line_axis, revers...  17.5 us
  transfers between devices with their start and end apart: 8, of which 7 were waited for; matrix products, arithmetic and copies ran while one was open for 5% of the time, Pallas kernels for 0%

profile of v9, /device:TPU:0, one launch (start us, length us, event | category | flops | bytes accessed | tf_op | source)
XLA Modules:
  0.0 655.4 jit_solution(15515063848881938498)
XLA Ops:
  10.3 5.7 fusion.4
  16.8 11.7 %all-to-all-start = ((f32[128,1,32]{2,1,0:T(1,128)}), f32[128,1,32]{2,1,0:T(1,128)}, u32[]{:S(2)}, u32[]{:S(2)}) async-start(f32[128,1,32]{2,1,0:T(1,128)} %bitcast.5), calls=%async_computation | async-start | bytes 131072 | tf_op jit(solution)/shard_map/all_to_all | solution.py:284
  37.5 1.6 pad_bitcast_fusion.1
  40.1 1.7 multiply_add_fusion.93
  44.1 1.7 slice.2275
  46.4 1.6 reduce.17
  48.1 22.7 %scatter_custom_fusion = f32[81920]{0:T(1024)} fusion(s32[4096]{0:T(1024)} %bitcast.2474, f32[4096]{0:T(1024)S(1)} %reshape.27326, f32[]{:T(128)} %constant.117.clone.1), kind=kCustom, calls=%fused_computation.439 | custom fusion | flops 4096 | bytes 328192 | tf_op jit(solution)/shard_map/scatter-add | solution.py:275
  81.9 13.1 %all-gather = f32[40,2,40,8]{2,3,1,0:T(8,128)S(1)} all-gather(f32[5,2,40,8]{2,3,1,0:T(8,128)S(1)} %pad_maximum_fusion.6), channel_id=2, replica_groups=mesh['gx'=16,'gy'=8] {'gy'}, dimensions={0}, use_global_device_ids=true | all-gather | bytes 115200 | tf_op jit(solution)/shard_map/all_gather | solution.py:133
  103.6 1.7 pad_bitcast_fusion
  105.3 25.7 %all-gather.1 = f32[48,1,40,128]{3,2,1,0:T(8,128)S(1)} all-gather(f32[3,1,40,128]{3,2,1,0:T(8,128)S(1)} %pad_maximum_fusion.5), channel_id=3, replica_groups=mesh['gx'=16,'gy'=8] {'gx'}, dimensions={0}, use_global_device_ids=true | all-gather | bytes 1044480 | tf_op jit(solution)/shard_map/all_gather | solution.py:71
  134.4 11.4 %all-gather.17.cloned.1.call-done = f32[32,2,40,128]{3,2,1,0:T(8,128)} async-done(((f32[2,2,40,128]{3,2,1,0:T(8,128)}), f32[32,2,40,128]{3,2,1,0:T(8,128)}) %all-gather.17.cloned.1.call-update) | async-done | bytes 1310736 | tf_op jit(solution)/shard_map/all_gather | solution.py:137
  145.8 1.8 constant_dynamic-update-slice_fusion.47
  153.4 1.5 reshape_squeeze.9
  158.3 37.9 %all-gather.19.cloned.1.call-done = f32[32,2,40,128]{3,2,1,0:T(8,128)} async-done(((f32[2,2,40,128]{3,2,1,0:T(8,128)}), f32[32,2,40,128]{3,2,1,0:T(8,128)}) %all-gather.19.cloned.1.call-update) | async-done | bytes 1310736 | tf_op jit(solution)/shard_map/all_gather | solution.py:137
  196.2 1.9 constant_dynamic-update-slice_fusion.79
  204.3 1.7 copy.920
  206.0 1.7 copy.919
  208.5 13.4 %all-gather.4 = f32[16,2,40,8]{2,3,1,0:T(8,128)S(1)} all-gather(f32[2,2,40,8]{2,3,1,0:T(8,128)S(1)} %pad_maximum_fusion.7), channel_id=6, replica_groups=mesh['gx'=16,'gy'=8] {'gy'}, dimensions={0}, use_global_device_ids=true | all-gather | bytes 46080 | tf_op jit(solution)/shard_map/all_gather | solution.py:137
  230.9 2.0 slice_add_fusion.6
  234.3 2.1 multiply_multiply_fusion.7
  236.4 4.8 shard_map.86
  241.2 2.0 reduce.18
  246.1 16.4 %all_to_all.54 = f32[128,1,33]{2,1,0:T(1,128)S(1)} all-to-all(f32[128,1,33]{2,1,0:T(1,128)S(1)} %bitcast.2443), channel_id=1, replica_groups=mesh['gx'=16,'gy'=8] {'gx','gy'}, dimensions={0} | all-to-all | bytes 33792 | tf_op jit(solution)/shard_map/all_to_all | solution.py:232
  264.6 1.5 reshape.27364
  266.1 5.7 fusion.2
  273.8 2.2 multiply_reduce_fusion.4
  277.3 1.5 concatenate.527
  278.8 5.7 all-to-all-start.2
  285.1 8.6 %all-to-all-done.2 = f32[128,1,33]{2,1,0:T(1,128)} async-done(((f32[128,1,33]{2,1,0:T(1,128)}), f32[128,1,33]{2,1,0:T(1,128)}, u32[]{:S(2)}, u32[]{:S(2)}) %all-to-all-start.2) | async-done | bytes 16928 | tf_op jit(solution)/shard_map/all_to_all | solution.py:232
  293.8 1.5 reshape.27334
  295.3 22.9 %scatter_custom_fusion.1 = f32[81920]{0:T(1024)} fusion(s32[4096]{0:T(1024)} %bitcast.2475, f32[4096]{0:T(1024)} %reshape.27334, f32[]{:T(128)} %constant.117.clone.1), kind=kCustom, calls=%fused_computation.437 | custom fusion | flops 4096 | bytes 328192 | tf_op jit(solution)/shard_map/scatter-add | solution.py:275
  324.4 1.7 copy.927
  326.1 1.7 copy.926
  328.6 12.7 %all-gather.5 = f32[16,2,40,8]{2,3,1,0:T(8,128)S(1)} all-gather(f32[2,2,40,8]{2,3,1,0:T(8,128)S(1)} %pad_maximum_fusion.8), channel_id=7, replica_groups=mesh['gx'=16,'gy'=8] {'gy'}, dimensions={0}, use_global_device_ids=true | all-gather | bytes 46080 | tf_op jit(solution)/shard_map/all_gather | solution.py:137
  350.3 2.0 slice_add_fusion.5
  358.7 1.5 slice_reduce_fusion.3
  360.2 1.5 slice_reduce_fusion.2
  362.9 35.3 %all-gather.21.cloned.1.call-done = f32[32,2,40,128]{3,2,1,0:T(8,128)} async-done(((f32[2,2,40,128]{3,2,1,0:T(8,128)}), f32[32,2,40,128]{3,2,1,0:T(8,128)}) %all-gather.21.cloned.1.call-update) | async-done | bytes 1310736 | tf_op jit(solution)/shard_map/all_gather | solution.py:137
  398.3 1.9 constant_dynamic-update-slice_fusion.143
  407.7 42.2 %all-gather.23.cloned.1.call-done = f32[32,2,40,128]{3,2,1,0:T(8,128)} async-done(((f32[2,2,40,128]{3,2,1,0:T(8,128)}), f32[32,2,40,128]{3,2,1,0:T(8,128)}) %all-gather.23.cloned.1.call-update) | async-done | bytes 1310736 | tf_op jit(solution)/shard_map/all_gather | solution.py:137
  449.9 1.9 constant_dynamic-update-slice_fusion.175
  457.9 1.7 copy.941
  459.6 1.7 copy.940
  462.1 13.2 %all-gather.8 = f32[16,2,40,8]{2,3,1,0:T(8,128)S(1)} all-gather(f32[2,2,40,8]{2,3,1,0:T(8,128)S(1)} %pad_maximum_fusion.9), channel_id=10, replica_groups=mesh['gx'=16,'gy'=8] {'gy'}, dimensions={0}, use_global_device_ids=true | all-gather | bytes 46080 | tf_op jit(solution)/shard_map/all_gather | solution.py:137
  484.3 2.0 slice_add_fusion.2
  487.7 2.1 multiply_multiply_fusion.2
  489.8 4.8 shard_map.87
  494.6 2.0 reduce.19
  498.0 1.5 concatenate.572
  499.6 16.4 %all_to_all.55 = f32[128,1,33]{2,1,0:T(1,128)S(1)} all-to-all(f32[128,1,33]{2,1,0:T(1,128)S(1)} %bitcast.2442), channel_id=1, replica_groups=mesh['gx'=16,'gy'=8] {'gx','gy'}, dimensions={0} | all-to-all | bytes 33792 | tf_op jit(solution)/shard_map/all_to_all | solution.py:232
  518.6 1.7 multiply_reduce_fusion
  520.2 1.6 fusion.19
  521.8 1.5 reshape.27366
  523.4 5.7 fusion
  531.1 2.3 multiply_reduce_fusion.3
  534.5 1.5 concatenate.573
  536.0 5.7 all-to-all-start.4
  542.3 8.6 %all-to-all-done.4 = f32[128,1,33]{2,1,0:T(1,128)} async-done(((f32[128,1,33]{2,1,0:T(1,128)}), f32[128,1,33]{2,1,0:T(1,128)}, u32[]{:S(2)}, u32[]{:S(2)}) %all-to-all-start.4) | async-done | bytes 16928 | tf_op jit(solution)/shard_map/all_to_all | solution.py:232
  551.0 1.5 reshape.27342
  552.5 23.0 %scatter_custom_fusion.2 = f32[81920]{0:T(1024)} fusion(s32[4096]{0:T(1024)} %bitcast.2476, f32[4096]{0:T(1024)} %reshape.27342, f32[]{:T(128)} %constant.117.clone.1), kind=kCustom, calls=%fused_computation.435 | custom fusion | flops 4096 | bytes 328192 | tf_op jit(solution)/shard_map/scatter-add | solution.py:275
  581.9 12.7 %all-gather.9 = f32[16,2,40,8]{2,3,1,0:T(8,128)S(1)} all-gather(f32[2,2,40,8]{2,3,1,0:T(8,128)S(1)} %pad_maximum_fusion.10), channel_id=11, replica_groups=mesh['gx'=16,'gy'=8] {'gy'}, dimensions={0}, use_global_device_ids=true | all-gather | bytes 46080 | tf_op jit(solution)/shard_map/all_gather | solution.py:137
  604.2 1.6 slice_reduce_fusion
  607.2 36.7 %all-gather.25.cloned.1.call-done = f32[32,2,40,128]{3,2,1,0:T(8,128)} async-done(((f32[2,2,40,128]{3,2,1,0:T(8,128)}), f32[32,2,40,128]{3,2,1,0:T(8,128)}) %all-gather.25.cloned.1.call-update) | async-done | bytes 1310736 | tf_op jit(solution)/shard_map/all_gather | solution.py:137
  644.2 1.8 constant_dynamic-update-slice_fusion.239
  (885 shorter events, 140.6 us)
Async XLA Ops:
  10.3 18.3 %copy-start.143 = (s32[1,128,32]{1,2,0:T(8,128)S(1)}, s32[1,128,32]{1,2,0:T(8,128)}, u32[]{:S(2)}) copy-start(s32[1,128,32]{1,2,0:T(8,128)} %param.10) | copy-start | bytes 49156
  10.3 19.6 %copy-start.34 = (f32[40,8,128]{2,1,0:T(8,128)S(1)}, f32[40,8,128]{2,1,0:T(8,128)}, u32[]{:S(2)}) copy-start(f32[40,8,128]{2,1,0:T(8,128)} %param.7) | copy-start | bytes 491524
  16.8 29.0 %all-to-all-start = ((f32[128,1,32]{2,1,0:T(1,128)}), f32[128,1,32]{2,1,0:T(1,128)}, u32[]{:S(2)}, u32[]{:S(2)}) async-start(f32[128,1,32]{2,1,0:T(1,128)} %bitcast.5), calls=%async_computation | async-start | bytes 131072 | tf_op jit(solution)/shard_map/all_to_all | solution.py:284
  28.5 117.3 %all-gather.17.cloned.1.call-start = ((), (), s32[]{:S(2)}) async-start(), calls=%async_computation.5 | async-start | bytes 1392640 | tf_op jit(solution)/shard_map/all_gather | solution.py:137
  30.3 72.4 %copy-start = (f32[1,40,8,128]{3,2,1,0:T(8,128)}, f32[1,40,8,128]{3,2,1,0:T(8,128)S(1)}, u32[]{:S(2)}) copy-start(f32[1,40,8,128]{3,2,1,0:T(8,128)S(1)} %get-tuple-element.232) | copy-start | bytes 491524
  44.1 54.8 %copy-start.8 = (f32[40,8,128]{2,0,1:T(8,128)}, f32[40,8,128]{2,0,1:T(8,128)S(1)}, u32[]{:S(2)}) copy-start(f32[40,8,128]{2,0,1:T(8,128)S(1)} %copy.875) | copy-start | bytes 491524
  79.8 15.4 %copy-start.145 = (f32[8,2,40,8]{2,3,1,0:T(8,128)S(1)}, f32[8,2,40,8]{2,3,1,0:T(8,128)}, u32[]{:S(2)}) copy-start(f32[8,2,40,8]{2,3,1,0:T(8,128)} %constant_dynamic-update-slice_fusion.7) | copy-start | bytes 61444
  101.3 94.9 %all-gather.19.cloned.1.call-start = ((), (), s32[]{:S(2)}) async-start(), calls=%async_computation.6 | async-start | bytes 1392640 | tf_op jit(solution)/shard_map/all_gather | solution.py:137
  103.6 45.5 %copy-start.19 = (f32[40,7,128]{2,1,0:T(8,128)}, f32[40,7,128]{2,1,0:T(8,128)S(1)}, u32[]{:S(2)}) copy-start(f32[40,7,128]{2,1,0:T(8,128)S(1)} %slice.2351) | copy-start | bytes 430084
  132.9 15.3 %copy-start.58 = (f32[40,128]{1,0:T(8,128)}, f32[40,128]{1,0:T(8,128)S(1)}, u32[]{:S(2)}) copy-start(f32[40,128]{1,0:T(8,128)S(1)} %get-tuple-element.292) | copy-start | bytes 61444
  133.6 14.0 %copy-start.79 = (f32[40,128]{1,0:T(8,128)}, f32[40,128]{1,0:T(8,128)S(1)}, u32[]{:S(2)}) copy-start(f32[40,128]{1,0:T(8,128)S(1)} %get-tuple-element.293) | copy-start | bytes 61444
  133.6 14.0 %copy-start.81 = (f32[40,128]{1,0:T(8,128)}, f32[40,128]{1,0:T(8,128)S(1)}, u32[]{:S(2)}) copy-start(f32[40,128]{1,0:T(8,128)S(1)} %get-tuple-element.294) | copy-start | bytes 61444
  133.6 14.0 %copy-start.83 = (f32[40,128]{1,0:T(8,128)}, f32[40,128]{1,0:T(8,128)S(1)}, u32[]{:S(2)}) copy-start(f32[40,128]{1,0:T(8,128)S(1)} %get-tuple-element.295) | copy-start | bytes 61444
  133.6 14.0 %copy-start.85 = (f32[40,128]{1,0:T(8,128)}, f32[40,128]{1,0:T(8,128)S(1)}, u32[]{:S(2)}) copy-start(f32[40,128]{1,0:T(8,128)S(1)} %get-tuple-element.296) | copy-start | bytes 61444
  133.6 14.0 %copy-start.87 = (f32[40,128]{1,0:T(8,128)}, f32[40,128]{1,0:T(8,128)S(1)}, u32[]{:S(2)}) copy-start(f32[40,128]{1,0:T(8,128)S(1)} %get-tuple-element.297) | copy-start | bytes 61444
  278.8 15.0 %all-to-all-start.2 = ((f32[128,1,33]{2,1,0:T(1,128)}), f32[128,1,33]{2,1,0:T(1,128)}, u32[]{:S(2)}, u32[]{:S(2)}) async-start(f32[128,1,33]{2,1,0:T(1,128)} %bitcast.2440), calls=%async_computation.2 | async-start | bytes 131072 | tf_op jit(solution)/shard_map/all_to_all | solution.py:232
  284.5 113.8 %all-gather.21.cloned.1.call-start = ((), (), s32[]{:S(2)}) async-start(), calls=%async_computation.7 | async-start | bytes 1392640 | tf_op jit(solution)/shard_map/all_gather | solution.py:137
  358.6 91.2 %all-gather.23.cloned.1.call-start = ((), (), s32[]{:S(2)}) async-start(), calls=%async_computation.8 | async-start | bytes 1392640 | tf_op jit(solution)/shard_map/all_gather | solution.py:137
  536.0 14.9 %all-to-all-start.4 = ((f32[128,1,33]{2,1,0:T(1,128)}), f32[128,1,33]{2,1,0:T(1,128)}, u32[]{:S(2)}, u32[]{:S(2)}) async-start(f32[128,1,33]{2,1,0:T(1,128)} %bitcast.2441), calls=%async_computation.4 | async-start | bytes 131072 | tf_op jit(solution)/shard_map/all_to_all | solution.py:232
  541.7 102.1 %all-gather.25.cloned.1.call-start = ((), (), s32[]{:S(2)}) async-start(), calls=%async_computation.9 | async-start | bytes 1392640 | tf_op jit(solution)/shard_map/all_gather | solution.py:137
  580.8 19.6 %copy-start.24 = (f32[40,8,127]{2,1,0:T(8,128)S(1)}, f32[40,8,127]{2,1,0:T(8,128)}, u32[]{:S(2)}) copy-start(f32[40,8,127]{2,1,0:T(8,128)} %slice.2275) | copy-start | bytes 487684
  580.9 18.1 %copy-start.123 = (f32[40,8]{0,1:T(8,128)S(1)}, f32[40,8]{0,1:T(8,128)}, u32[]{:S(2)}) copy-start(f32[40,8]{0,1:T(8,128)} %copy-done.122) | copy-start | bytes 3844
  580.9 18.1 %copy-start.125 = (f32[40,8]{0,1:T(8,128)S(1)}, f32[40,8]{0,1:T(8,128)}, u32[]{:S(2)}) copy-start(f32[40,8]{0,1:T(8,128)} %copy-done.124) | copy-start | bytes 3844
  580.9 19.8 %copy-start.18 = (f32[40,8,128]{2,1,0:T(8,128)S(1)}, f32[40,8,128]{2,1,0:T(8,128)}, u32[]{:S(2)}) copy-start(f32[40,8,128]{2,1,0:T(8,128)} %pad_bitcast_fusion.1) | copy-start | bytes 491524
  602.9 40.9 %copy-start.52 = (f32[40,128]{1,0:T(8,128)S(1)}, f32[40,128]{1,0:T(8,128)}, u32[]{:S(2)}) copy-start(f32[40,128]{1,0:T(8,128)} %copy-done.48) | copy-start | bytes 61444
  602.9 40.9 %copy-start.57 = (f32[40,128]{1,0:T(8,128)S(1)}, f32[40,128]{1,0:T(8,128)}, u32[]{:S(2)}) copy-start(f32[40,128]{1,0:T(8,128)} %copy-done.53) | copy-start | bytes 61444
  603.0 40.9 %copy-start.62 = (f32[40,128]{1,0:T(8,128)S(1)}, f32[40,128]{1,0:T(8,128)}, u32[]{:S(2)}) copy-start(f32[40,128]{1,0:T(8,128)} %copy-done.58) | copy-start | bytes 61444
  603.0 40.9 %copy-start.80 = (f32[40,128]{1,0:T(8,128)S(1)}, f32[40,128]{1,0:T(8,128)}, u32[]{:S(2)}) copy-start(f32[40,128]{1,0:T(8,128)} %copy-done.79) | copy-start | bytes 61444
  603.0 40.9 %copy-start.82 = (f32[40,128]{1,0:T(8,128)S(1)}, f32[40,128]{1,0:T(8,128)}, u32[]{:S(2)}) copy-start(f32[40,128]{1,0:T(8,128)} %copy-done.81) | copy-start | bytes 61444
  603.0 40.9 %copy-start.84 = (f32[40,128]{1,0:T(8,128)S(1)}, f32[40,128]{1,0:T(8,128)}, u32[]{:S(2)}) copy-start(f32[40,128]{1,0:T(8,128)} %copy-done.83) | copy-start | bytes 61444
  603.0 40.9 %copy-start.86 = (f32[40,128]{1,0:T(8,128)S(1)}, f32[40,128]{1,0:T(8,128)}, u32[]{:S(2)}) copy-start(f32[40,128]{1,0:T(8,128)} %copy-done.85) | copy-start | bytes 61444
  603.0 40.9 %copy-start.88 = (f32[40,128]{1,0:T(8,128)S(1)}, f32[40,128]{1,0:T(8,128)}, u32[]{:S(2)}) copy-start(f32[40,128]{1,0:T(8,128)} %copy-done.87) | copy-start | bytes 61444
  603.0 40.9 %copy-start.89 = (f32[40,128]{1,0:T(8,128)S(1)}, f32[40,128]{1,0:T(8,128)}, u32[]{:S(2)}) copy-start(f32[40,128]{1,0:T(8,128)} %get-tuple-element.298) | copy-start | bytes 61444
  603.0 40.9 %copy-start.90 = (f32[40,128]{1,0:T(8,128)S(1)}, f32[40,128]{1,0:T(8,128)}, u32[]{:S(2)}) copy-start(f32[40,128]{1,0:T(8,128)} %get-tuple-element.299) | copy-start | bytes 61444
  603.0 40.9 %copy-start.91 = (f32[40,128]{1,0:T(8,128)S(1)}, f32[40,128]{1,0:T(8,128)}, u32[]{:S(2)}) copy-start(f32[40,128]{1,0:T(8,128)} %get-tuple-element.300) | copy-start | bytes 61444
  603.0 40.9 %copy-start.92 = (f32[40,128]{1,0:T(8,128)S(1)}, f32[40,128]{1,0:T(8,128)}, u32[]{:S(2)}) copy-start(f32[40,128]{1,0:T(8,128)} %get-tuple-element.301) | copy-start | bytes 61444
  603.1 40.9 %copy-start.93 = (f32[40,128]{1,0:T(8,128)S(1)}, f32[40,128]{1,0:T(8,128)}, u32[]{:S(2)}) copy-start(f32[40,128]{1,0:T(8,128)} %get-tuple-element.302) | copy-start | bytes 61444
  603.1 40.9 %copy-start.94 = (f32[40,128]{1,0:T(8,128)S(1)}, f32[40,128]{1,0:T(8,128)}, u32[]{:S(2)}) copy-start(f32[40,128]{1,0:T(8,128)} %get-tuple-element.303) | copy-start | bytes 61444
  603.1 40.9 %copy-start.95 = (f32[40,128]{1,0:T(8,128)S(1)}, f32[40,128]{1,0:T(8,128)}, u32[]{:S(2)}) copy-start(f32[40,128]{1,0:T(8,128)} %get-tuple-element.304) | copy-start | bytes 61444
  603.1 40.9 %copy-start.96 = (f32[40,128]{1,0:T(8,128)S(1)}, f32[40,128]{1,0:T(8,128)}, u32[]{:S(2)}) copy-start(f32[40,128]{1,0:T(8,128)} %get-tuple-element.305) | copy-start | bytes 61444
  603.1 40.9 %copy-start.97 = (f32[40,128]{1,0:T(8,128)S(1)}, f32[40,128]{1,0:T(8,128)}, u32[]{:S(2)}) copy-start(f32[40,128]{1,0:T(8,128)} %get-tuple-element.306) | copy-start | bytes 61444
  603.1 40.9 %copy-start.98 = (f32[40,128]{1,0:T(8,128)S(1)}, f32[40,128]{1,0:T(8,128)}, u32[]{:S(2)}) copy-start(f32[40,128]{1,0:T(8,128)} %get-tuple-element.307) | copy-start | bytes 61444
  603.1 40.9 %copy-start.99 = (f32[40,128]{1,0:T(8,128)S(1)}, f32[40,128]{1,0:T(8,128)}, u32[]{:S(2)}) copy-start(f32[40,128]{1,0:T(8,128)} %get-tuple-element.308) | copy-start | bytes 61444
  603.1 40.9 %copy-start.100 = (f32[40,128]{1,0:T(8,128)S(1)}, f32[40,128]{1,0:T(8,128)}, u32[]{:S(2)}) copy-start(f32[40,128]{1,0:T(8,128)} %get-tuple-element.309) | copy-start | bytes 61444
  603.1 40.9 %copy-start.101 = (f32[40,128]{1,0:T(8,128)S(1)}, f32[40,128]{1,0:T(8,128)}, u32[]{:S(2)}) copy-start(f32[40,128]{1,0:T(8,128)} %get-tuple-element.262) | copy-start | bytes 61444
  603.1 40.9 %copy-start.102 = (f32[40,128]{1,0:T(8,128)S(1)}, f32[40,128]{1,0:T(8,128)}, u32[]{:S(2)}) copy-start(f32[40,128]{1,0:T(8,128)} %get-tuple-element.264) | copy-start | bytes 61444
  603.2 40.9 %copy-start.103 = (f32[40,128]{1,0:T(8,128)S(1)}, f32[40,128]{1,0:T(8,128)}, u32[]{:S(2)}) copy-start(f32[40,128]{1,0:T(8,128)} %get-tuple-element.266) | copy-start | bytes 61444
  603.2 40.9 %copy-start.104 = (f32[40,128]{1,0:T(8,128)S(1)}, f32[40,128]{1,0:T(8,128)}, u32[]{:S(2)}) copy-start(f32[40,128]{1,0:T(8,128)} %get-tuple-element.268) | copy-start | bytes 61444
  603.2 40.9 %copy-start.105 = (f32[40,128]{1,0:T(8,128)S(1)}, f32[40,128]{1,0:T(8,128)}, u32[]{:S(2)}) copy-start(f32[40,128]{1,0:T(8,128)} %get-tuple-element.270) | copy-start | bytes 61444
  603.2 40.9 %copy-start.106 = (f32[40,128]{1,0:T(8,128)S(1)}, f32[40,128]{1,0:T(8,128)}, u32[]{:S(2)}) copy-start(f32[40,128]{1,0:T(8,128)} %get-tuple-element.272) | copy-start | bytes 61444
  603.2 40.9 %copy-start.107 = (f32[40,128]{1,0:T(8,128)S(1)}, f32[40,128]{1,0:T(8,128)}, u32[]{:S(2)}) copy-start(f32[40,128]{1,0:T(8,128)} %get-tuple-element.274) | copy-start | bytes 61444
  603.2 40.9 %copy-start.108 = (f32[40,128]{1,0:T(8,128)S(1)}, f32[40,128]{1,0:T(8,128)}, u32[]{:S(2)}) copy-start(f32[40,128]{1,0:T(8,128)} %get-tuple-element.276) | copy-start | bytes 61444
  603.2 40.9 %copy-start.109 = (f32[40,128]{1,0:T(8,128)S(1)}, f32[40,128]{1,0:T(8,128)}, u32[]{:S(2)}) copy-start(f32[40,128]{1,0:T(8,128)} %get-tuple-element.277) | copy-start | bytes 61444
  603.2 40.9 %copy-start.110 = (f32[40,128]{1,0:T(8,128)S(1)}, f32[40,128]{1,0:T(8,128)}, u32[]{:S(2)}) copy-start(f32[40,128]{1,0:T(8,128)} %get-tuple-element.278) | copy-start | bytes 61444
  603.2 40.9 %copy-start.111 = (f32[40,128]{1,0:T(8,128)S(1)}, f32[40,128]{1,0:T(8,128)}, u32[]{:S(2)}) copy-start(f32[40,128]{1,0:T(8,128)} %get-tuple-element.279) | copy-start | bytes 61444
  603.2 40.9 %copy-start.112 = (f32[40,128]{1,0:T(8,128)S(1)}, f32[40,128]{1,0:T(8,128)}, u32[]{:S(2)}) copy-start(f32[40,128]{1,0:T(8,128)} %get-tuple-element.280) | copy-start | bytes 61444
  603.3 40.9 %copy-start.113 = (f32[40,128]{1,0:T(8,128)S(1)}, f32[40,128]{1,0:T(8,128)}, u32[]{:S(2)}) copy-start(f32[40,128]{1,0:T(8,128)} %multiply_subtract_fusion.3) | copy-start | bytes 61444
  603.3 40.9 %copy-start.114 = (f32[40,128]{1,0:T(8,128)S(1)}, f32[40,128]{1,0:T(8,128)}, u32[]{:S(2)}) copy-start(f32[40,128]{1,0:T(8,128)} %multiply_subtract_fusion.2) | copy-start | bytes 61444
  603.3 40.9 %copy-start.115 = (f32[40,128]{1,0:T(8,128)S(1)}, f32[40,128]{1,0:T(8,128)}, u32[]{:S(2)}) copy-start(f32[40,128]{1,0:T(8,128)} %get-tuple-element.281) | copy-start | bytes 61444
  603.3 40.9 %copy-start.116 = (f32[40,128]{1,0:T(8,128)S(1)}, f32[40,128]{1,0:T(8,128)}, u32[]{:S(2)}) copy-start(f32[40,128]{1,0:T(8,128)} %get-tuple-element.282) | copy-start | bytes 61444
  603.3 40.9 %copy-start.117 = (f32[40,128]{1,0:T(8,128)S(1)}, f32[40,128]{1,0:T(8,128)}, u32[]{:S(2)}) copy-start(f32[40,128]{1,0:T(8,128)} %get-tuple-element.283) | copy-start | bytes 61444
  603.3 40.9 %copy-start.118 = (f32[40,128]{1,0:T(8,128)S(1)}, f32[40,128]{1,0:T(8,128)}, u32[]{:S(2)}) copy-start(f32[40,128]{1,0:T(8,128)} %get-tuple-element.284) | copy-start | bytes 61444
  603.3 40.9 %copy-start.119 = (f32[40,128]{1,0:T(8,128)S(1)}, f32[40,128]{1,0:T(8,128)}, u32[]{:S(2)}) copy-start(f32[40,128]{1,0:T(8,128)} %get-tuple-element.285) | copy-start | bytes 61444
  603.3 40.9 %copy-start.120 = (f32[40,128]{1,0:T(8,128)S(1)}, f32[40,128]{1,0:T(8,128)}, u32[]{:S(2)}) copy-start(f32[40,128]{1,0:T(8,128)} %get-tuple-element.286) | copy-start | bytes 61444
  (91 other events, 135.7 us)
Sparse Core Ops, SparseCore 0:
  101.4 44.3 all-gather.16
  153.6 42.6 all-gather.18
  358.7 39.4 all-gather.20
  407.2 42.6 all-gather.22
  604.3 39.4 all-gather.24
